TPU v7x, 128 devices: a whole 4x4x4 slice. The times are simulated.
128 devices in a mesh: lon: 16 (over x_hi, y, core), lat: 8 (over x_lo, z).
Axes of the slice: x: 4 (x_hi: 2, x_lo: 2; x = x_hi * 2 + x_lo), y: 4, z: 4, core: 2. Of those that a mesh axis runs over, the one named last changes fastest.
Arguments:
- atmosphere: bfloat16 [256, 1024, 256], P('lat', 'lon'), may hold values from -6 to 6
- conv_weight: float32 [7, 7, 256], replicated, may hold values from -0.875 to 0.875
- atm_gain: float32 [256], replicated, may hold values from 0.1 to 1.9
- atm_up: bfloat16 [256, 1024], replicated, may hold values from -0.375 to 0.375
- atm_down: bfloat16 [1024, 256], replicated, may hold values from -0.1875 to 0.1875
- flux_weight: bfloat16 [256, 256], replicated, may hold values from -0.375 to 0.375
- land_mask: int32 [256, 1024], P('lat', 'lon'), may hold values from 0 to 1, as said below
- tile_owner: int32 [8, 16, 128], P('lat', 'lon'), may hold values from 0 to 127, as said below
- ocean_state: bfloat16 [128, 128, 2, 16, 256], P(('lat', 'lon')), may hold values from -6 to 6
- ocn_gain: float32 [256], replicated, may hold values from 0.1 to 1.9
- ocn_up: bfloat16 [256, 1024], replicated, may hold values from -0.375 to 0.375
- ocn_down: bfloat16 [1024, 256], replicated, may hold values from -0.1875 to 0.1875
Outputs:
- atm_out: bfloat16 [256, 1024, 256], P('lat', 'lon')
- ocean_out: bfloat16 [128, 128, 2, 16, 256], P(('lat', 'lon'))
Inputs may be any that keep to these rules, and one draw needn't show every extreme that they name: `tile_owner`: each entry is the index along lat+lon (lat slowest) of the device that owns the tile. No device owns more than 2 tiles of one device's block, and one device owns exactly 2 tiles of every device's block. `land_mask`: no bound on the number of ocean cells of a tile or of a device may be relied on.
All inputs are finite; a program needn't handle non-finite values.
Results may differ from a plain program's by a relative error of at most 0.0056.
Values may be sent and summed in bfloat16 or wider, within the bound.
A program may use at most 64 MiB of HBM per device.

v0:
```python
import jax
import jax.numpy as jnp
from jax import lax
from jax.sharding import PartitionSpec as P


def padded_2(x, sides, width, wrap):
    for axis, dim in sides:
        devices, length = (lax.axis_size(axis), x.shape[dim])
        up = [(i, (i + 1) % devices) for i in range(devices if wrap else devices - 1)]
        down = [(j, i) for i, j in up]
        last = lax.slice_in_dim(x, length - width, length, axis=dim)
        leading = lax.slice_in_dim(x, 0, width, axis=dim)
        before = lax.ppermute(last, axis, up)
        after = lax.ppermute(leading, axis, down)
        x = jnp.concatenate([before, x, after], axis=dim)
    return x


def depthwise(padded, kernel, lat_rows, lon_cols):
    summed = jnp.zeros((lat_rows, lon_cols, padded.shape[2]), jnp.float32)
    for row_off in range(kernel.shape[0]):
        for col_off in range(kernel.shape[1]):
            window = padded[row_off : row_off + lat_rows, col_off : col_off + lon_cols, :].astype(
                jnp.float32
            )
            summed = summed + window * kernel[row_off, col_off]
    return summed


def normalize(values, scales):
    average = jnp.mean(values, axis=-1, keepdims=True)
    centred = values - average
    spread = jnp.mean(centred * centred, axis=-1, keepdims=True)
    return centred * lax.rsqrt(spread + 1e-06) * scales


def channel_mixer(values, scales, w_up, w_down):
    normed = normalize(values, scales).astype(jnp.bfloat16)
    hidden = jax.nn.gelu(
        jnp.dot(normed, w_up, preferred_element_type=jnp.float32), approximate=True
    ).astype(jnp.bfloat16)
    return jnp.dot(hidden, w_down, preferred_element_type=jnp.float32)


def per_device(
    atmosphere,
    conv_weight,
    atm_gain,
    atm_up,
    atm_down,
    flux_weight,
    land_mask,
    tile_owner,
    ocean_state,
    ocn_gain,
    ocn_up,
    ocn_down,
):
    lat_rows, lon_cols, channels = atmosphere.shape
    margin = conv_weight.shape[0] // 2
    lon_padded = padded_2(atmosphere, (("lon", 1),), margin, True)
    padded = padded_2(lon_padded, (("lat", 0),), margin, False)
    mixed = depthwise(padded, conv_weight, lat_rows, lon_cols).reshape(
        lat_rows * lon_cols, channels
    )
    branch = channel_mixer(mixed, atm_gain, atm_up, atm_down)
    flat_atmos = atmosphere.reshape(lat_rows * lon_cols, channels)
    atmos_new = (flat_atmos.astype(jnp.float32) + branch).astype(jnp.bfloat16)
    wet_cells = land_mask.reshape(lat_rows * lon_cols, 1).astype(jnp.float32)
    fluxes = (
        jnp.dot(atmos_new, flux_weight, preferred_element_type=jnp.float32) * wet_cells
    ).astype(jnp.bfloat16)
    owners = tile_owner.reshape(-1)
    tile_count = owners.shape[0]
    peer_count = ocean_state.shape[1]
    capacity = ocean_state.shape[2]
    tile_cells = ocean_state.shape[3]
    flux_tiles = fluxes.reshape(tile_count, tile_cells, channels)
    member = (owners[:, None] == jnp.arange(peer_count, dtype=jnp.int32)[None, :]).astype(jnp.int32)
    tile_rank = jnp.sum(jnp.cumsum(member, axis=0) * member, axis=1) - 1
    slot_index = owners * capacity + tile_rank
    outgoing = (
        jnp.zeros((peer_count * capacity, tile_cells, channels), jnp.bfloat16)
        .at[slot_index]
        .set(flux_tiles)
    )
    outgoing = outgoing.reshape(peer_count, capacity, tile_cells, channels)
    occupied = (
        jnp.zeros((peer_count * capacity,), jnp.bfloat16)
        .at[slot_index]
        .set(1.0)
        .reshape(peer_count, capacity)
    )
    arrived, filled = (
        lax.all_to_all(outgoing, ("lat", "lon"), split_axis=0, concat_axis=0, tiled=True),
        lax.all_to_all(occupied, ("lat", "lon"), split_axis=0, concat_axis=0, tiled=True),
    )
    states = ocean_state[0].astype(jnp.float32) + arrived.astype(jnp.float32)
    flat_states = states.reshape(peer_count * capacity * tile_cells, channels)
    result = flat_states + channel_mixer(flat_states, ocn_gain, ocn_up, ocn_down)
    result = (
        result.reshape(peer_count, capacity, tile_cells, channels)
        * filled.astype(jnp.float32)[:, :, None, None]
    )
    ocean_out = result.astype(jnp.bfloat16)[None]
    return (atmos_new.reshape(lat_rows, lon_cols, channels), ocean_out)


def solution(mesh):
    placed = (
        P("lat", "lon", None),
        P(),
        P(),
        P(),
        P(),
        P(),
        P("lat", "lon"),
        P("lat", "lon", None),
        P(("lat", "lon"), None, None, None, None),
        P(),
        P(),
        P(),
    )
    return jax.shard_map(
        per_device,
        mesh=mesh,
        in_specs=placed,
        out_specs=(P("lat", "lon", None), P(("lat", "lon"), None, None, None, None)),
        check_vma=False,
    )
```

profile of v0, /device:TPU:1, one launch (start us, length us, event | category | flops | bytes accessed | tf_op | source)
XLA Modules:
  0.0 137.6 jit_solution(12112586482620131455)
XLA Ops:
  0.7 1.1 fusion.56
  1.8 2.8 %collective-permute-start = (bf16[32,3,256]{2,1,0:T(4,128)(2,1)S(1)}, bf16[32,3,256]{2,1,0:T(4,128)(2,1)S(1)}, u32[]{:S(2)}, u32[]{:S(2)}) collective-permute-start(bf16[32,3,256]{2,1,0:T(4,128)(2,1)S(1)} %get-tuple-element.10), channel_id=1, source_target_pairs={{0,8},{8,16},{16,24},{24,32},{32,40},{40,48},{48,56},{56,64},{64,7... | collective-permute-start | bytes 147464 | tf_op jit(solution)/shard_map/ppermute | solution.py:14
  7.0 1.3 scatter_custom_fusion.1
  9.1 11.5 %all-to-all-start.1 = ((bf16[128,1,2]{2,1,0:T(2,128)(2,1)}), bf16[128,1,2]{2,1,0:T(2,128)(2,1)S(1)}, u32[]{:S(2)}, u32[]{:S(2)}) async-start(bf16[128,1,2]{2,1,0:T(2,128)(2,1)} %all_to_all.12), calls=%async_computation.1 | async-start | bytes 131072 | tf_op jit(solution)/shard_map/all_to_all | solution.py:97
  20.7 1.0 fusion.57
  21.7 1.0 fusion.58
  23.6 1.3 constant_dynamic-update-slice_fusion.1
  25.1 3.4 %collective-permute-start.2 = (bf16[3,70,256]{2,1,0:T(8,128)(2,1)S(1)}, bf16[3,70,256]{2,1,0:T(8,128)(2,1)S(1)}, u32[]{:S(2)}, u32[]{:S(2)}) collective-permute-start(bf16[3,70,256]{2,1,0:T(8,128)(2,1)S(1)} %get-tuple-element.8), channel_id=1, source_target_pairs={{0,1},{1,2},{2,3},{3,4},{4,5},{5,6},{6,7},{8,9},{9,10},{10,11},{11... | collective-permute-start | bytes 322568 | tf_op jit(solution)/shard_map/ppermute | solution.py:14
  28.5 1.3 collective-permute-start.3
  30.6 3.8 %collective-permute-done.3 = bf16[3,70,256]{2,1,0:T(8,128)(2,1)S(1)} collective-permute-done((bf16[3,70,256]{2,1,0:T(8,128)(2,1)S(1)}, bf16[3,70,256]{2,1,0:T(8,128)(2,1)S(1)}, u32[]{:S(2)}, u32[]{:S(2)}) %collective-permute-start.3) | collective-permute-done | bytes 107552 | tf_op jit(solution)/shard_map/ppermute | solution.py:15
  34.4 1.3 maximum_maximum_fusion
  35.7 17.2 %fusion.55 = (f32[32,64]{1,0:T(8,128)S(1)}, f32[32,64,256]{2,1,0:T(8,128)S(1)}) fusion(f32[256]{0:T(256)S(1)} %bitcast.150, bf16[35,70,256]{2,1,0:T(8,128)(2,1)S(1)} %get-tuple-element.7, f32[256]{0:T(256)S(1)} %bitcast.151, f32[256]{0:T(256)S(1)} %bitcast.104, f32[256]{0:T(256)S(1)} %bitcast.105, f32[256]{0:T(256)S(1)} %bitcast.106, f32[256]{0:T(256)S(1)} %bitcast.107, ...), kind=kLoop, calls=%fused_computation.77 | loop fusion | flops 81786880 | bytes 50439168 | tf_op jit(solution)/shard_map/reduce_sum | solution.py:32
  53.7 1.6 %fusion.39 = bf16[2048,256]{1,0:T(8,128)(2,1)} fusion(f32[32,64,256]{2,1,0:T(8,128)S(1)} %get-tuple-element.3, f32[256]{0:T(256)S(1)} %copy-done.8, f32[2048]{0:T(1024)S(1)} %rsqrt.23, f32[2048]{0:T(1024)S(1)} %div.17), kind=kLoop, calls=%fused_computation.39 | loop fusion | flops 2097152 | bytes 3163136 | tf_op jit(solution)/shard_map/convert_element_type | solution.py:39
  55.4 5.0 %fusion.33 = bf16[2048,256]{1,0:T(8,128)(2,1)S(1)} fusion(bf16[1024,256]{1,0:T(8,128)(2,1)} %param.16, bf16[2048,256]{1,0:T(8,128)(2,1)} %fusion.39, bf16[256,1024]{1,0:T(8,128)(2,1)} %param.15, bf16[2048,256]{1,0:T(8,128)(2,1)} %bitcast.96), kind=kOutput, calls=%fused_computation.34 | convolution fusion | flops 2167930880 | bytes 4194304 | tf_op jit(solution)/shard_map/dot_general | solution.py:43
  60.4 1.4 %fusion.36 = bf16[2048,256]{1,0:T(8,128)(2,1)} fusion(bf16[2048,256]{1,0:T(8,128)(2,1)S(1)} %fusion.33, bf16[256,256]{1,0:T(8,128)(2,1)S(1)} %copy-done.6, f32[2048]{0:T(1024)S(1)} %convert_element_type.272), kind=kOutput, calls=%fused_computation.35 | convolution fusion | flops 269484032 | bytes 2236416 | tf_op jit(solution)/shard_map/dot_general | solution.py:72
  62.0 9.7 %scatter_fusion = bf16[256,16,256]{2,1,0:T(8,128)(2,1)S(1)} fusion(bf16[256,16,256]{2,1,0:T(8,128)(2,1)S(1)} %broadcast_in_dim.6, s32[128]{0:T(128)S(1)} %fusion.43, bf16[128,16,256]{2,1,0:T(8,128)(2,1)} %bitcast.100), kind=kCustom, calls=%fused_computation | custom fusion | bytes 3146240 | tf_op jit(solution)/shard_map/scatter | solution.py:86
  71.7 1.3 copy-done.4
  73.0 11.6 %all-to-all-start = ((bf16[128,2,16,256]{3,2,1,0:T(8,128)(2,1)}), bf16[128,2,16,256]{3,2,1,0:T(8,128)(2,1)S(1)}, u32[]{:S(2)}, u32[]{:S(2)}) async-start(bf16[128,2,16,256]{3,2,1,0:T(8,128)(2,1)} %bitcast.98), calls=%async_computation | async-start | bytes 4194304 | tf_op jit(solution)/shard_map/all_to_all | solution.py:96
  84.7 30.4 %all-to-all-done = bf16[128,2,16,256]{3,2,1,0:T(8,128)(2,1)S(1)} async-done(((bf16[128,2,16,256]{3,2,1,0:T(8,128)(2,1)}), bf16[128,2,16,256]{3,2,1,0:T(8,128)(2,1)S(1)}, u32[]{:S(2)}, u32[]{:S(2)}) %all-to-all-start) | async-done | bytes 2097184 | tf_op jit(solution)/shard_map/all_to_all | solution.py:96
  115.1 2.3 %fusion.54 = f32[128,2,16]{2,1,0:T(2,128)S(1)} fusion(bf16[128,2,16,256]{3,2,1,0:T(8,128)(2,1)S(1)} %all-to-all-done, bf16[1,128,2,16,256]{4,3,2,1,0:T(8,128)(2,1)} %param.20), kind=kLoop, calls=%fused_computation.76 | loop fusion | flops 4190208 | bytes 4210688 | tf_op jit(solution)/shard_map/reduce_sum | solution.py:32
  117.6 3.7 %multiply_reduce_fusion = (f32[128,2,16]{2,1,0:T(2,128)S(1)}, f32[128,2,16,256]{3,2,1,0:T(8,128)}) fusion(f32[128,2,16]{2,1,0:T(2,128)S(1)} %broadcast_multiply_fusion, bf16[128,2,16,256]{3,2,1,0:T(8,128)(2,1)S(1)} %all-to-all-done, bf16[1,128,2,16,256]{4,3,2,1,0:T(8,128)(2,1)} %param.20), kind=kLoop, calls=%fused_computation.29 | loop fusion | flops 6287360 | bytes 8421376 | tf_op jit(solution)/shard_map/reduce_sum | solution.py:34
  121.7 2.9 %fusion.25 = bf16[4096,256]{1,0:T(8,128)(2,1)S(1)} fusion(f32[128,2,16,256]{3,2,1,0:T(8,128)} %get-tuple-element.5, f32[256]{0:T(256)S(1)} %copy-done.9, f32[4096]{0:T(1024)S(1)} %rsqrt.25, f32[4096]{0:T(1024)S(1)} %div.20), kind=kLoop, calls=%fused_computation.27 | loop fusion | flops 4194304 | bytes 6325248 | tf_op jit(solution)/shard_map/convert_element_type | solution.py:39
  124.6 9.1 %fusion.18 = f32[4096,256]{1,0:T(8,128)} fusion(f32[4096,256]{1,0:T(8,128)} %bitcast.97, bf16[1024,256]{1,0:T(8,128)(2,1)S(1)} %copy-done, bf16[4096,256]{1,0:T(8,128)(2,1)S(1)} %fusion.25, bf16[256,1024]{1,0:T(8,128)(2,1)S(1)} %copy-done.10), kind=kOutput, calls=%fused_computation.21 | convolution fusion | flops 4333764608 | bytes 11534336 | tf_op jit(solution)/shard_map/dot_general | solution.py:43
  133.8 3.8 %multiply_convert_fusion = bf16[1,128,2,16,256]{4,3,2,1,0:T(8,128)(2,1)} fusion(f32[1,128,2,16,256]{4,3,2,1,0:T(8,128)} %bitcast.99, f32[128,2]{1,0:T(8,128)S(1)} %bitcast.102), kind=kLoop, calls=%fused_computation.28 | loop fusion | flops 2097152 | bytes 6292480 | tf_op jit(solution)/shard_map/convert_element_type | solution.py:106
  (48 shorter events, 6.6 us)
Async XLA Ops:
  0.6 124.0 %copy-start = (bf16[1024,256]{1,0:T(8,128)(2,1)S(1)}, bf16[1024,256]{1,0:T(8,128)(2,1)}, u32[]{:S(2)}) copy-start(bf16[1024,256]{1,0:T(8,128)(2,1)} %param.23) | copy-start | bytes 1572868
  0.6 24.4 %copy-start.1 = (bf16[32,64,256]{2,1,0:T(8,128)(2,1)S(1)}, bf16[32,64,256]{2,1,0:T(8,128)(2,1)}, u32[]{:S(2)}) copy-start(bf16[32,64,256]{2,1,0:T(8,128)(2,1)} %param.12) | copy-start | bytes 3145732
  0.7 24.3 %copy-start.7 = (s32[32,64]{1,0:T(8,128)S(1)}, s32[32,64]{1,0:T(8,128)}, u32[]{:S(2)}) copy-start(s32[32,64]{1,0:T(8,128)} %param.18) | copy-start | bytes 24580
  1.8 23.2 %collective-permute-start = (bf16[32,3,256]{2,1,0:T(4,128)(2,1)S(1)}, bf16[32,3,256]{2,1,0:T(4,128)(2,1)S(1)}, u32[]{:S(2)}, u32[]{:S(2)}) collective-permute-start(bf16[32,3,256]{2,1,0:T(4,128)(2,1)S(1)} %get-tuple-element.10), channel_id=1, source_target_pairs={{0,8},{8,16},{16,24},{24,32},{32,40},{40,48},{48,56},{56,64},{64,7... | collective-permute-start | bytes 147464 | tf_op jit(solution)/shard_map/ppermute | solution.py:14
  4.6 20.5 %collective-permute-start.1 = (bf16[32,3,256]{2,1,0:T(4,128)(2,1)S(1)}, bf16[32,3,256]{2,1,0:T(4,128)(2,1)S(1)}, u32[]{:S(2)}, u32[]{:S(2)}) collective-permute-start(bf16[32,3,256]{2,1,0:T(4,128)(2,1)S(1)} %get-tuple-element.11), channel_id=1, source_target_pairs={{8,0},{16,8},{24,16},{32,24},{40,32},{48,40},{56,48},{64,56},{72,6... | collective-permute-start | bytes 147464 | tf_op jit(solution)/shard_map/ppermute | solution.py:15
  9.1 62.6 %all-to-all-start.1 = ((bf16[128,1,2]{2,1,0:T(2,128)(2,1)}), bf16[128,1,2]{2,1,0:T(2,128)(2,1)S(1)}, u32[]{:S(2)}, u32[]{:S(2)}) async-start(bf16[128,1,2]{2,1,0:T(2,128)(2,1)} %all_to_all.12), calls=%async_computation.1 | async-start | bytes 131072 | tf_op jit(solution)/shard_map/all_to_all | solution.py:97
  25.1 5.5 %collective-permute-start.2 = (bf16[3,70,256]{2,1,0:T(8,128)(2,1)S(1)}, bf16[3,70,256]{2,1,0:T(8,128)(2,1)S(1)}, u32[]{:S(2)}, u32[]{:S(2)}) collective-permute-start(bf16[3,70,256]{2,1,0:T(8,128)(2,1)S(1)} %get-tuple-element.8), channel_id=1, source_target_pairs={{0,1},{1,2},{2,3},{3,4},{4,5},{5,6},{6,7},{8,9},{9,10},{10,11},{11... | collective-permute-start | bytes 322568 | tf_op jit(solution)/shard_map/ppermute | solution.py:14
  28.5 5.9 %collective-permute-start.3 = (bf16[3,70,256]{2,1,0:T(8,128)(2,1)S(1)}, bf16[3,70,256]{2,1,0:T(8,128)(2,1)S(1)}, u32[]{:S(2)}, u32[]{:S(2)}) collective-permute-start(bf16[3,70,256]{2,1,0:T(8,128)(2,1)S(1)} %get-tuple-element.9), channel_id=1, source_target_pairs={{1,0},{2,1},{3,2},{4,3},{5,4},{6,5},{7,6},{9,8},{10,9},{11,10},{12... | collective-permute-start | bytes 322568 | tf_op jit(solution)/shard_map/ppermute | solution.py:15
  29.9 5.8 %copy-start.3 = (bf16[32,67,256]{2,1,0:T(8,128)(2,1)}, bf16[32,67,256]{2,1,0:T(8,128)(2,1)S(1)}, u32[]{:S(2)}) copy-start(bf16[32,67,256]{2,1,0:T(8,128)(2,1)S(1)} %constant_dynamic-update-slice_fusion) | copy-start | bytes 3293188
  29.9 5.8 %copy-start.2 = (bf16[32,64,256]{2,1,0:T(8,128)(2,1)S(1)}, bf16[32,64,256]{2,1,0:T(8,128)(2,1)}, u32[]{:S(2)}) copy-start(bf16[32,64,256]{2,1,0:T(8,128)(2,1)} %param.12) | copy-start | bytes 3145732
  52.9 0.8 copy-start.8
  55.4 5.0 %copy-start.6 = (bf16[256,256]{1,0:T(8,128)(2,1)S(1)}, bf16[256,256]{1,0:T(8,128)(2,1)}, u32[]{:S(2)}) copy-start(bf16[256,256]{1,0:T(8,128)(2,1)} %param.17) | copy-start | bytes 393220
  60.4 1.4 %copy-start.5 = (bf16[2048,256]{1,0:T(8,128)(2,1)}, bf16[2048,256]{1,0:T(8,128)(2,1)S(1)}, u32[]{:S(2)}) copy-start(bf16[2048,256]{1,0:T(8,128)(2,1)S(1)} %fusion.33) | copy-start | bytes 3145732
  71.7 1.3 copy-start.4
  73.0 42.1 %all-to-all-start = ((bf16[128,2,16,256]{3,2,1,0:T(8,128)(2,1)}), bf16[128,2,16,256]{3,2,1,0:T(8,128)(2,1)S(1)}, u32[]{:S(2)}, u32[]{:S(2)}) async-start(bf16[128,2,16,256]{3,2,1,0:T(8,128)(2,1)} %bitcast.98), calls=%async_computation | async-start | bytes 4194304 | tf_op jit(solution)/shard_map/all_to_all | solution.py:96
  117.6 4.0 %copy-start.9 = (f32[256]{0:T(256)S(1)}, f32[256]{0:T(256)}, u32[]{:S(2)}) copy-start(f32[256]{0:T(256)} %param.21) | copy-start | bytes 3076
  121.7 2.9 %copy-start.10 = (bf16[256,1024]{1,0:T(8,128)(2,1)S(1)}, bf16[256,1024]{1,0:T(8,128)(2,1)}, u32[]{:S(2)}) copy-start(bf16[256,1024]{1,0:T(8,128)(2,1)} %param.22) | copy-start | bytes 1572868
where the time goes:
time: 138 us
  other arithmetic  36.2 us (26%)
  waiting for transfers between devices  34.9 us (25%)
  starting transfers between devices  30.6 us (22%)
  local copies, waits for them, and re-layouts  19.3 us (14%)
  matrix products  15.6 us (11%)
    all_to_all x1, waiting for transfers between devices, per_device(): lax.all_to_all(outgoing, ('lat', 'lon'), split_axis=0, concat_axis=0, til...  30.4 us
    reduce_sum x2, other arithmetic, normalize(): average = jnp.mean(values, axis=-1, keepdims=True)  19.5 us
    dot_general x2, matrix products, channel_mixer(): return jnp.dot(hidden, w_down, preferred_element_type=jnp.float32)  14.2 us
    all_to_all x1, starting transfers between devices, per_device(): lax.all_to_all(outgoing, ('lat', 'lon'), split_axis=0, concat_axis=0, til...  11.6 us
    all_to_all x1, starting transfers between devices, per_device(): lax.all_to_all(occupied, ('lat', 'lon'), split_axis=0, concat_axis=0, til...  11.5 us
    scatter x1, local copies, waits for them, and re-layouts, per_device(): outgoing = jnp.zeros((peer_count * capacity, tile_cells, channels), jnp.b...  9.72 us
    ppermute x2, starting transfers between devices, padded_2(): before = lax.ppermute(last, axis, up)  6.17 us
    convert_element_type x2, other arithmetic, channel_mixer(): normed = normalize(values, scales).astype(jnp.bfloat16)  4.57 us
  transfers between devices with their start and end apart: 6, of which 3 were waited for; matrix products, arithmetic and copies ran while one was open for 33% of the time, Pallas kernels for 0%

commit v1 on v0

--- a/solution.py
+++ b/solution.py
@@ -3,18 +3,41 @@
 from jax import lax
 from jax.sharding import PartitionSpec as P
 
+AXES = ("lat", "lon")
 
-def padded_2(x, sides, width, wrap):
-    for axis, dim in sides:
-        devices, length = (lax.axis_size(axis), x.shape[dim])
-        up = [(i, (i + 1) % devices) for i in range(devices if wrap else devices - 1)]
-        down = [(j, i) for i, j in up]
-        last = lax.slice_in_dim(x, length - width, length, axis=dim)
-        leading = lax.slice_in_dim(x, 0, width, axis=dim)
-        before = lax.ppermute(last, axis, up)
-        after = lax.ppermute(leading, axis, down)
-        x = jnp.concatenate([before, x, after], axis=dim)
-    return x
+
+def halo_pad(x, width):
+    n_lat, n_lon = lax.axis_size("lat"), lax.axis_size("lon")
+    rows, cols = x.shape[0], x.shape[1]
+
+    def lin(l, c):
+        return c * n_lat + l
+
+    def shift(piece, d_lat, d_lon):
+        pairs = []
+        for l in range(n_lat):
+            for c in range(n_lon):
+                tl = l + d_lat
+                if 0 <= tl < n_lat:
+                    pairs.append((lin(l, c), lin(tl, (c + d_lon) % n_lon)))
+        return lax.ppermute(piece, ("lon", "lat"), pairs)
+
+    top_rows = x[:width]
+    bottom_rows = x[rows - width:]
+    left_cols = x[:, :width]
+    right_cols = x[:, cols - width:]
+    from_above = shift(bottom_rows, 1, 0)
+    from_below = shift(top_rows, -1, 0)
+    from_left = shift(right_cols, 0, 1)
+    from_right = shift(left_cols, 0, -1)
+    c_above_left = shift(x[rows - width:, cols - width:], 1, 1)
+    c_above_right = shift(x[rows - width:, :width], 1, -1)
+    c_below_left = shift(x[:width, cols - width:], -1, 1)
+    c_below_right = shift(x[:width, :width], -1, -1)
+    top = jnp.concatenate([c_above_left, from_above, c_above_right], axis=1)
+    mid = jnp.concatenate([from_left, x, from_right], axis=1)
+    bottom = jnp.concatenate([c_below_left, from_below, c_below_right], axis=1)
+    return jnp.concatenate([top, mid, bottom], axis=0)
 
 
 def depthwise(padded, kernel, lat_rows, lon_cols):
@@ -59,8 +82,17 @@
 ):
     lat_rows, lon_cols, channels = atmosphere.shape
     margin = conv_weight.shape[0] // 2
-    lon_padded = padded_2(atmosphere, (("lon", 1),), margin, True)
-    padded = padded_2(lon_padded, (("lat", 0),), margin, False)
+    owners = tile_owner.reshape(-1)
+    tile_count = owners.shape[0]
+    peer_count = ocean_state.shape[1]
+    capacity = ocean_state.shape[2]
+    tile_cells = ocean_state.shape[3]
+    all_owners = lax.all_gather(owners, AXES, axis=0, tiled=False)
+    me = lax.axis_index("lat") * lax.axis_size("lon") + lax.axis_index("lon")
+    mine = jnp.sum((all_owners == me).astype(jnp.int32), axis=1)
+    filled = (jnp.arange(capacity, dtype=jnp.int32)[None, :] < mine[:, None]).astype(jnp.float32)
+
+    padded = halo_pad(atmosphere, margin)
     mixed = depthwise(padded, conv_weight, lat_rows, lon_cols).reshape(
         lat_rows * lon_cols, channels
     )
@@ -71,38 +103,20 @@
     fluxes = (
         jnp.dot(atmos_new, flux_weight, preferred_element_type=jnp.float32) * wet_cells
     ).astype(jnp.bfloat16)
-    owners = tile_owner.reshape(-1)
-    tile_count = owners.shape[0]
-    peer_count = ocean_state.shape[1]
-    capacity = ocean_state.shape[2]
-    tile_cells = ocean_state.shape[3]
-    flux_tiles = fluxes.reshape(tile_count, tile_cells, channels)
+    flux_tiles = fluxes.reshape(tile_count, tile_cells * channels)
     member = (owners[:, None] == jnp.arange(peer_count, dtype=jnp.int32)[None, :]).astype(jnp.int32)
     tile_rank = jnp.sum(jnp.cumsum(member, axis=0) * member, axis=1) - 1
     slot_index = owners * capacity + tile_rank
-    outgoing = (
-        jnp.zeros((peer_count * capacity, tile_cells, channels), jnp.bfloat16)
-        .at[slot_index]
-        .set(flux_tiles)
-    )
+    onehot = (
+        jnp.arange(peer_count * capacity, dtype=jnp.int32)[:, None] == slot_index[None, :]
+    ).astype(jnp.bfloat16)
+    outgoing = jnp.dot(onehot, flux_tiles, preferred_element_type=jnp.float32).astype(jnp.bfloat16)
     outgoing = outgoing.reshape(peer_count, capacity, tile_cells, channels)
-    occupied = (
-        jnp.zeros((peer_count * capacity,), jnp.bfloat16)
-        .at[slot_index]
-        .set(1.0)
-        .reshape(peer_count, capacity)
-    )
-    arrived, filled = (
-        lax.all_to_all(outgoing, ("lat", "lon"), split_axis=0, concat_axis=0, tiled=True),
-        lax.all_to_all(occupied, ("lat", "lon"), split_axis=0, concat_axis=0, tiled=True),
-    )
+    arrived = lax.all_to_all(outgoing, AXES, split_axis=0, concat_axis=0, tiled=True)
     states = ocean_state[0].astype(jnp.float32) + arrived.astype(jnp.float32)
     flat_states = states.reshape(peer_count * capacity * tile_cells, channels)
     result = flat_states + channel_mixer(flat_states, ocn_gain, ocn_up, ocn_down)
-    result = (
-        result.reshape(peer_count, capacity, tile_cells, channels)
-        * filled.astype(jnp.float32)[:, :, None, None]
-    )
+    result = result.reshape(peer_count, capacity, tile_cells, channels) * filled[:, :, None, None]
     ocean_out = result.astype(jnp.bfloat16)[None]
     return (atmos_new.reshape(lat_rows, lon_cols, channels), ocean_out)
 

time: 138 us -> 300 us (2.17)
  blocking collectives: 0 us -> 191 us
  waiting for transfers between devices: 34.9 us -> 8.11 us
  local copies, waits for them, and re-layouts: 19.3 us -> 11.2 us
  starting transfers between devices: 30.6 us -> 34.4 us
    all_gather x0 -> x1, blocking collectives: none -> 191 us  [per_device(): all_owners = lax.all_gather(owners, AXES, axis=0, tiled=False)]
    all_to_all x2 -> x1, waiting for transfers between devices: 30.4 us -> 0.01 us  [per_device(): lax.all_to_all(outgoing, AXES, split_axis=0, concat_axis=0, tiled=True)]
    ppermute x4 -> x8, starting transfers between devices: 7.47 us -> 22.9 us  [shift(): return lax.ppermute(piece, ('lon', 'lat'), pairs)]
    all_to_all x2 -> x1, starting transfers between devices: 23.1 us -> 11.5 us  [per_device(): lax.all_to_all(outgoing, AXES, split_axis=0, concat_axis=0, tiled=True)]
    scatter x2 -> x0, local copies, waits for them, and re-layouts: 11.1 us -> none  [the longest x1 9.72 us: per_device(): outgoing = jnp.zeros((peer_count * capacity, tile_cells, channels), jnp.b...]
    ppermute x4 -> x8, waiting for transfers between devices: 4.48 us -> 8.11 us  [shift(): return lax.ppermute(piece, ('lon', 'lat'), pairs)]
  transfers between devices with their start and end apart: 6 -> 9, of which waited for: 3 -> 2; matrix products, arithmetic and copies ran while one was open for 33% -> 4% of each run, Pallas kernels for 0% -> 0%
where the time goes in v1:
time: 300 us
  blocking collectives  191 us (64%)
  other arithmetic  38.8 us (13%)
  starting transfers between devices  34.4 us (11%)
  matrix products  15.3 us (5%)
  local copies, waits for them, and re-layouts  11.2 us (4%)
  waiting for transfers between devices  8.11 us (3%)
    all_gather x1, blocking collectives, per_device(): all_owners = lax.all_gather(owners, AXES, axis=0, tiled=False)  191 us
    ppermute x8, starting transfers between devices, shift(): return lax.ppermute(piece, ('lon', 'lat'), pairs)  22.9 us
    reduce_sum x2, other arithmetic, normalize(): average = jnp.mean(values, axis=-1, keepdims=True)  19.5 us
    dot_general x2, matrix products, channel_mixer(): return jnp.dot(hidden, w_down, preferred_element_type=jnp.float32)  14.2 us
    all_to_all x1, starting transfers between devices, per_device(): lax.all_to_all(outgoing, AXES, split_axis=0, concat_axis=0, tiled=True)  11.5 us
    ppermute x8, waiting for transfers between devices, shift(): return lax.ppermute(piece, ('lon', 'lat'), pairs)  8.11 us
  transfers between devices with their start and end apart: 9, of which 2 were waited for; matrix products, arithmetic and copies ran while one was open for 4% of the time, Pallas kernels for 0%

profile of v1, /device:TPU:1, one launch (start us, length us, event | category | flops | bytes accessed | tf_op | source)
XLA Modules:
  0.0 299.5 jit_solution(3679355529104258559)
XLA Ops:
  1.6 5.9 %collective-permute-start = (bf16[3,3,256]{2,1,0:T(4,128)(2,1)S(1)}, bf16[3,3,256]{2,1,0:T(4,128)(2,1)S(1)}, u32[]{:S(2)}, u32[]{:S(2)}) collective-permute-start(bf16[3,3,256]{2,1,0:T(4,128)(2,1)S(1)} %get-tuple-element.8), channel_id=1, source_target_pairs={{0,9},{8,17},{16,25},{24,33},{32,41},{40,49},{48,57},{56,65},{64,7... | collective-permute-start | bytes 13832 | tf_op jit(solution)/shard_map/ppermute | solution.py:23
  7.5 2.3 collective-permute-start.2
  9.8 1.3 collective-permute-start.5
  11.1 1.3 collective-permute-start.7
  12.4 1.0 fusion.58
  13.4 5.3 %collective-permute-start.4 = (bf16[32,3,256]{2,1,0:T(4,128)(2,1)S(1)}, bf16[32,3,256]{2,1,0:T(4,128)(2,1)S(1)}, u32[]{:S(2)}, u32[]{:S(2)}) collective-permute-start(bf16[32,3,256]{2,1,0:T(4,128)(2,1)S(1)} %get-tuple-element.15), channel_id=1, source_target_pairs={{0,120},{8,0},{16,8},{24,16},{32,24},{40,32},{48,40},{56,48},{64,5... | collective-permute-start | bytes 147464 | tf_op jit(solution)/shard_map/ppermute | solution.py:23
  20.6 1.0 fusion.60
  25.0 1.3 constant_dynamic-update-slice_fusion.1
  26.4 5.6 %collective-permute-start.1 = (bf16[3,64,256]{2,1,0:T(8,128)(2,1)S(1)}, bf16[3,64,256]{2,1,0:T(8,128)(2,1)S(1)}, u32[]{:S(2)}, u32[]{:S(2)}) collective-permute-start(bf16[3,64,256]{2,1,0:T(8,128)(2,1)S(1)} %get-tuple-element.12), channel_id=1, source_target_pairs={{0,1},{8,9},{16,17},{24,25},{32,33},{40,41},{48,49},{56,57},{64,65... | collective-permute-start | bytes 294920 | tf_op jit(solution)/shard_map/ppermute | solution.py:23
  32.0 1.3 collective-permute-start.6
  33.6 7.9 %collective-permute-done.6 = bf16[3,64,256]{2,1,0:T(8,128)(2,1)S(1)} collective-permute-done((bf16[3,64,256]{2,1,0:T(8,128)(2,1)S(1)}, bf16[3,64,256]{2,1,0:T(8,128)(2,1)S(1)}, u32[]{:S(2)}, u32[]{:S(2)}) %collective-permute-start.6) | collective-permute-done | bytes 98336 | tf_op jit(solution)/shard_map/ppermute | solution.py:23
  41.5 1.5 maximum_maximum_fusion
  43.0 17.2 %fusion.55 = (f32[32,64]{1,0:T(8,128)S(1)}, f32[32,64,256]{2,1,0:T(8,128)S(1)}) fusion(f32[256]{0:T(256)S(1)} %bitcast.145, bf16[35,70,256]{2,1,0:T(8,128)(2,1)S(1)} %get-tuple-element.7, f32[256]{0:T(256)S(1)} %bitcast.146, f32[256]{0:T(256)S(1)} %bitcast.99, f32[256]{0:T(256)S(1)} %bitcast.100, f32[256]{0:T(256)S(1)} %bitcast.101, f32[256]{0:T(256)S(1)} %bitcast.102, ...), kind=kLoop, calls=%fused_computation.75 | loop fusion | flops 81786880 | bytes 50439168 | tf_op jit(solution)/shard_map/reduce_sum | solution.py:55
  61.0 1.6 fusion.39
  62.7 5.0 %fusion.33 = bf16[2048,256]{1,0:T(8,128)(2,1)S(1)} fusion(bf16[1024,256]{1,0:T(8,128)(2,1)} %param.16, bf16[2048,256]{1,0:T(8,128)(2,1)} %fusion.39, bf16[256,1024]{1,0:T(8,128)(2,1)} %param.15, bf16[2048,256]{1,0:T(8,128)(2,1)} %bitcast.91), kind=kOutput, calls=%fused_computation.33 | convolution fusion | flops 2167930880 | bytes 4194304 | tf_op jit(solution)/shard_map/dot_general | solution.py:66
  70.4 2.0 copy.14
  72.4 11.5 %all-to-all-start = ((bf16[128,2,16,256]{3,2,1,0:T(8,128)(2,1)}), bf16[128,2,16,256]{3,2,1,0:T(8,128)(2,1)S(1)}, u32[]{:S(2)}, u32[]{:S(2)}) async-start(bf16[128,2,16,256]{3,2,1,0:T(8,128)(2,1)} %bitcast.92), calls=%async_computation | async-start | bytes 4194304 | tf_op jit(solution)/shard_map/all_to_all | solution.py:115
  83.9 190.7 %all-gather = s32[128,1,128]{2,1,0:T(1,128)S(1)} all-gather(s32[1,1,128]{2,1,0:T(1,128)S(1)} %copy-done.7), channel_id=2, replica_groups=mesh['lon'=16,'lat'=8] {'lat','lon'}, dimensions={0}, use_global_device_ids=true | all-gather | bytes 66048 | tf_op jit(solution)/shard_map/all_gather | solution.py:90
  274.6 2.4 fusion.42
  277.0 2.3 fusion.54
  279.6 3.7 %multiply_reduce_fusion = (f32[128,2,16]{2,1,0:T(2,128)S(1)}, f32[128,2,16,256]{3,2,1,0:T(8,128)}) fusion(f32[128,2,16]{2,1,0:T(2,128)S(1)} %broadcast_multiply_fusion, bf16[128,2,16,256]{3,2,1,0:T(8,128)(2,1)S(1)} %all-to-all-done, bf16[1,128,2,16,256]{4,3,2,1,0:T(8,128)(2,1)} %param.20), kind=kLoop, calls=%fused_computation.28 | loop fusion | flops 6287360 | bytes 8421376 | tf_op jit(solution)/shard_map/reduce_sum | solution.py:57
  283.6 2.9 fusion.25
  286.6 9.1 %fusion.18 = f32[4096,256]{1,0:T(8,128)} fusion(f32[4096,256]{1,0:T(8,128)} %bitcast.90, bf16[1024,256]{1,0:T(8,128)(2,1)S(1)} %copy-done, bf16[4096,256]{1,0:T(8,128)(2,1)S(1)} %fusion.25, bf16[256,1024]{1,0:T(8,128)(2,1)S(1)} %copy-done.10), kind=kOutput, calls=%fused_computation.19 | convolution fusion | flops 4333764608 | bytes 11534336 | tf_op jit(solution)/shard_map/dot_general | solution.py:66
  295.7 3.8 %multiply_convert_fusion = bf16[1,128,2,16,256]{4,3,2,1,0:T(8,128)(2,1)} fusion(f32[1,128,2,16,256]{4,3,2,1,0:T(8,128)} %bitcast.94, f32[128,2]{1,0:T(8,128)S(1)} %fusion.45), kind=kLoop, calls=%fused_computation.27 | loop fusion | flops 2097152 | bytes 6292480 | tf_op jit(solution)/shard_map/convert_element_type | solution.py:120
  (55 shorter events, 10.6 us)
Async XLA Ops:
  0.6 285.9 %copy-start = (bf16[1024,256]{1,0:T(8,128)(2,1)S(1)}, bf16[1024,256]{1,0:T(8,128)(2,1)}, u32[]{:S(2)}) copy-start(bf16[1024,256]{1,0:T(8,128)(2,1)} %param.23) | copy-start | bytes 1572868
  0.6 40.9 %copy-start.2 = (bf16[32,64,256]{2,1,0:T(8,128)(2,1)S(1)}, bf16[32,64,256]{2,1,0:T(8,128)(2,1)}, u32[]{:S(2)}) copy-start(bf16[32,64,256]{2,1,0:T(8,128)(2,1)} %param.12) | copy-start | bytes 3145732
  0.7 25.6 %copy-start.6 = (s32[32,64]{1,0:T(8,128)S(1)}, s32[32,64]{1,0:T(8,128)}, u32[]{:S(2)}) copy-start(s32[32,64]{1,0:T(8,128)} %param.18) | copy-start | bytes 24580
  1.6 24.8 %collective-permute-start = (bf16[3,3,256]{2,1,0:T(4,128)(2,1)S(1)}, bf16[3,3,256]{2,1,0:T(4,128)(2,1)S(1)}, u32[]{:S(2)}, u32[]{:S(2)}) collective-permute-start(bf16[3,3,256]{2,1,0:T(4,128)(2,1)S(1)} %get-tuple-element.8), channel_id=1, source_target_pairs={{0,9},{8,17},{16,25},{24,33},{32,41},{40,49},{48,57},{56,65},{64,7... | collective-permute-start | bytes 13832 | tf_op jit(solution)/shard_map/ppermute | solution.py:23
  7.5 18.9 %collective-permute-start.2 = (bf16[3,3,256]{2,1,0:T(4,128)(2,1)S(1)}, bf16[3,3,256]{2,1,0:T(4,128)(2,1)S(1)}, u32[]{:S(2)}, u32[]{:S(2)}) collective-permute-start(bf16[3,3,256]{2,1,0:T(4,128)(2,1)S(1)} %get-tuple-element.10), channel_id=1, source_target_pairs={{0,121},{8,1},{16,9},{24,17},{32,25},{40,33},{48,41},{56,49},{64,5... | collective-permute-start | bytes 13832 | tf_op jit(solution)/shard_map/ppermute | solution.py:23
  9.8 23.6 %collective-permute-start.5 = (bf16[3,3,256]{2,1,0:T(4,128)(2,1)S(1)}, bf16[3,3,256]{2,1,0:T(4,128)(2,1)S(1)}, u32[]{:S(2)}, u32[]{:S(2)}) collective-permute-start(bf16[3,3,256]{2,1,0:T(4,128)(2,1)S(1)} %get-tuple-element.9), channel_id=1, source_target_pairs={{1,8},{9,16},{17,24},{25,32},{33,40},{41,48},{49,56},{57,64},{65,7... | collective-permute-start | bytes 13832 | tf_op jit(solution)/shard_map/ppermute | solution.py:23
  11.1 22.4 %collective-permute-start.7 = (bf16[3,3,256]{2,1,0:T(4,128)(2,1)S(1)}, bf16[3,3,256]{2,1,0:T(4,128)(2,1)S(1)}, u32[]{:S(2)}, u32[]{:S(2)}) collective-permute-start(bf16[3,3,256]{2,1,0:T(4,128)(2,1)S(1)} %get-tuple-element.11), channel_id=1, source_target_pairs={{1,120},{9,0},{17,8},{25,16},{33,24},{41,32},{49,40},{57,48},{65,5... | collective-permute-start | bytes 13832 | tf_op jit(solution)/shard_map/ppermute | solution.py:23
  13.4 18.6 %collective-permute-start.4 = (bf16[32,3,256]{2,1,0:T(4,128)(2,1)S(1)}, bf16[32,3,256]{2,1,0:T(4,128)(2,1)S(1)}, u32[]{:S(2)}, u32[]{:S(2)}) collective-permute-start(bf16[32,3,256]{2,1,0:T(4,128)(2,1)S(1)} %get-tuple-element.15), channel_id=1, source_target_pairs={{0,120},{8,0},{16,8},{24,16},{32,24},{40,32},{48,40},{56,48},{64,5... | collective-permute-start | bytes 147464 | tf_op jit(solution)/shard_map/ppermute | solution.py:23
  26.4 7.1 %collective-permute-start.3 = (bf16[32,3,256]{2,1,0:T(4,128)(2,1)S(1)}, bf16[32,3,256]{2,1,0:T(4,128)(2,1)S(1)}, u32[]{:S(2)}, u32[]{:S(2)}) collective-permute-start(bf16[32,3,256]{2,1,0:T(4,128)(2,1)S(1)} %get-tuple-element.14), channel_id=1, source_target_pairs={{0,8},{8,16},{16,24},{24,32},{32,40},{40,48},{48,56},{56,64},{64,7... | collective-permute-start | bytes 147464 | tf_op jit(solution)/shard_map/ppermute | solution.py:23
  26.4 7.2 %collective-permute-start.1 = (bf16[3,64,256]{2,1,0:T(8,128)(2,1)S(1)}, bf16[3,64,256]{2,1,0:T(8,128)(2,1)S(1)}, u32[]{:S(2)}, u32[]{:S(2)}) collective-permute-start(bf16[3,64,256]{2,1,0:T(8,128)(2,1)S(1)} %get-tuple-element.12), channel_id=1, source_target_pairs={{0,1},{8,9},{16,17},{24,25},{32,33},{40,41},{48,49},{56,57},{64,65... | collective-permute-start | bytes 294920 | tf_op jit(solution)/shard_map/ppermute | solution.py:23
  32.0 9.5 %collective-permute-start.6 = (bf16[3,64,256]{2,1,0:T(8,128)(2,1)S(1)}, bf16[3,64,256]{2,1,0:T(8,128)(2,1)S(1)}, u32[]{:S(2)}, u32[]{:S(2)}) collective-permute-start(bf16[3,64,256]{2,1,0:T(8,128)(2,1)S(1)} %get-tuple-element.13), channel_id=1, source_target_pairs={{1,0},{9,8},{17,16},{25,24},{33,32},{41,40},{49,48},{57,56},{65,64... | collective-permute-start | bytes 294920 | tf_op jit(solution)/shard_map/ppermute | solution.py:23
  33.4 9.6 %copy-start.1 = (bf16[32,67,256]{2,1,0:T(8,128)(2,1)}, bf16[32,67,256]{2,1,0:T(8,128)(2,1)S(1)}, u32[]{:S(2)}) copy-start(bf16[32,67,256]{2,1,0:T(8,128)(2,1)S(1)} %constant_dynamic-update-slice_fusion) | copy-start | bytes 3293188
  33.4 9.6 %copy-start.3 = (bf16[32,64,256]{2,1,0:T(8,128)(2,1)S(1)}, bf16[32,64,256]{2,1,0:T(8,128)(2,1)}, u32[]{:S(2)}) copy-start(bf16[32,64,256]{2,1,0:T(8,128)(2,1)} %param.12) | copy-start | bytes 3145732
  60.2 0.8 copy-start.8
  62.7 6.0 %copy-start.5 = (bf16[256,256]{1,0:T(8,128)(2,1)S(1)}, bf16[256,256]{1,0:T(8,128)(2,1)}, u32[]{:S(2)}) copy-start(bf16[256,256]{1,0:T(8,128)(2,1)} %param.17) | copy-start | bytes 393220
  67.7 1.0 copy-start.4
  72.4 11.5 %copy-start.7 = (s32[1,1,128]{2,1,0:T(1,128)S(1)}, s32[1,1,128]{2,1,0:T(1,128)}, u32[]{:S(2)}) copy-start(s32[1,1,128]{2,1,0:T(1,128)} %param.19) | copy-start | bytes 1540
  72.4 204.6 %all-to-all-start = ((bf16[128,2,16,256]{3,2,1,0:T(8,128)(2,1)}), bf16[128,2,16,256]{3,2,1,0:T(8,128)(2,1)S(1)}, u32[]{:S(2)}, u32[]{:S(2)}) async-start(bf16[128,2,16,256]{3,2,1,0:T(8,128)(2,1)} %bitcast.92), calls=%async_computation | async-start | bytes 4194304 | tf_op jit(solution)/shard_map/all_to_all | solution.py:115
  279.6 4.0 %copy-start.9 = (f32[256]{0:T(256)S(1)}, f32[256]{0:T(256)}, u32[]{:S(2)}) copy-start(f32[256]{0:T(256)} %param.21) | copy-start | bytes 3076
  283.6 2.9 copy-start.10

commit v2 on v0

--- a/solution.py
+++ b/solution.py
@@ -2,6 +2,8 @@
 import jax.numpy as jnp
 from jax import lax
 from jax.sharding import PartitionSpec as P
+
+AXES = ("lat", "lon")
 
 
 def padded_2(x, sides, width, wrap):
@@ -59,6 +61,11 @@
 ):
     lat_rows, lon_cols, channels = atmosphere.shape
     margin = conv_weight.shape[0] // 2
+    owners = tile_owner.reshape(-1)
+    tile_count = owners.shape[0]
+    peer_count = ocean_state.shape[1]
+    capacity = ocean_state.shape[2]
+    tile_cells = ocean_state.shape[3]
     lon_padded = padded_2(atmosphere, (("lon", 1),), margin, True)
     padded = padded_2(lon_padded, (("lat", 0),), margin, False)
     mixed = depthwise(padded, conv_weight, lat_rows, lon_cols).reshape(
@@ -71,38 +78,23 @@
     fluxes = (
         jnp.dot(atmos_new, flux_weight, preferred_element_type=jnp.float32) * wet_cells
     ).astype(jnp.bfloat16)
-    owners = tile_owner.reshape(-1)
-    tile_count = owners.shape[0]
-    peer_count = ocean_state.shape[1]
-    capacity = ocean_state.shape[2]
-    tile_cells = ocean_state.shape[3]
-    flux_tiles = fluxes.reshape(tile_count, tile_cells, channels)
+    flux_tiles = fluxes.reshape(tile_count, tile_cells * channels)
     member = (owners[:, None] == jnp.arange(peer_count, dtype=jnp.int32)[None, :]).astype(jnp.int32)
     tile_rank = jnp.sum(jnp.cumsum(member, axis=0) * member, axis=1) - 1
     slot_index = owners * capacity + tile_rank
-    outgoing = (
-        jnp.zeros((peer_count * capacity, tile_cells, channels), jnp.bfloat16)
-        .at[slot_index]
-        .set(flux_tiles)
-    )
+    onehot = (
+        jnp.arange(peer_count * capacity, dtype=jnp.int32)[:, None] == slot_index[None, :]
+    ).astype(jnp.bfloat16)
+    outgoing = jnp.dot(onehot, flux_tiles, preferred_element_type=jnp.float32).astype(jnp.bfloat16)
+    used = jnp.sum(onehot.astype(jnp.float32), axis=1) > 0
+    outgoing = jnp.where(used[:, None], outgoing, jnp.nan).astype(jnp.bfloat16)
     outgoing = outgoing.reshape(peer_count, capacity, tile_cells, channels)
-    occupied = (
-        jnp.zeros((peer_count * capacity,), jnp.bfloat16)
-        .at[slot_index]
-        .set(1.0)
-        .reshape(peer_count, capacity)
-    )
-    arrived, filled = (
-        lax.all_to_all(outgoing, ("lat", "lon"), split_axis=0, concat_axis=0, tiled=True),
-        lax.all_to_all(occupied, ("lat", "lon"), split_axis=0, concat_axis=0, tiled=True),
-    )
+    arrived = lax.all_to_all(outgoing, AXES, split_axis=0, concat_axis=0, tiled=True)
+    filled = arrived[:, :, 0, 0] == arrived[:, :, 0, 0]
     states = ocean_state[0].astype(jnp.float32) + arrived.astype(jnp.float32)
     flat_states = states.reshape(peer_count * capacity * tile_cells, channels)
     result = flat_states + channel_mixer(flat_states, ocn_gain, ocn_up, ocn_down)
-    result = (
-        result.reshape(peer_count, capacity, tile_cells, channels)
-        * filled.astype(jnp.float32)[:, :, None, None]
-    )
+    result = jnp.where(filled[:, :, None, None], result.reshape(peer_count, capacity, tile_cells, channels), 0.0)
     ocean_out = result.astype(jnp.bfloat16)[None]
     return (atmos_new.reshape(lat_rows, lon_cols, channels), ocean_out)
 

time: 138 us -> 114 us (0.83)
  blocking collectives: 0 us -> 43.3 us
  waiting for transfers between devices: 34.9 us -> 4.3 us
  starting transfers between devices: 30.6 us -> 7.6 us
  local copies, waits for them, and re-layouts: 19.3 us -> 8.92 us
  other arithmetic: 36.2 us -> 33.7 us
    all_to_all x0 -> x1, blocking collectives: none -> 43.3 us  [per_device(): lax.all_to_all(outgoing, AXES, split_axis=0, concat_axis=0, tiled=True)]
    all_to_all x2 -> x0, waiting for transfers between devices: 30.4 us -> none  [the longest x1 30.4 us: per_device(): lax.all_to_all(outgoing, ('lat', 'lon'), split_axis=0, concat_axis=0, til...]
    all_to_all x2 -> x0, starting transfers between devices: 23.1 us -> none  [the longest x1 11.6 us: per_device(): lax.all_to_all(outgoing, ('lat', 'lon'), split_axis=0, concat_axis=0, til...]
    scatter x2 -> x0, local copies, waits for them, and re-layouts: 11.1 us -> none  [the longest x1 9.72 us: per_device(): outgoing = jnp.zeros((peer_count * capacity, tile_cells, channels), jnp.b...]
    reduce_sum x2, other arithmetic: 19.5 us -> 18 us  [normalize(): average = jnp.mean(values, axis=-1, keepdims=True)]
    unnamed x23 -> x27, local copies, waits for them, and re-layouts: 2.65 us -> 3.19 us
  transfers between devices with their start and end apart: 6 -> 4, of which waited for: 3 -> 2; matrix products, arithmetic and copies ran while one was open for 33% -> 6% of each run, Pallas kernels for 0% -> 0%
where the time goes in v2:
time: 114 us
  blocking collectives  43.3 us (38%)
  other arithmetic  33.7 us (30%)
  matrix products  15 us (13%)
  local copies, waits for them, and re-layouts  8.92 us (8%)
  starting transfers between devices  7.6 us (7%)
  waiting for transfers between devices  4.3 us (4%)
    all_to_all x1, blocking collectives, per_device(): lax.all_to_all(outgoing, AXES, split_axis=0, concat_axis=0, tiled=True)  43.3 us
    reduce_sum x2, other arithmetic, normalize(): average = jnp.mean(values, axis=-1, keepdims=True)  18 us
    dot_general x2, matrix products, channel_mixer(): return jnp.dot(hidden, w_down, preferred_element_type=jnp.float32)  13.8 us
    ppermute x2, starting transfers between devices, padded_2(): before = lax.ppermute(last, axis, up)  6.3 us
    convert_element_type x2, other arithmetic, channel_mixer(): normed = normalize(values, scales).astype(jnp.bfloat16)  4.57 us
    reduce_sum x2, other arithmetic, normalize(): spread = jnp.mean(centred * centred, axis=-1, keepdims=True)  4.37 us
    ppermute x2, waiting for transfers between devices, padded_2(): after = lax.ppermute(leading, axis, down)  3.95 us
    unnamed x27, local copies, waits for them, and re-layouts  3.19 us
  transfers between devices with their start and end apart: 4, of which 2 were waited for; matrix products, arithmetic and copies ran while one was open for 6% of the time, Pallas kernels for 0%

profile of v2, /device:TPU:1, one launch (start us, length us, event | category | flops | bytes accessed | tf_op | source)
XLA Modules:
  0.0 113.7 jit_solution(13519626661043151760)
XLA Ops:
  0.7 1.1 %fusion.56 = (bf16[32,3,256]{2,1,0:T(4,128)(2,1)S(1)}, bf16[32,3,256]{2,1,0:T(4,128)(2,1)S(1)}) fusion(bf16[32,64,256]{2,1,0:T(8,128)(2,1)} %param.12), kind=kLoop, calls=%fused_computation.80 | loop fusion | bytes 196608 | tf_op jit(solution)/shard_map/slice | solution.py:14
  1.8 2.8 %collective-permute-start = (bf16[32,3,256]{2,1,0:T(4,128)(2,1)S(1)}, bf16[32,3,256]{2,1,0:T(4,128)(2,1)S(1)}, u32[]{:S(2)}, u32[]{:S(2)}) collective-permute-start(bf16[32,3,256]{2,1,0:T(4,128)(2,1)S(1)} %get-tuple-element.10), channel_id=1, source_target_pairs={{0,8},{8,16},{16,24},{24,32},{32,40},{40,48},{48,56},{56,64},{64,7... | collective-permute-start | bytes 147464 | tf_op jit(solution)/shard_map/ppermute | solution.py:16
  4.6 0.9 fusion.59
  5.5 1.0 fusion.57
  6.5 1.0 fusion.58
  7.5 0.7 fusion.45
  8.4 0.8 select_reduce_fusion
  9.3 0.7 add_add_fusion
  10.1 1.3 %constant_dynamic-update-slice_fusion.1 = bf16[32,67,256]{2,1,0:T(8,128)(2,1)S(1)} fusion(bf16[32,64,256]{2,1,0:T(8,128)(2,1)} %param.12), kind=kLoop, calls=%fused_computation.66 | loop fusion | bytes 2097152
  11.5 3.5 %collective-permute-start.2 = (bf16[3,70,256]{2,1,0:T(8,128)(2,1)S(1)}, bf16[3,70,256]{2,1,0:T(8,128)(2,1)S(1)}, u32[]{:S(2)}, u32[]{:S(2)}) collective-permute-start(bf16[3,70,256]{2,1,0:T(8,128)(2,1)S(1)} %get-tuple-element.8), channel_id=1, source_target_pairs={{0,1},{1,2},{2,3},{3,4},{4,5},{5,6},{6,7},{8,9},{9,10},{10,11},{11... | collective-permute-start | bytes 322568 | tf_op jit(solution)/shard_map/ppermute | solution.py:16
  15.1 1.3 %collective-permute-start.3 = (bf16[3,70,256]{2,1,0:T(8,128)(2,1)S(1)}, bf16[3,70,256]{2,1,0:T(8,128)(2,1)S(1)}, u32[]{:S(2)}, u32[]{:S(2)}) collective-permute-start(bf16[3,70,256]{2,1,0:T(8,128)(2,1)S(1)} %get-tuple-element.9), channel_id=1, source_target_pairs={{1,0},{2,1},{3,2},{4,3},{5,4},{6,5},{7,6},{9,8},{10,9},{11,10},{12... | collective-permute-start | bytes 322568 | tf_op jit(solution)/shard_map/ppermute | solution.py:17
  16.8 3.9 %collective-permute-done.3 = bf16[3,70,256]{2,1,0:T(8,128)(2,1)S(1)} collective-permute-done((bf16[3,70,256]{2,1,0:T(8,128)(2,1)S(1)}, bf16[3,70,256]{2,1,0:T(8,128)(2,1)S(1)}, u32[]{:S(2)}, u32[]{:S(2)}) %collective-permute-start.3) | collective-permute-done | bytes 107552 | tf_op jit(solution)/shard_map/ppermute | solution.py:17
  20.8 1.3 %maximum_maximum_fusion = (bf16[35,70,256]{2,1,0:T(8,128)(2,1)S(1)}, bf16[35,70,256]{2,1,0:T(8,128)(2,1)S(1)}) fusion(bf16[32,3,256]{2,1,0:T(4,128)(2,1)S(1)} %collective-permute-done.1, bf16[32,64,256]{2,1,0:T(8,128)(2,1)S(1)} %copy-done.1, bf16[32,3,256]{2,1,0:T(4,128)(2,1)S(1)} %collective-permute-done, ...), kind=kLoop, calls=%fused_computation.44 | loop fusion | flops 10035200 | bytes 3870720 | tf_op jit(solution)/shard_map/concatenate | solution.py:18
  22.1 17.3 %fusion.55 = (f32[32,64]{1,0:T(8,128)S(1)}, f32[32,64,256]{2,1,0:T(8,128)S(1)}) fusion(f32[256]{0:T(256)S(1)} %bitcast.107, bf16[35,70,256]{2,1,0:T(8,128)(2,1)S(1)} %get-tuple-element.7, f32[256]{0:T(256)S(1)} %bitcast.108, f32[256]{0:T(256)S(1)} %bitcast.110, f32[256]{0:T(256)S(1)} %bitcast.111, f32[256]{0:T(256)S(1)} %bitcast.112, f32[256]{0:T(256)S(1)} %bitcast.113, ...), kind=kLoop, calls=%fused_computation.79 | loop fusion | flops 81786880 | bytes 50439168 | tf_op jit(solution)/shard_map/reduce_sum | solution.py:34
  40.2 1.6 %fusion.40 = bf16[2048,256]{1,0:T(8,128)(2,1)} fusion(f32[32,64,256]{2,1,0:T(8,128)S(1)} %get-tuple-element.3, f32[256]{0:T(256)S(1)} %copy-done.8, f32[2048]{0:T(1024)S(1)} %rsqrt.23, f32[2048]{0:T(1024)S(1)} %div.17), kind=kLoop, calls=%fused_computation.39 | loop fusion | flops 2097152 | bytes 3163136 | tf_op jit(solution)/shard_map/convert_element_type | solution.py:41
  41.8 5.0 %fusion.34 = bf16[2048,256]{1,0:T(8,128)(2,1)S(1)} fusion(bf16[1024,256]{1,0:T(8,128)(2,1)} %param.16, bf16[2048,256]{1,0:T(8,128)(2,1)} %fusion.40, bf16[256,1024]{1,0:T(8,128)(2,1)} %param.15, bf16[2048,256]{1,0:T(8,128)(2,1)} %bitcast.92), kind=kOutput, calls=%fused_computation.34 | convolution fusion | flops 2167930880 | bytes 4194304 | tf_op jit(solution)/shard_map/dot_general | solution.py:45
  46.9 1.0 copy-done.5
  48.8 0.7 fusion.23
  50.2 43.3 %all_to_all.5 = bf16[128,2,16,256]{3,2,1,0:T(8,128)(2,1)S(1)} all-to-all(bf16[128,2,16,256]{3,2,1,0:T(8,128)(2,1)S(1)} %bitcast.95), channel_id=1, replica_groups=mesh['lon'=16,'lat'=8] {'lat','lon'}, dimensions={0} | all-to-all | bytes 4194304 | tf_op jit(solution)/shard_map/all_to_all | solution.py:92
  93.5 0.7 fusion.54
  95.0 3.7 %multiply_reduce_fusion = (f32[128,2,16]{2,1,0:T(2,128)S(1)}, f32[128,2,16,256]{3,2,1,0:T(8,128)}) fusion(f32[128,2,16]{2,1,0:T(2,128)S(1)} %copy.38, bf16[128,2,16,256]{3,2,1,0:T(8,128)(2,1)S(1)} %all_to_all.5, bf16[1,128,2,16,256]{4,3,2,1,0:T(8,128)(2,1)} %param.20), kind=kLoop, calls=%fused_computation.29 | loop fusion | flops 6287360 | bytes 8421376 | tf_op jit(solution)/shard_map/reduce_sum | solution.py:36
  99.1 2.9 %fusion.26 = bf16[4096,256]{1,0:T(8,128)(2,1)S(1)} fusion(f32[128,2,16,256]{3,2,1,0:T(8,128)} %get-tuple-element.5, f32[256]{0:T(256)S(1)} %copy-done.9, f32[4096]{0:T(1024)S(1)} %rsqrt.25, f32[4096]{0:T(1024)S(1)} %div.20), kind=kLoop, calls=%fused_computation.27 | loop fusion | flops 4194304 | bytes 6325248 | tf_op jit(solution)/shard_map/convert_element_type | solution.py:41
  102.1 8.8 %fusion.18 = bf16[4096,256]{1,0:T(8,128)(2,1)} fusion(f32[4096,256]{1,0:T(8,128)} %bitcast.93, bf16[1024,256]{1,0:T(8,128)(2,1)S(1)} %copy-done, bf16[4096,256]{1,0:T(8,128)(2,1)S(1)} %fusion.26, bf16[256,1024]{1,0:T(8,128)(2,1)S(1)} %copy-done.10), kind=kOutput, calls=%fused_computation.19 | convolution fusion | flops 4334813184 | bytes 9437184 | tf_op jit(solution)/shard_map/dot_general | solution.py:45
  110.9 2.8 %select_convert_fusion = bf16[1,128,2,16,256]{4,3,2,1,0:T(8,128)(2,1)} fusion(bf16[1,128,2,16,256]{4,3,2,1,0:T(8,128)(2,1)} %bitcast.96, pred[128,2]{1,0:T(8,128)(4,1)S(1)} %copy.36), kind=kLoop, calls=%fused_computation.28 | loop fusion | flops 1048576 | bytes 4194560 | tf_op jit(solution)/shard_map/convert_element_type | solution.py:98
  (52 shorter events, 4.5 us)
Async XLA Ops:
  0.6 101.4 %copy-start = (bf16[1024,256]{1,0:T(8,128)(2,1)S(1)}, bf16[1024,256]{1,0:T(8,128)(2,1)}, u32[]{:S(2)}) copy-start(bf16[1024,256]{1,0:T(8,128)(2,1)} %param.23) | copy-start | bytes 1572868
  0.6 10.8 %copy-start.1 = (bf16[32,64,256]{2,1,0:T(8,128)(2,1)S(1)}, bf16[32,64,256]{2,1,0:T(8,128)(2,1)}, u32[]{:S(2)}) copy-start(bf16[32,64,256]{2,1,0:T(8,128)(2,1)} %param.12) | copy-start | bytes 3145732
  0.7 10.7 %copy-start.7 = (s32[32,64]{1,0:T(8,128)S(1)}, s32[32,64]{1,0:T(8,128)}, u32[]{:S(2)}) copy-start(s32[32,64]{1,0:T(8,128)} %param.18) | copy-start | bytes 24580
  1.8 9.6 %collective-permute-start = (bf16[32,3,256]{2,1,0:T(4,128)(2,1)S(1)}, bf16[32,3,256]{2,1,0:T(4,128)(2,1)S(1)}, u32[]{:S(2)}, u32[]{:S(2)}) collective-permute-start(bf16[32,3,256]{2,1,0:T(4,128)(2,1)S(1)} %get-tuple-element.10), channel_id=1, source_target_pairs={{0,8},{8,16},{16,24},{24,32},{32,40},{40,48},{48,56},{56,64},{64,7... | collective-permute-start | bytes 147464 | tf_op jit(solution)/shard_map/ppermute | solution.py:16
  4.6 6.9 %collective-permute-start.1 = (bf16[32,3,256]{2,1,0:T(4,128)(2,1)S(1)}, bf16[32,3,256]{2,1,0:T(4,128)(2,1)S(1)}, u32[]{:S(2)}, u32[]{:S(2)}) collective-permute-start(bf16[32,3,256]{2,1,0:T(4,128)(2,1)S(1)} %get-tuple-element.11), channel_id=1, source_target_pairs={{8,0},{16,8},{24,16},{32,24},{40,32},{48,40},{56,48},{64,56},{72,6... | collective-permute-start | bytes 147464 | tf_op jit(solution)/shard_map/ppermute | solution.py:17
  11.5 5.3 %collective-permute-start.2 = (bf16[3,70,256]{2,1,0:T(8,128)(2,1)S(1)}, bf16[3,70,256]{2,1,0:T(8,128)(2,1)S(1)}, u32[]{:S(2)}, u32[]{:S(2)}) collective-permute-start(bf16[3,70,256]{2,1,0:T(8,128)(2,1)S(1)} %get-tuple-element.8), channel_id=1, source_target_pairs={{0,1},{1,2},{2,3},{3,4},{4,5},{5,6},{6,7},{8,9},{9,10},{10,11},{11... | collective-permute-start | bytes 322568 | tf_op jit(solution)/shard_map/ppermute | solution.py:16
  15.1 5.7 %collective-permute-start.3 = (bf16[3,70,256]{2,1,0:T(8,128)(2,1)S(1)}, bf16[3,70,256]{2,1,0:T(8,128)(2,1)S(1)}, u32[]{:S(2)}, u32[]{:S(2)}) collective-permute-start(bf16[3,70,256]{2,1,0:T(8,128)(2,1)S(1)} %get-tuple-element.9), channel_id=1, source_target_pairs={{1,0},{2,1},{3,2},{4,3},{5,4},{6,5},{7,6},{9,8},{10,9},{11,10},{12... | collective-permute-start | bytes 322568 | tf_op jit(solution)/shard_map/ppermute | solution.py:17
  16.5 5.6 %copy-start.3 = (bf16[32,67,256]{2,1,0:T(8,128)(2,1)}, bf16[32,67,256]{2,1,0:T(8,128)(2,1)S(1)}, u32[]{:S(2)}) copy-start(bf16[32,67,256]{2,1,0:T(8,128)(2,1)S(1)} %constant_dynamic-update-slice_fusion) | copy-start | bytes 3293188
  16.5 5.6 %copy-start.2 = (bf16[32,64,256]{2,1,0:T(8,128)(2,1)S(1)}, bf16[32,64,256]{2,1,0:T(8,128)(2,1)}, u32[]{:S(2)}) copy-start(bf16[32,64,256]{2,1,0:T(8,128)(2,1)} %param.12) | copy-start | bytes 3145732
  39.3 0.8 copy-start.8
  41.8 6.0 %copy-start.6 = (bf16[256,256]{1,0:T(8,128)(2,1)S(1)}, bf16[256,256]{1,0:T(8,128)(2,1)}, u32[]{:S(2)}) copy-start(bf16[256,256]{1,0:T(8,128)(2,1)} %param.17) | copy-start | bytes 393220
  46.9 1.0 copy-start.5
  50.2 43.3 %copy-start.4 = (bf16[1,128,2,16,256]{4,3,2,1,0:T(8,128)(2,1)S(1)}, bf16[1,128,2,16,256]{4,3,2,1,0:T(8,128)(2,1)}, u32[]{:S(2)}) copy-start(bf16[1,128,2,16,256]{4,3,2,1,0:T(8,128)(2,1)} %param.20) | copy-start | bytes 6291460
  95.0 4.2 %copy-start.9 = (f32[256]{0:T(256)S(1)}, f32[256]{0:T(256)}, u32[]{:S(2)}) copy-start(f32[256]{0:T(256)} %param.21) | copy-start | bytes 3076
  99.1 2.9 %copy-start.10 = (bf16[256,1024]{1,0:T(8,128)(2,1)S(1)}, bf16[256,1024]{1,0:T(8,128)(2,1)}, u32[]{:S(2)}) copy-start(bf16[256,1024]{1,0:T(8,128)(2,1)} %param.22) | copy-start | bytes 1572868

commit v3 on v2

--- a/solution.py
+++ b/solution.py
@@ -1,7 +1,13 @@
+import functools
+
 import jax
 import jax.numpy as jnp
 from jax import lax
+from jax.experimental import pallas as pl
+from jax.experimental.pallas import tpu as pltpu
 from jax.sharding import PartitionSpec as P
+
+MESH = pl.DeviceIdType.MESH
 
 AXES = ("lat", "lon")
 
@@ -17,6 +23,67 @@
         after = lax.ppermute(leading, axis, down)
         x = jnp.concatenate([before, x, after], axis=dim)
     return x
+
+
+def a2a_body(n_lon, n, out_ref, recv_ref, send_sems, recv_sems):
+    me = lax.axis_index("lat") * n_lon + lax.axis_index("lon")
+
+    def coords(d):
+        return (lax.rem(d, n_lon), lax.div(d, n_lon))
+
+    barrier = pltpu.get_barrier_semaphore()
+
+    @pl.loop(1, n)
+    def _(j):
+        pl.semaphore_signal(barrier, inc=1, device_id=coords(lax.rem(me + j, n)), device_id_type=MESH)
+
+    pl.semaphore_wait(barrier, n - 1)
+
+    def send_copy(j):
+        peer = lax.rem(me + j, n)
+        return pltpu.make_async_remote_copy(
+            src_ref=out_ref.at[peer],
+            dst_ref=recv_ref.at[me],
+            send_sem=send_sems.at[j],
+            recv_sem=recv_sems.at[j],
+            device_id=coords(peer),
+            device_id_type=MESH,
+        )
+
+    def recv_copy(j):
+        source = lax.rem(me - j + n, n)
+        return pltpu.make_async_remote_copy(
+            src_ref=out_ref.at[source],
+            dst_ref=recv_ref.at[source],
+            send_sem=send_sems.at[j],
+            recv_sem=recv_sems.at[j],
+            device_id=coords(source),
+            device_id_type=MESH,
+        )
+
+    @pl.loop(1, n)
+    def _(j):
+        send_copy(j).start()
+
+    recv_ref[me] = out_ref[me]
+
+    @pl.loop(1, n)
+    def _(j):
+        send_copy(j).wait_send()
+        recv_copy(j).wait_recv()
+
+
+def all_to_all_kernel(outgoing):
+    n_lon = lax.axis_size("lon")
+    n = n_lon * lax.axis_size("lat")
+    return pl.pallas_call(
+        functools.partial(a2a_body, n_lon, n),
+        out_shape=jax.ShapeDtypeStruct(outgoing.shape, outgoing.dtype),
+        in_specs=[pl.BlockSpec(memory_space=pltpu.VMEM)],
+        out_specs=pl.BlockSpec(memory_space=pltpu.VMEM),
+        scratch_shapes=[pltpu.SemaphoreType.DMA((n,)), pltpu.SemaphoreType.DMA((n,))],
+        compiler_params=pltpu.CompilerParams(collective_id=0, has_side_effects=True),
+    )(outgoing)
 
 
 def depthwise(padded, kernel, lat_rows, lon_cols):
@@ -89,7 +156,7 @@
     used = jnp.sum(onehot.astype(jnp.float32), axis=1) > 0
     outgoing = jnp.where(used[:, None], outgoing, jnp.nan).astype(jnp.bfloat16)
     outgoing = outgoing.reshape(peer_count, capacity, tile_cells, channels)
-    arrived = lax.all_to_all(outgoing, AXES, split_axis=0, concat_axis=0, tiled=True)
+    arrived = all_to_all_kernel(outgoing)
     filled = arrived[:, :, 0, 0] == arrived[:, :, 0, 0]
     states = ocean_state[0].astype(jnp.float32) + arrived.astype(jnp.float32)
     flat_states = states.reshape(peer_count * capacity * tile_cells, channels)

time: 114 us -> 123 us (1.079)
  Pallas kernels: 0 us -> 47.1 us
  blocking collectives: 43.3 us -> 0 us
  other arithmetic: 33.7 us -> 37.4 us
    pallas_call x0 -> x1, Pallas kernels: none -> 47.1 us  [all_to_all_kernel(): pl.pallas_call(functools.partial(a2a_body, n_lon, n), out_shape=jax.Shape...]
    all_to_all x1 -> x0, blocking collectives: 43.3 us -> none  [per_device(): lax.all_to_all(outgoing, AXES, split_axis=0, concat_axis=0, tiled=True)]
    reduce_sum x2, other arithmetic: 18 us -> 20.3 us  [normalize(): average = jnp.mean(values, axis=-1, keepdims=True)]
    unnamed x27 -> x22, local copies, waits for them, and re-layouts: 3.19 us -> 4.28 us
where the time goes in v3:
time: 123 us; the launch traced here: 122 us
  Pallas kernels  47.1 us (38%)
  other arithmetic  37.4 us (30%)
  matrix products  15.1 us (12%)
  local copies, waits for them, and re-layouts  9.8 us (8%)
  starting transfers between devices  7.6 us (6%)
  waiting for transfers between devices  4.3 us (3%)
    pallas_call x1, Pallas kernels, all_to_all_kernel(): pl.pallas_call(functools.partial(a2a_body, n_lon, n), out_shape=jax.Shape...  47.1 us
    reduce_sum x2, other arithmetic, normalize(): average = jnp.mean(values, axis=-1, keepdims=True)  20.3 us
    dot_general x2, matrix products, channel_mixer(): return jnp.dot(hidden, w_down, preferred_element_type=jnp.float32)  13.9 us
    ppermute x2, starting transfers between devices, padded_2(): before = lax.ppermute(last, axis, up)  6.3 us
    convert_element_type x2, other arithmetic, channel_mixer(): normed = normalize(values, scales).astype(jnp.bfloat16)  4.68 us
    reduce_sum x2, other arithmetic, normalize(): spread = jnp.mean(centred * centred, axis=-1, keepdims=True)  4.37 us
    unnamed x22, local copies, waits for them, and re-layouts  4.28 us
    ppermute x2, waiting for transfers between devices, padded_2(): after = lax.ppermute(leading, axis, down)  3.95 us
  transfers between devices with their start and end apart: 4, of which 2 were waited for; matrix products, arithmetic and copies ran while one was open for 6% of the time, Pallas kernels for 0%

profile of v3, /device:TPU:1, one launch (start us, length us, event | category | flops | bytes accessed | tf_op | source)
XLA Modules:
  0.0 122.3 jit_solution(13213827287708275217)
XLA Ops:
  0.7 1.1 fusion.56
  1.8 2.8 %collective-permute-start = (bf16[32,3,256]{2,1,0:T(4,128)(2,1)S(1)}, bf16[32,3,256]{2,1,0:T(4,128)(2,1)S(1)}, u32[]{:S(2)}, u32[]{:S(2)}) collective-permute-start(bf16[32,3,256]{2,1,0:T(4,128)(2,1)S(1)} %get-tuple-element.10), channel_id=1, source_target_pairs={{0,8},{8,16},{16,24},{24,32},{32,40},{40,48},{48,56},{56,64},{64,7... | collective-permute-start | bytes 147464 | tf_op jit(solution)/shard_map/ppermute | solution.py:22
  4.6 0.9 fusion.59
  5.5 1.0 fusion.57
  6.5 1.0 fusion.58
  7.5 0.7 fusion.45
  8.4 0.8 select_reduce_fusion
  10.1 1.3 %constant_dynamic-update-slice_fusion.1 = bf16[32,67,256]{2,1,0:T(8,128)(2,1)S(1)} fusion(bf16[32,64,256]{2,1,0:T(8,128)(2,1)} %param.12), kind=kLoop, calls=%fused_computation.67 | loop fusion | bytes 2097152
  11.5 3.5 %collective-permute-start.2 = (bf16[3,70,256]{2,1,0:T(8,128)(2,1)S(1)}, bf16[3,70,256]{2,1,0:T(8,128)(2,1)S(1)}, u32[]{:S(2)}, u32[]{:S(2)}) collective-permute-start(bf16[3,70,256]{2,1,0:T(8,128)(2,1)S(1)} %get-tuple-element.8), channel_id=1, source_target_pairs={{0,1},{1,2},{2,3},{3,4},{4,5},{5,6},{6,7},{8,9},{9,10},{10,11},{11... | collective-permute-start | bytes 322568 | tf_op jit(solution)/shard_map/ppermute | solution.py:22
  15.1 1.3 %collective-permute-start.3 = (bf16[3,70,256]{2,1,0:T(8,128)(2,1)S(1)}, bf16[3,70,256]{2,1,0:T(8,128)(2,1)S(1)}, u32[]{:S(2)}, u32[]{:S(2)}) collective-permute-start(bf16[3,70,256]{2,1,0:T(8,128)(2,1)S(1)} %get-tuple-element.9), channel_id=1, source_target_pairs={{1,0},{2,1},{3,2},{4,3},{5,4},{6,5},{7,6},{9,8},{10,9},{11,10},{12... | collective-permute-start | bytes 322568 | tf_op jit(solution)/shard_map/ppermute | solution.py:23
  16.8 3.9 %collective-permute-done.3 = bf16[3,70,256]{2,1,0:T(8,128)(2,1)S(1)} collective-permute-done((bf16[3,70,256]{2,1,0:T(8,128)(2,1)S(1)}, bf16[3,70,256]{2,1,0:T(8,128)(2,1)S(1)}, u32[]{:S(2)}, u32[]{:S(2)}) %collective-permute-start.3) | collective-permute-done | bytes 107552 | tf_op jit(solution)/shard_map/ppermute | solution.py:23
  20.8 1.3 %maximum_maximum_fusion = (bf16[35,70,256]{2,1,0:T(8,128)(2,1)S(1)}, bf16[35,70,256]{2,1,0:T(8,128)(2,1)S(1)}) fusion(bf16[32,3,256]{2,1,0:T(4,128)(2,1)S(1)} %collective-permute-done.1, bf16[32,64,256]{2,1,0:T(8,128)(2,1)S(1)} %copy-done.2, bf16[32,3,256]{2,1,0:T(4,128)(2,1)S(1)} %collective-permute-done, ...), kind=kLoop, calls=%fused_computation.44 | loop fusion | flops 10035200 | bytes 3870720 | tf_op jit(solution)/shard_map/concatenate | solution.py:24
  22.1 17.3 %fusion.55 = (f32[32,64]{1,0:T(8,128)S(1)}, f32[32,64,256]{2,1,0:T(8,128)S(1)}) fusion(f32[256]{0:T(256)S(1)} %bitcast.106, bf16[35,70,256]{2,1,0:T(8,128)(2,1)S(1)} %get-tuple-element.7, f32[256]{0:T(256)S(1)} %bitcast.107, f32[256]{0:T(256)S(1)} %bitcast.109, f32[256]{0:T(256)S(1)} %bitcast.110, f32[256]{0:T(256)S(1)} %bitcast.111, f32[256]{0:T(256)S(1)} %bitcast.112, ...), kind=kLoop, calls=%fused_computation.79 | loop fusion | flops 81786880 | bytes 50439168 | tf_op jit(solution)/shard_map/reduce_sum | solution.py:101
  40.2 1.6 %fusion.40 = bf16[2048,256]{1,0:T(8,128)(2,1)} fusion(f32[32,64,256]{2,1,0:T(8,128)S(1)} %get-tuple-element.3, f32[256]{0:T(256)S(1)} %copy-done.8, f32[2048]{0:T(1024)S(1)} %rsqrt.23, f32[2048]{0:T(1024)S(1)} %div.17), kind=kLoop, calls=%fused_computation.39 | loop fusion | flops 2097152 | bytes 3163136 | tf_op jit(solution)/shard_map/convert_element_type | solution.py:108
  41.8 5.0 %fusion.34 = bf16[2048,256]{1,0:T(8,128)(2,1)S(1)} fusion(bf16[1024,256]{1,0:T(8,128)(2,1)} %param.16, bf16[2048,256]{1,0:T(8,128)(2,1)} %fusion.40, bf16[256,1024]{1,0:T(8,128)(2,1)} %param.15, bf16[2048,256]{1,0:T(8,128)(2,1)} %bitcast.91), kind=kOutput, calls=%fused_computation.34 | convolution fusion | flops 2167930880 | bytes 4194304 | tf_op jit(solution)/shard_map/dot_general | solution.py:112
  46.9 1.0 copy-done.5
  49.5 2.0 %copy.20 = bf16[32,8,16,256]{3,2,1,0:T(8,128)(2,1)} copy(bf16[32,8,16,256]{3,1,2,0:T(8,128)(2,1)S(1)} %bitcast.93) | data formatting | bytes 4194304
  51.5 47.1 %shard_map.131 = bf16[128,2,16,256]{3,2,1,0:T(8,128)(2,1)} custom-call(bf16[128,2,16,256]{3,2,1,0:T(8,128)(2,1)} %bitcast.94), custom_call_target="tpu_custom_call" | custom-call | tf_op jit(solution)/shard_map/pallas_call | solution.py:79
  98.6 1.2 slice_compare_fusion
  99.8 3.1 %fusion.54 = f32[128,2,16]{2,1,0:T(2,128)S(1)} fusion(bf16[128,2,16,256]{3,2,1,0:T(8,128)(2,1)} %shard_map.131, bf16[1,128,2,16,256]{4,3,2,1,0:T(8,128)(2,1)} %param.20), kind=kLoop, calls=%fused_computation.78 | loop fusion | flops 4190208 | bytes 4210688 | tf_op jit(solution)/shard_map/reduce_sum | solution.py:101
  103.2 3.7 %multiply_reduce_fusion = (f32[128,2,16]{2,1,0:T(2,128)S(1)}, f32[128,2,16,256]{3,2,1,0:T(8,128)}) fusion(f32[128,2,16]{2,1,0:T(2,128)S(1)} %broadcast_multiply_fusion, bf16[128,2,16,256]{3,2,1,0:T(8,128)(2,1)S(1)} %copy-done.1, bf16[1,128,2,16,256]{4,3,2,1,0:T(8,128)(2,1)} %param.20), kind=kLoop, calls=%fused_computation.29 | loop fusion | flops 6287360 | bytes 8421376 | tf_op jit(solution)/shard_map/reduce_sum | solution.py:103
  107.5 3.0 %fusion.26 = bf16[4096,256]{1,0:T(8,128)(2,1)S(1)} fusion(f32[128,2,16,256]{3,2,1,0:T(8,128)} %get-tuple-element.5, f32[256]{0:T(256)S(1)} %copy-done.9, f32[4096]{0:T(1024)S(1)} %rsqrt.25, f32[4096]{0:T(1024)S(1)} %div.20), kind=kLoop, calls=%fused_computation.27 | loop fusion | flops 4194304 | bytes 6325248 | tf_op jit(solution)/shard_map/convert_element_type | solution.py:108
  110.5 8.9 %fusion.18 = bf16[4096,256]{1,0:T(8,128)(2,1)} fusion(f32[4096,256]{1,0:T(8,128)} %bitcast.92, bf16[1024,256]{1,0:T(8,128)(2,1)S(1)} %copy-done, bf16[4096,256]{1,0:T(8,128)(2,1)S(1)} %fusion.26, bf16[256,1024]{1,0:T(8,128)(2,1)} %param.22), kind=kOutput, calls=%fused_computation.19 | convolution fusion | flops 4334813184 | bytes 9437184 | tf_op jit(solution)/shard_map/dot_general | solution.py:112
  119.4 2.8 %select_convert_fusion = bf16[1,128,2,16,256]{4,3,2,1,0:T(8,128)(2,1)} fusion(bf16[1,128,2,16,256]{4,3,2,1,0:T(8,128)(2,1)} %bitcast.95, pred[128,2]{1,0:T(8,128)(4,1)S(1)} %copy.19), kind=kLoop, calls=%fused_computation.28 | loop fusion | flops 1048576 | bytes 4194560 | tf_op jit(solution)/shard_map/convert_element_type | solution.py:165
  (45 shorter events, 4.8 us)
Async XLA Ops:
  0.6 109.9 %copy-start = (bf16[1024,256]{1,0:T(8,128)(2,1)S(1)}, bf16[1024,256]{1,0:T(8,128)(2,1)}, u32[]{:S(2)}) copy-start(bf16[1024,256]{1,0:T(8,128)(2,1)} %param.23) | copy-start | bytes 1572868
  0.6 10.8 %copy-start.2 = (bf16[32,64,256]{2,1,0:T(8,128)(2,1)S(1)}, bf16[32,64,256]{2,1,0:T(8,128)(2,1)}, u32[]{:S(2)}) copy-start(bf16[32,64,256]{2,1,0:T(8,128)(2,1)} %param.12) | copy-start | bytes 3145732
  0.7 10.7 %copy-start.7 = (s32[32,64]{1,0:T(8,128)S(1)}, s32[32,64]{1,0:T(8,128)}, u32[]{:S(2)}) copy-start(s32[32,64]{1,0:T(8,128)} %param.18) | copy-start | bytes 24580
  1.8 9.6 %collective-permute-start = (bf16[32,3,256]{2,1,0:T(4,128)(2,1)S(1)}, bf16[32,3,256]{2,1,0:T(4,128)(2,1)S(1)}, u32[]{:S(2)}, u32[]{:S(2)}) collective-permute-start(bf16[32,3,256]{2,1,0:T(4,128)(2,1)S(1)} %get-tuple-element.10), channel_id=1, source_target_pairs={{0,8},{8,16},{16,24},{24,32},{32,40},{40,48},{48,56},{56,64},{64,7... | collective-permute-start | bytes 147464 | tf_op jit(solution)/shard_map/ppermute | solution.py:22
  4.6 6.9 %collective-permute-start.1 = (bf16[32,3,256]{2,1,0:T(4,128)(2,1)S(1)}, bf16[32,3,256]{2,1,0:T(4,128)(2,1)S(1)}, u32[]{:S(2)}, u32[]{:S(2)}) collective-permute-start(bf16[32,3,256]{2,1,0:T(4,128)(2,1)S(1)} %get-tuple-element.11), channel_id=1, source_target_pairs={{8,0},{16,8},{24,16},{32,24},{40,32},{48,40},{56,48},{64,56},{72,6... | collective-permute-start | bytes 147464 | tf_op jit(solution)/shard_map/ppermute | solution.py:23
  11.5 5.3 %collective-permute-start.2 = (bf16[3,70,256]{2,1,0:T(8,128)(2,1)S(1)}, bf16[3,70,256]{2,1,0:T(8,128)(2,1)S(1)}, u32[]{:S(2)}, u32[]{:S(2)}) collective-permute-start(bf16[3,70,256]{2,1,0:T(8,128)(2,1)S(1)} %get-tuple-element.8), channel_id=1, source_target_pairs={{0,1},{1,2},{2,3},{3,4},{4,5},{5,6},{6,7},{8,9},{9,10},{10,11},{11... | collective-permute-start | bytes 322568 | tf_op jit(solution)/shard_map/ppermute | solution.py:22
  15.1 5.7 %collective-permute-start.3 = (bf16[3,70,256]{2,1,0:T(8,128)(2,1)S(1)}, bf16[3,70,256]{2,1,0:T(8,128)(2,1)S(1)}, u32[]{:S(2)}, u32[]{:S(2)}) collective-permute-start(bf16[3,70,256]{2,1,0:T(8,128)(2,1)S(1)} %get-tuple-element.9), channel_id=1, source_target_pairs={{1,0},{2,1},{3,2},{4,3},{5,4},{6,5},{7,6},{9,8},{10,9},{11,10},{12... | collective-permute-start | bytes 322568 | tf_op jit(solution)/shard_map/ppermute | solution.py:23
  16.5 5.6 %copy-start.4 = (bf16[32,67,256]{2,1,0:T(8,128)(2,1)}, bf16[32,67,256]{2,1,0:T(8,128)(2,1)S(1)}, u32[]{:S(2)}) copy-start(bf16[32,67,256]{2,1,0:T(8,128)(2,1)S(1)} %constant_dynamic-update-slice_fusion) | copy-start | bytes 3293188
  16.5 5.6 %copy-start.3 = (bf16[32,64,256]{2,1,0:T(8,128)(2,1)S(1)}, bf16[32,64,256]{2,1,0:T(8,128)(2,1)}, u32[]{:S(2)}) copy-start(bf16[32,64,256]{2,1,0:T(8,128)(2,1)} %param.12) | copy-start | bytes 3145732
  39.3 0.8 copy-start.8
  41.8 6.0 %copy-start.6 = (bf16[256,256]{1,0:T(8,128)(2,1)S(1)}, bf16[256,256]{1,0:T(8,128)(2,1)}, u32[]{:S(2)}) copy-start(bf16[256,256]{1,0:T(8,128)(2,1)} %param.17) | copy-start | bytes 393220
  46.9 1.0 copy-start.5
  99.8 3.3 %copy-start.1 = (bf16[128,2,16,256]{3,2,1,0:T(8,128)(2,1)S(1)}, bf16[128,2,16,256]{3,2,1,0:T(8,128)(2,1)}, u32[]{:S(2)}) copy-start(bf16[128,2,16,256]{3,2,1,0:T(8,128)(2,1)} %shard_map.131) | copy-start | bytes 6291460
  103.1 4.3 %copy-start.9 = (f32[256]{0:T(256)S(1)}, f32[256]{0:T(256)}, u32[]{:S(2)}) copy-start(f32[256]{0:T(256)} %param.21) | copy-start | bytes 3076

commit v4 on v3

--- a/solution.py
+++ b/solution.py
@@ -25,7 +25,8 @@
     return x
 
 
-def a2a_body(n_lon, n, out_ref, recv_ref, send_sems, recv_sems):
+def exchange_body(n_lon, n, group, out_ref, state_ref, gain_ref, up_ref, down_ref,
+                  res_ref, recv_ref, stage_ref, send_sems, recv_sems):
     me = lax.axis_index("lat") * n_lon + lax.axis_index("lon")
 
     def coords(d):
@@ -43,7 +44,7 @@
         peer = lax.rem(me + j, n)
         return pltpu.make_async_remote_copy(
             src_ref=out_ref.at[peer],
-            dst_ref=recv_ref.at[me],
+            dst_ref=recv_ref.at[j],
             send_sem=send_sems.at[j],
             recv_sem=recv_sems.at[j],
             device_id=coords(peer),
@@ -54,7 +55,7 @@
         source = lax.rem(me - j + n, n)
         return pltpu.make_async_remote_copy(
             src_ref=out_ref.at[source],
-            dst_ref=recv_ref.at[source],
+            dst_ref=recv_ref.at[j],
             send_sem=send_sems.at[j],
             recv_sem=recv_sems.at[j],
             device_id=coords(source),
@@ -65,25 +66,72 @@
     def _(j):
         send_copy(j).start()
 
-    recv_ref[me] = out_ref[me]
+    recv_ref[0] = out_ref[me]
+    slots, cells, channels = out_ref.shape[1], out_ref.shape[2], out_ref.shape[3]
+    rows = group * slots * cells
+
+    @pl.loop(0, n // group)
+    def _(g):
+        base = g * group
+
+        @pl.loop(0, group)
+        def _(i):
+            j = base + i
+
+            @pl.when(j > 0)
+            def _():
+                recv_copy(j).wait_recv()
+
+            stage_ref[i] = state_ref[lax.rem(me - j + n, n)]
+
+        fluxes = recv_ref[pl.ds(base, group)]
+        used = fluxes[:, :, 0:1, 0:1] == fluxes[:, :, 0:1, 0:1]
+        states = (stage_ref[...].astype(jnp.float32) + fluxes.astype(jnp.float32)).reshape(rows, channels)
+        average = jnp.mean(states, axis=-1, keepdims=True)
+        centred = states - average
+        spread = jnp.mean(centred * centred, axis=-1, keepdims=True)
+        normed = (centred * lax.rsqrt(spread + 1e-06) * gain_ref[...]).astype(jnp.bfloat16)
+        hidden = jax.nn.gelu(
+            jnp.dot(normed, up_ref[...], preferred_element_type=jnp.float32), approximate=True
+        ).astype(jnp.bfloat16)
+        result = states + jnp.dot(hidden, down_ref[...], preferred_element_type=jnp.float32)
+        result = result.reshape(group, slots, cells, channels)
+        stage_ref[...] = jnp.where(used, result, 0.0).astype(jnp.bfloat16)
+
+        @pl.loop(0, group)
+        def _(i):
+            res_ref[lax.rem(me - base - i + n, n)] = stage_ref[i]
 
     @pl.loop(1, n)
     def _(j):
         send_copy(j).wait_send()
-        recv_copy(j).wait_recv()
-
-
-def all_to_all_kernel(outgoing):
+
+
+def exchange_and_ocean(outgoing, state, gain, w_up, w_down):
     n_lon = lax.axis_size("lon")
     n = n_lon * lax.axis_size("lat")
+    group = 16
+    rows = outgoing.shape[0] * outgoing.shape[1] * outgoing.shape[2]
+    channels, hid = w_up.shape
+    vmem = pl.BlockSpec(memory_space=pltpu.VMEM)
     return pl.pallas_call(
-        functools.partial(a2a_body, n_lon, n),
+        functools.partial(exchange_body, n_lon, n, group),
         out_shape=jax.ShapeDtypeStruct(outgoing.shape, outgoing.dtype),
-        in_specs=[pl.BlockSpec(memory_space=pltpu.VMEM)],
-        out_specs=pl.BlockSpec(memory_space=pltpu.VMEM),
-        scratch_shapes=[pltpu.SemaphoreType.DMA((n,)), pltpu.SemaphoreType.DMA((n,))],
-        compiler_params=pltpu.CompilerParams(collective_id=0, has_side_effects=True),
-    )(outgoing)
+        in_specs=[vmem] * 5,
+        out_specs=vmem,
+        scratch_shapes=[
+            pltpu.VMEM(outgoing.shape, outgoing.dtype),
+            pltpu.VMEM((group,) + outgoing.shape[1:], outgoing.dtype),
+            pltpu.SemaphoreType.DMA((n,)),
+            pltpu.SemaphoreType.DMA((n,)),
+        ],
+        compiler_params=pltpu.CompilerParams(
+            collective_id=0, has_side_effects=True, vmem_limit_bytes=48 * 1024 * 1024
+        ),
+        cost_estimate=pl.CostEstimate(
+            flops=4 * rows * channels * hid, transcendentals=rows * hid, bytes_accessed=4 * rows * channels * 2
+        ),
+    )(outgoing, state, gain.reshape(1, channels), w_up, w_down)
 
 
 def depthwise(padded, kernel, lat_rows, lon_cols):
@@ -156,13 +204,7 @@
     used = jnp.sum(onehot.astype(jnp.float32), axis=1) > 0
     outgoing = jnp.where(used[:, None], outgoing, jnp.nan).astype(jnp.bfloat16)
     outgoing = outgoing.reshape(peer_count, capacity, tile_cells, channels)
-    arrived = all_to_all_kernel(outgoing)
-    filled = arrived[:, :, 0, 0] == arrived[:, :, 0, 0]
-    states = ocean_state[0].astype(jnp.float32) + arrived.astype(jnp.float32)
-    flat_states = states.reshape(peer_count * capacity * tile_cells, channels)
-    result = flat_states + channel_mixer(flat_states, ocn_gain, ocn_up, ocn_down)
-    result = jnp.where(filled[:, :, None, None], result.reshape(peer_count, capacity, tile_cells, channels), 0.0)
-    ocean_out = result.astype(jnp.bfloat16)[None]
+    ocean_out = exchange_and_ocean(outgoing, ocean_state[0], ocn_gain, ocn_up, ocn_down)[None]
     return (atmos_new.reshape(lat_rows, lon_cols, channels), ocean_out)
 
 

time: 123 us -> 106 us (0.86)
  the two profiles are of different devices: /device:TPU:1 before, /device:TPU:99 now
where the time goes in v4:
time: 106 us; the launch traced here: 105 us
  Pallas kernels  56.1 us (53%)
  other arithmetic  23.5 us (22%)
  local copies, waits for them, and re-layouts  9.65 us (9%)
  starting transfers between devices  7.21 us (7%)
  matrix products  6.02 us (6%)
  waiting for transfers between devices  1.66 us (2%)
    pallas_call x1, Pallas kernels, exchange_and_ocean(): pl.pallas_call(functools.partial(exchange_body, n_lon, n, group), out_sha...  56.1 us
    reduce_sum x1, other arithmetic, normalize(): average = jnp.mean(values, axis=-1, keepdims=True)  17.4 us
    dot_general x1, matrix products, channel_mixer(): return jnp.dot(hidden, w_down, preferred_element_type=jnp.float32)  4.88 us
    unnamed x25, local copies, waits for them, and re-layouts  4.8 us
    ppermute x2, starting transfers between devices, padded_2(): after = lax.ppermute(leading, axis, down)  4 us
    ppermute x2, starting transfers between devices, padded_2(): before = lax.ppermute(last, axis, up)  3.22 us
    slice x3, local copies, waits for them, and re-layouts, depthwise(): summed = summed + window * kernel[row_off, col_off]  2.92 us
  transfers between devices with their start and end apart: 4, of which 2 were waited for; matrix products, arithmetic and copies ran while one was open for 7% of the time, Pallas kernels for 0%

profile of v4, /device:TPU:99, one launch (start us, length us, event | category | flops | bytes accessed | tf_op | source)
XLA Modules:
  0.0 105.1 jit_solution(9893012226890625434)
XLA Ops:
  0.7 1.1 %fusion.33 = (bf16[32,3,256]{2,1,0:T(4,128)(2,1)S(1)}, bf16[32,3,256]{2,1,0:T(4,128)(2,1)S(1)}) fusion(bf16[32,64,256]{2,1,0:T(8,128)(2,1)} %param.12), kind=kLoop, calls=%fused_computation.53 | loop fusion | bytes 196608 | tf_op jit(solution)/shard_map/slice | solution.py:20
  1.8 1.9 %collective-permute-start = (bf16[32,3,256]{2,1,0:T(4,128)(2,1)S(1)}, bf16[32,3,256]{2,1,0:T(4,128)(2,1)S(1)}, u32[]{:S(2)}, u32[]{:S(2)}) collective-permute-start(bf16[32,3,256]{2,1,0:T(4,128)(2,1)S(1)} %get-tuple-element.8), channel_id=1, source_target_pairs={{0,8},{8,16},{16,24},{24,32},{32,40},{40,48},{48,56},{56,64},{64,7... | collective-permute-start | bytes 147464 | tf_op jit(solution)/shard_map/ppermute | solution.py:22
  3.7 1.0 fusion.34
  4.7 1.0 fusion.35
  5.8 0.9 fusion.36
  6.7 0.7 fusion.27
  7.6 0.8 select_reduce_fusion
  8.4 0.7 add_add_fusion
  9.2 1.3 %constant_dynamic-update-slice_fusion.1 = bf16[32,67,256]{2,1,0:T(8,128)(2,1)S(1)} fusion(bf16[32,64,256]{2,1,0:T(8,128)(2,1)} %param.12), kind=kLoop, calls=%fused_computation.45 | loop fusion | bytes 2097152
  10.7 1.3 %collective-permute-start.2 = (bf16[3,70,256]{2,1,0:T(8,128)(2,1)S(1)}, bf16[3,70,256]{2,1,0:T(8,128)(2,1)S(1)}, u32[]{:S(2)}, u32[]{:S(2)}) collective-permute-start(bf16[3,70,256]{2,1,0:T(8,128)(2,1)S(1)} %get-tuple-element.6), channel_id=1, source_target_pairs={{0,1},{1,2},{2,3},{3,4},{4,5},{5,6},{6,7},{8,9},{9,10},{10,11},{11... | collective-permute-start | bytes 322568 | tf_op jit(solution)/shard_map/ppermute | solution.py:22
  12.0 4.0 %collective-permute-start.3 = (bf16[3,70,256]{2,1,0:T(8,128)(2,1)S(1)}, bf16[3,70,256]{2,1,0:T(8,128)(2,1)S(1)}, u32[]{:S(2)}, u32[]{:S(2)}) collective-permute-start(bf16[3,70,256]{2,1,0:T(8,128)(2,1)S(1)} %get-tuple-element.7), channel_id=1, source_target_pairs={{1,0},{2,1},{3,2},{4,3},{5,4},{6,5},{7,6},{9,8},{10,9},{11,10},{12... | collective-permute-start | bytes 322568 | tf_op jit(solution)/shard_map/ppermute | solution.py:23
  16.2 1.5 %collective-permute-done.3 = bf16[3,70,256]{2,1,0:T(8,128)(2,1)S(1)} collective-permute-done((bf16[3,70,256]{2,1,0:T(8,128)(2,1)S(1)}, bf16[3,70,256]{2,1,0:T(8,128)(2,1)S(1)}, u32[]{:S(2)}, u32[]{:S(2)}) %collective-permute-start.3) | collective-permute-done | bytes 107552 | tf_op jit(solution)/shard_map/ppermute | solution.py:23
  17.7 1.3 %maximum_maximum_fusion = (bf16[35,70,256]{2,1,0:T(8,128)(2,1)S(1)}, bf16[35,70,256]{2,1,0:T(8,128)(2,1)S(1)}) fusion(bf16[32,3,256]{2,1,0:T(4,128)(2,1)S(1)} %collective-permute-done.1, bf16[32,64,256]{2,1,0:T(8,128)(2,1)S(1)} %copy-done.4, bf16[32,3,256]{2,1,0:T(4,128)(2,1)S(1)} %collective-permute-done, ...), kind=kLoop, calls=%fused_computation.25 | loop fusion | flops 10035200 | bytes 3870720 | tf_op jit(solution)/shard_map/concatenate | solution.py:24
  19.0 17.4 %fusion.32 = (f32[32,64]{1,0:T(8,128)S(1)}, f32[32,64,256]{2,1,0:T(8,128)S(1)}) fusion(f32[256]{0:T(256)S(1)} %bitcast.127, bf16[35,70,256]{2,1,0:T(8,128)(2,1)S(1)} %get-tuple-element.5, f32[256]{0:T(256)S(1)} %bitcast.128, f32[256]{0:T(256)S(1)} %bitcast.81, f32[256]{0:T(256)S(1)} %bitcast.82, f32[256]{0:T(256)S(1)} %bitcast.83, f32[256]{0:T(256)S(1)} %bitcast.84, ...), kind=kLoop, calls=%fused_computation.52 | loop fusion | flops 81786880 | bytes 50439168 | tf_op jit(solution)/shard_map/reduce_sum | solution.py:149
  36.5 0.6 multiply_reduce_fusion
  37.2 1.6 %fusion.22 = bf16[2048,256]{1,0:T(8,128)(2,1)} fusion(f32[32,64,256]{2,1,0:T(8,128)S(1)} %get-tuple-element.3, f32[256]{0:T(256)S(1)} %copy-done.10, f32[2048]{0:T(1024)S(1)} %rsqrt.12, f32[2048]{0:T(1024)S(1)} %div.9), kind=kLoop, calls=%fused_computation.20 | loop fusion | flops 2097152 | bytes 3163136 | tf_op jit(solution)/shard_map/convert_element_type | solution.py:156
  38.9 4.9 %fusion.16 = bf16[2048,256]{1,0:T(8,128)(2,1)S(1)} fusion(bf16[1024,256]{1,0:T(8,128)(2,1)S(1)} %copy-done, bf16[2048,256]{1,0:T(8,128)(2,1)} %fusion.22, bf16[256,1024]{1,0:T(8,128)(2,1)} %param.15, bf16[2048,256]{1,0:T(8,128)(2,1)} %bitcast.77), kind=kOutput, calls=%fused_computation.15 | convolution fusion | flops 2167930880 | bytes 4194304 | tf_op jit(solution)/shard_map/dot_general | solution.py:160
  43.8 1.0 copy-done.7
  44.7 0.4 fusion.19
  45.2 0.5 reshape.83
  45.7 0.7 fusion.8
  46.5 0.6 copy.14
  47.6 56.1 %shard_map.131 = bf16[128,2,16,256]{3,2,1,0:T(8,128)(2,1)S(1)} custom-call(bf16[128,2,16,256]{3,2,1,0:T(8,128)(2,1)S(1)} %bitcast.74, bf16[128,2,16,256]{3,2,1,0:T(8,128)(2,1)} %bitcast.131, f32[1,256]{1,0:T(1,128)S(1)} %bitcast.76, bf16[256,1024]{1,0:T(8,128)(2,1)S(1)} %copy-done.1, bf16[1024,256]{1,0:T(8,128)(2,1)S(1)} %copy-done.2), custom_call_target="tpu_custom_call" | custom-call | flops 4294967296 | bytes 8388608 | tf_op jit(solution)/shard_map/pallas_call | solution.py:117
  103.8 1.3 %copy.17 = bf16[1,128,2,16,256]{4,3,2,1,0:T(8,128)(2,1)} copy(bf16[1,128,2,16,256]{4,3,2,1,0:T(8,128)(2,1)S(1)} %bitcast.75) | data formatting | bytes 4194304
  (36 shorter events, 1.3 us)
Async XLA Ops:
  0.6 38.2 %copy-start = (bf16[1024,256]{1,0:T(8,128)(2,1)S(1)}, bf16[1024,256]{1,0:T(8,128)(2,1)}, u32[]{:S(2)}) copy-start(bf16[1024,256]{1,0:T(8,128)(2,1)} %param.16) | copy-start | bytes 1572868
  0.6 10.0 %copy-start.4 = (bf16[32,64,256]{2,1,0:T(8,128)(2,1)S(1)}, bf16[32,64,256]{2,1,0:T(8,128)(2,1)}, u32[]{:S(2)}) copy-start(bf16[32,64,256]{2,1,0:T(8,128)(2,1)} %param.12) | copy-start | bytes 3145732
  0.7 9.9 %copy-start.9 = (s32[32,64]{1,0:T(8,128)S(1)}, s32[32,64]{1,0:T(8,128)}, u32[]{:S(2)}) copy-start(s32[32,64]{1,0:T(8,128)} %param.18) | copy-start | bytes 24580
  1.8 8.8 %collective-permute-start = (bf16[32,3,256]{2,1,0:T(4,128)(2,1)S(1)}, bf16[32,3,256]{2,1,0:T(4,128)(2,1)S(1)}, u32[]{:S(2)}, u32[]{:S(2)}) collective-permute-start(bf16[32,3,256]{2,1,0:T(4,128)(2,1)S(1)} %get-tuple-element.8), channel_id=1, source_target_pairs={{0,8},{8,16},{16,24},{24,32},{32,40},{40,48},{48,56},{56,64},{64,7... | collective-permute-start | bytes 147464 | tf_op jit(solution)/shard_map/ppermute | solution.py:22
  3.7 6.9 %collective-permute-start.1 = (bf16[32,3,256]{2,1,0:T(4,128)(2,1)S(1)}, bf16[32,3,256]{2,1,0:T(4,128)(2,1)S(1)}, u32[]{:S(2)}, u32[]{:S(2)}) collective-permute-start(bf16[32,3,256]{2,1,0:T(4,128)(2,1)S(1)} %get-tuple-element.9), channel_id=1, source_target_pairs={{8,0},{16,8},{24,16},{32,24},{40,32},{48,40},{56,48},{64,56},{72,6... | collective-permute-start | bytes 147464 | tf_op jit(solution)/shard_map/ppermute | solution.py:23
  10.7 5.5 %collective-permute-start.2 = (bf16[3,70,256]{2,1,0:T(8,128)(2,1)S(1)}, bf16[3,70,256]{2,1,0:T(8,128)(2,1)S(1)}, u32[]{:S(2)}, u32[]{:S(2)}) collective-permute-start(bf16[3,70,256]{2,1,0:T(8,128)(2,1)S(1)} %get-tuple-element.6), channel_id=1, source_target_pairs={{0,1},{1,2},{2,3},{3,4},{4,5},{5,6},{6,7},{8,9},{9,10},{10,11},{11... | collective-permute-start | bytes 322568 | tf_op jit(solution)/shard_map/ppermute | solution.py:22
  12.0 5.7 %collective-permute-start.3 = (bf16[3,70,256]{2,1,0:T(8,128)(2,1)S(1)}, bf16[3,70,256]{2,1,0:T(8,128)(2,1)S(1)}, u32[]{:S(2)}, u32[]{:S(2)}) collective-permute-start(bf16[3,70,256]{2,1,0:T(8,128)(2,1)S(1)} %get-tuple-element.7), channel_id=1, source_target_pairs={{1,0},{2,1},{3,2},{4,3},{5,4},{6,5},{7,6},{9,8},{10,9},{11,10},{12... | collective-permute-start | bytes 322568 | tf_op jit(solution)/shard_map/ppermute | solution.py:23
  16.1 3.0 %copy-start.6 = (bf16[32,67,256]{2,1,0:T(8,128)(2,1)}, bf16[32,67,256]{2,1,0:T(8,128)(2,1)S(1)}, u32[]{:S(2)}) copy-start(bf16[32,67,256]{2,1,0:T(8,128)(2,1)S(1)} %constant_dynamic-update-slice_fusion) | copy-start | bytes 3293188
  16.1 3.0 %copy-start.5 = (bf16[32,64,256]{2,1,0:T(8,128)(2,1)S(1)}, bf16[32,64,256]{2,1,0:T(8,128)(2,1)}, u32[]{:S(2)}) copy-start(bf16[32,64,256]{2,1,0:T(8,128)(2,1)} %param.12) | copy-start | bytes 3145732
  36.4 0.8 copy-start.10
  38.9 5.9 %copy-start.8 = (bf16[256,256]{1,0:T(8,128)(2,1)S(1)}, bf16[256,256]{1,0:T(8,128)(2,1)}, u32[]{:S(2)}) copy-start(bf16[256,256]{1,0:T(8,128)(2,1)} %param.17) | copy-start | bytes 393220
  43.8 1.0 copy-start.7
  46.4 1.0 copy-start.1
  46.4 1.2 %copy-start.2 = (bf16[1024,256]{1,0:T(8,128)(2,1)S(1)}, bf16[1024,256]{1,0:T(8,128)(2,1)}, u32[]{:S(2)}) copy-start(bf16[1024,256]{1,0:T(8,128)(2,1)} %down_ref.1) | copy-start | bytes 1572868
  46.5 1.2 %copy-start.3 = (f32[256]{0:T(256)S(1)}, f32[256]{0:T(256)}, u32[]{:S(2)}) copy-start(f32[256]{0:T(256)} %param.21) | copy-start | bytes 3076

commit v5 on v4

--- a/solution.py
+++ b/solution.py
@@ -12,17 +12,83 @@
 AXES = ("lat", "lon")
 
 
-def padded_2(x, sides, width, wrap):
-    for axis, dim in sides:
-        devices, length = (lax.axis_size(axis), x.shape[dim])
-        up = [(i, (i + 1) % devices) for i in range(devices if wrap else devices - 1)]
-        down = [(j, i) for i, j in up]
-        last = lax.slice_in_dim(x, length - width, length, axis=dim)
-        leading = lax.slice_in_dim(x, 0, width, axis=dim)
-        before = lax.ppermute(last, axis, up)
-        after = lax.ppermute(leading, axis, down)
-        x = jnp.concatenate([before, x, after], axis=dim)
-    return x
+HALO_MOVES = ((1, 0), (-1, 0), (0, 1), (0, -1), (1, 1), (1, -1), (-1, 1), (-1, -1))
+
+
+def halo_body(n_lat, n_lon, *refs):
+    pieces, got, send_sems, recv_sems = refs[:8], refs[8:16], refs[16], refs[17]
+    lat, lon = lax.axis_index("lat"), lax.axis_index("lon")
+    has_up = lat > 0
+    has_down = lat < n_lat - 1
+
+    def exists(d_lat):
+        return has_down if d_lat > 0 else (has_up if d_lat < 0 else lat >= 0)
+
+    def exists_from(d_lat):
+        return has_up if d_lat > 0 else (has_down if d_lat < 0 else lat >= 0)
+
+    def target(d_lat, d_lon):
+        return (lax.rem(lon + d_lon + n_lon, n_lon), lat + d_lat)
+
+    barrier = pltpu.get_barrier_semaphore()
+    for d_lat, d_lon in HALO_MOVES:
+        @pl.when(exists(d_lat))
+        def _():
+            pl.semaphore_signal(barrier, inc=1, device_id=target(d_lat, d_lon), device_id_type=MESH)
+
+    pl.semaphore_wait(barrier, 2 + 3 * has_up.astype(jnp.int32) + 3 * has_down.astype(jnp.int32))
+
+    def copy(p):
+        d_lat, d_lon = HALO_MOVES[p]
+        return pltpu.make_async_remote_copy(
+            src_ref=pieces[p],
+            dst_ref=got[p],
+            send_sem=send_sems.at[p],
+            recv_sem=recv_sems.at[p],
+            device_id=target(d_lat, d_lon),
+            device_id_type=MESH,
+        )
+
+    for p, (d_lat, d_lon) in enumerate(HALO_MOVES):
+        @pl.when(exists(d_lat))
+        def _():
+            copy(p).start()
+
+    for p, (d_lat, d_lon) in enumerate(HALO_MOVES):
+        @pl.when(exists_from(d_lat))
+        def _():
+            copy(p).wait_recv()
+
+        @pl.when(jnp.logical_not(exists_from(d_lat)))
+        def _():
+            got[p][...] = jnp.zeros(got[p].shape, got[p].dtype)
+
+    for p, (d_lat, d_lon) in enumerate(HALO_MOVES):
+        @pl.when(exists(d_lat))
+        def _():
+            copy(p).wait_send()
+
+
+def halo_pad(x, w):
+    rows, cols = x.shape[0], x.shape[1]
+    pieces = (
+        x[rows - w:], x[:w], x[:, cols - w:], x[:, :w],
+        x[rows - w:, cols - w:], x[rows - w:, :w], x[:w, cols - w:], x[:w, :w],
+    )
+    vmem = pl.BlockSpec(memory_space=pltpu.VMEM)
+    got = pl.pallas_call(
+        functools.partial(halo_body, lax.axis_size("lat"), lax.axis_size("lon")),
+        out_shape=tuple(jax.ShapeDtypeStruct(p.shape, p.dtype) for p in pieces),
+        in_specs=[vmem] * 8,
+        out_specs=tuple([vmem] * 8),
+        scratch_shapes=[pltpu.SemaphoreType.DMA((8,)), pltpu.SemaphoreType.DMA((8,))],
+        compiler_params=pltpu.CompilerParams(collective_id=1, has_side_effects=True),
+    )(*pieces)
+    above, below, left, right, above_left, above_right, below_left, below_right = got
+    top = jnp.concatenate([above_left, above, above_right], axis=1)
+    mid = jnp.concatenate([left, x, right], axis=1)
+    bottom = jnp.concatenate([below_left, below, below_right], axis=1)
+    return jnp.concatenate([top, mid, bottom], axis=0)
 
 
 def exchange_body(n_lon, n, group, out_ref, state_ref, gain_ref, up_ref, down_ref,
@@ -181,8 +247,7 @@
     peer_count = ocean_state.shape[1]
     capacity = ocean_state.shape[2]
     tile_cells = ocean_state.shape[3]
-    lon_padded = padded_2(atmosphere, (("lon", 1),), margin, True)
-    padded = padded_2(lon_padded, (("lat", 0),), margin, False)
+    padded = halo_pad(atmosphere, margin)
     mixed = depthwise(padded, conv_weight, lat_rows, lon_cols).reshape(
         lat_rows * lon_cols, channels
     )

time: 106 us -> 101 us (0.953)
  the two profiles are of different devices: /device:TPU:99 before, /device:TPU:65 now
where the time goes in v5:
time: 101 us
  Pallas kernels  62.4 us (62%)
  other arithmetic  21.6 us (21%)
  local copies, waits for them, and re-layouts  10.1 us (10%)
  matrix products  5.87 us (6%)
    pallas_call x1, Pallas kernels, exchange_and_ocean(): pl.pallas_call(functools.partial(exchange_body, n_lon, n, group), out_sha...  50.9 us
    reduce_sum x1, other arithmetic, normalize(): average = jnp.mean(values, axis=-1, keepdims=True)  15.9 us
    pallas_call x1, Pallas kernels, halo_pad(): pl.pallas_call(functools.partial(halo_body, lax.axis_size('lat'), lax.axi...  11.5 us
    dot_general x1, matrix products, channel_mixer(): return jnp.dot(hidden, w_down, preferred_element_type=jnp.float32)  4.72 us
    unnamed x33, local copies, waits for them, and re-layouts  4.51 us
    concatenate x1, other arithmetic, halo_pad(): return jnp.concatenate([top, mid, bottom], axis=0)  2.79 us

profile of v5, /device:TPU:65, one launch (start us, length us, event | category | flops | bytes accessed | tf_op | source)
XLA Modules:
  0.0 100.8 jit_solution(3664383552592947393)
XLA Ops:
  0.6 1.4 %fusion.33 = (bf16[3,3,256]{2,1,0:T(4,128)(2,1)}, bf16[3,3,256]{2,1,0:T(4,128)(2,1)}, bf16[3,3,256]{2,1,0:T(4,128)(2,1)}, bf16[3,3,256]{2,1,0:T(4,128)(2,1)}) fusion(bf16[32,64,256]{2,1,0:T(8,128)(2,1)} %param.12), kind=kLoop, calls=%fused_computation.50 | loop fusion | bytes 36864 | tf_op jit(solution)/shard_map/slice | solution.py:76
  2.1 1.6 %fusion.35 = (bf16[3,64,256]{2,1,0:T(8,128)(2,1)}, bf16[3,64,256]{2,1,0:T(8,128)(2,1)}) fusion(bf16[32,64,256]{2,1,0:T(8,128)(2,1)} %param.12), kind=kLoop, calls=%fused_computation.52 | loop fusion | bytes 393216 | tf_op jit(solution)/shard_map/slice | solution.py:75
  3.7 1.7 %fusion.34 = (bf16[32,3,256]{2,1,0:T(4,128)(2,1)}, bf16[32,3,256]{2,1,0:T(4,128)(2,1)}) fusion(bf16[32,64,256]{2,1,0:T(8,128)(2,1)} %param.12), kind=kLoop, calls=%fused_computation.51 | loop fusion | bytes 196608 | tf_op jit(solution)/shard_map/slice | solution.py:75
  5.4 11.5 %shard_map.131 = (bf16[3,64,256]{2,1,0:T(8,128)(2,1)}, bf16[3,64,256]{2,1,0:T(8,128)(2,1)}, bf16[32,3,256]{2,1,0:T(4,128)(2,1)}, bf16[32,3,256]{2,1,0:T(4,128)(2...) custom-call(bf16[3,64,256]{2,1,0:T(8,128)(2,1)} %get-tuple-element.2, ...), custom_call_target="tpu_custom_call" | custom-call | tf_op jit(solution)/shard_map/pallas_call | solution.py:79
  16.9 2.8 %maximum_maximum_fusion = (bf16[35,70,256]{2,1,0:T(8,128)(2,1)S(1)}, bf16[35,70,256]{2,1,0:T(8,128)(2,1)S(1)}) fusion(bf16[32,3,256]{2,1,0:T(4,128)(2,1)} %get-tuple-element.14, bf16[32,64,256]{2,1,0:T(8,128)(2,1)} %param.12, bf16[32,3,256]{2,1,0:T(4,128)(2,1)} %get-tuple-element.13, bf16[3,3,256]{2,1,0:T(4,128)(2,1)} %get-tuple-element.12, ...), kind=kLoop, calls=%fused_computation.25 | loop fusion | flops 15052800 | bytes 3870720 | tf_op jit(solution)/shard_map/concatenate | solution.py:91
  19.9 0.6 copy-done.10
  20.6 0.4 copy-done.5
  20.9 15.9 %fusion.32 = (f32[32,64]{1,0:T(8,128)S(1)}, f32[32,64,256]{2,1,0:T(8,128)S(1)}) fusion(f32[256]{0:T(256)S(1)} %bitcast.127, bf16[35,70,256]{2,1,0:T(8,128)(2,1)S(1)} %get-tuple-element.21, f32[256]{0:T(256)S(1)} %bitcast.128, f32[256]{0:T(256)S(1)} %bitcast.81, f32[256]{0:T(256)S(1)} %bitcast.82, f32[256]{0:T(256)S(1)} %bitcast.83, f32[256]{0:T(256)S(1)} %bitcast.84, ...), kind=kLoop, calls=%fused_computation.49 | loop fusion | flops 81786880 | bytes 50439168 | tf_op jit(solution)/shard_map/reduce_sum | solution.py:215
  36.8 0.7 multiply_reduce_fusion
  37.7 1.6 %fusion.22 = bf16[2048,256]{1,0:T(8,128)(2,1)} fusion(f32[32,64,256]{2,1,0:T(8,128)S(1)} %get-tuple-element.19, f32[256]{0:T(256)S(1)} %copy-done.13, f32[2048]{0:T(1024)S(1)} %rsqrt.12, f32[2048]{0:T(1024)S(1)} %div.9), kind=kLoop, calls=%fused_computation.20 | loop fusion | flops 2097152 | bytes 3163136 | tf_op jit(solution)/shard_map/convert_element_type | solution.py:222
  39.3 4.7 %fusion.16 = bf16[2048,256]{1,0:T(8,128)(2,1)S(1)} fusion(bf16[1024,256]{1,0:T(8,128)(2,1)S(1)} %copy-done, bf16[2048,256]{1,0:T(8,128)(2,1)} %fusion.22, bf16[256,1024]{1,0:T(8,128)(2,1)S(1)} %copy-done.14, bf16[2048,256]{1,0:T(8,128)(2,1)} %bitcast.77), kind=kOutput, calls=%fused_computation.15 | convolution fusion | flops 2167930880 | bytes 4194304 | tf_op jit(solution)/shard_map/dot_general | solution.py:226
  44.2 0.9 copy-done.6
  45.0 0.4 fusion.19
  45.5 0.5 reshape.83
  46.0 0.1 fusion.27
  46.1 0.2 reduce_window_sum.11
  46.3 0.2 select_reduce_fusion
  46.5 0.1 convert_reduce_fusion
  46.6 0.7 fusion.8
  47.4 0.6 copy.14
  48.0 0.4 copy-done.1
  48.4 0.2 copy-done.2
  48.5 50.9 %shard_map.132 = bf16[128,2,16,256]{3,2,1,0:T(8,128)(2,1)S(1)} custom-call(bf16[128,2,16,256]{3,2,1,0:T(8,128)(2,1)S(1)} %bitcast.74, bf16[128,2,16,256]{3,2,1,0:T(8,128)(2,1)} %bitcast.131, f32[1,256]{1,0:T(1,128)S(1)} %bitcast.76, bf16[256,1024]{1,0:T(8,128)(2,1)S(1)} %copy-done.1, bf16[1024,256]{1,0:T(8,128)(2,1)S(1)} %copy-done.2), custom_call_target="tpu_custom_call" | custom-call | flops 4294967296 | bytes 8388608 | tf_op jit(solution)/shard_map/pallas_call | solution.py:183
  99.5 1.3 %copy.17 = bf16[1,128,2,16,256]{4,3,2,1,0:T(8,128)(2,1)} copy(bf16[1,128,2,16,256]{4,3,2,1,0:T(8,128)(2,1)S(1)} %bitcast.75) | data formatting | bytes 4194304
  (38 shorter events, 0.5 us)
Async XLA Ops:
  0.6 38.7 %copy-start = (bf16[1024,256]{1,0:T(8,128)(2,1)S(1)}, bf16[1024,256]{1,0:T(8,128)(2,1)}, u32[]{:S(2)}) copy-start(bf16[1024,256]{1,0:T(8,128)(2,1)} %param.16) | copy-start | bytes 1572868
  5.4 14.3 %copy-start.4 = (bf16[32,64,256]{2,1,0:T(8,128)(2,1)S(1)}, bf16[32,64,256]{2,1,0:T(8,128)(2,1)}, u32[]{:S(2)}) copy-start(bf16[32,64,256]{2,1,0:T(8,128)(2,1)} %param.12) | copy-start | bytes 3145732
  16.9 2.9 %copy-start.8 = (bf16[32,3,256]{2,1,0:T(4,128)(2,1)S(1)}, bf16[32,3,256]{2,1,0:T(4,128)(2,1)}, u32[]{:S(2)}) copy-start(bf16[32,3,256]{2,1,0:T(4,128)(2,1)} %get-tuple-element.14) | copy-start | bytes 147460
  19.7 0.8 copy-start.10
  19.7 1.2 %copy-start.5 = (bf16[32,64,256]{2,1,0:T(8,128)(2,1)S(1)}, bf16[32,64,256]{2,1,0:T(8,128)(2,1)}, u32[]{:S(2)}) copy-start(bf16[32,64,256]{2,1,0:T(8,128)(2,1)} %param.12) | copy-start | bytes 3145732
  19.7 1.2 %copy-start.7 = (bf16[32,3,256]{2,1,0:T(4,128)(2,1)S(1)}, bf16[32,3,256]{2,1,0:T(4,128)(2,1)}, u32[]{:S(2)}) copy-start(bf16[32,3,256]{2,1,0:T(4,128)(2,1)} %get-tuple-element.13) | copy-start | bytes 147460
  36.8 0.8 copy-start.13
  37.5 1.8 %copy-start.14 = (bf16[256,1024]{1,0:T(8,128)(2,1)S(1)}, bf16[256,1024]{1,0:T(8,128)(2,1)}, u32[]{:S(2)}) copy-start(bf16[256,1024]{1,0:T(8,128)(2,1)} %param.15) | copy-start | bytes 1572868
  39.3 4.7 %copy-start.11 = (s32[32,64]{1,0:T(8,128)S(1)}, s32[32,64]{1,0:T(8,128)}, u32[]{:S(2)}) copy-start(s32[32,64]{1,0:T(8,128)} %param.18) | copy-start | bytes 24580
  39.3 5.7 %copy-start.9 = (bf16[256,256]{1,0:T(8,128)(2,1)S(1)}, bf16[256,256]{1,0:T(8,128)(2,1)}, u32[]{:S(2)}) copy-start(bf16[256,256]{1,0:T(8,128)(2,1)} %param.17) | copy-start | bytes 393220
  44.1 1.0 copy-start.6
  45.0 1.0 copy-start.12
  47.3 1.0 %copy-start.1 = (bf16[256,1024]{1,0:T(8,128)(2,1)S(1)}, bf16[256,1024]{1,0:T(8,128)(2,1)}, u32[]{:S(2)}) copy-start(bf16[256,1024]{1,0:T(8,128)(2,1)} %up_ref.1) | copy-start | bytes 1572868
  47.3 1.2 %copy-start.2 = (bf16[1024,256]{1,0:T(8,128)(2,1)S(1)}, bf16[1024,256]{1,0:T(8,128)(2,1)}, u32[]{:S(2)}) copy-start(bf16[1024,256]{1,0:T(8,128)(2,1)} %down_ref.1) | copy-start | bytes 1572868
  47.4 1.2 %copy-start.3 = (f32[256]{0:T(256)S(1)}, f32[256]{0:T(256)}, u32[]{:S(2)}) copy-start(f32[256]{0:T(256)} %param.21) | copy-start | bytes 3076

commit v6 on v5

--- a/solution.py
+++ b/solution.py
@@ -200,15 +200,73 @@
     )(outgoing, state, gain.reshape(1, channels), w_up, w_down)
 
 
-def depthwise(padded, kernel, lat_rows, lon_cols):
-    summed = jnp.zeros((lat_rows, lon_cols, padded.shape[2]), jnp.float32)
-    for row_off in range(kernel.shape[0]):
-        for col_off in range(kernel.shape[1]):
-            window = padded[row_off : row_off + lat_rows, col_off : col_off + lon_cols, :].astype(
-                jnp.float32
-            )
-            summed = summed + window * kernel[row_off, col_off]
-    return summed
+def atmos_body(kw, band, pad_ref, w_ref, atm_ref, gain_ref, up_ref, down_ref, fw_ref, wet_ref,
+               out_ref, flux_ref, xf_ref, mixed_ref):
+    rows, cols, channels = atm_ref.shape
+    xf_ref[:, : pad_ref.shape[1], :] = pad_ref[...].astype(jnp.float32)
+
+    @pl.loop(0, rows // band)
+    def _(b):
+        r0 = b * band
+        for cb in range(channels // 128):
+            lanes = pl.ds(cb * 128, 128)
+            acc = [jnp.zeros((cols, 128), jnp.float32) for _ in range(band)]
+            for q in range(kw):
+                for i in range(band + kw - 1):
+                    line = xf_ref[r0 + i, pl.ds(q, cols), lanes]
+                    for p in range(kw):
+                        r = i - p
+                        if 0 <= r < band:
+                            acc[r] = acc[r] + line * w_ref[p, pl.ds(q, 1), lanes]
+            for r in range(band):
+                mixed_ref[r0 + r, :, lanes] = acc[r]
+
+    chunk = 8
+
+    @pl.loop(0, rows // chunk)
+    def _(k):
+        cells = chunk * cols
+        mixed = mixed_ref[pl.ds(k * chunk, chunk)].reshape(cells, channels)
+        average = jnp.mean(mixed, axis=-1, keepdims=True)
+        centred = mixed - average
+        spread = jnp.mean(centred * centred, axis=-1, keepdims=True)
+        normed = (centred * lax.rsqrt(spread + 1e-06) * gain_ref[...]).astype(jnp.bfloat16)
+        hidden = jax.nn.gelu(
+            jnp.dot(normed, up_ref[...], preferred_element_type=jnp.float32), approximate=True
+        ).astype(jnp.bfloat16)
+        branch = jnp.dot(hidden, down_ref[...], preferred_element_type=jnp.float32)
+        atmos = atm_ref[pl.ds(k * chunk, chunk)].reshape(cells, channels).astype(jnp.float32)
+        new = (atmos + branch).astype(jnp.bfloat16)
+        out_ref[pl.ds(k * chunk, chunk)] = new.reshape(chunk, cols, channels)
+        flux = jnp.dot(new, fw_ref[...], preferred_element_type=jnp.float32) * wet_ref[pl.ds(k * cells, cells)]
+        flux_ref[pl.ds(k * cells, cells)] = flux.astype(jnp.bfloat16)
+
+
+def atmosphere_block(padded, conv_weight, atmosphere, gain, w_up, w_down, flux_weight, wet):
+    rows, cols, channels = atmosphere.shape
+    kw = conv_weight.shape[0]
+    hid = w_up.shape[1]
+    vmem = pl.BlockSpec(memory_space=pltpu.VMEM)
+    cells = rows * cols
+    return pl.pallas_call(
+        functools.partial(atmos_body, kw, 4),
+        out_shape=(
+            jax.ShapeDtypeStruct(atmosphere.shape, atmosphere.dtype),
+            jax.ShapeDtypeStruct((cells, channels), jnp.bfloat16),
+        ),
+        in_specs=[vmem] * 8,
+        out_specs=(vmem, vmem),
+        scratch_shapes=[
+            pltpu.VMEM((padded.shape[0], -(-padded.shape[1] // 8) * 8, channels), jnp.float32),
+            pltpu.VMEM((rows, cols, channels), jnp.float32),
+        ],
+        compiler_params=pltpu.CompilerParams(vmem_limit_bytes=48 * 1024 * 1024),
+        cost_estimate=pl.CostEstimate(
+            flops=2 * cells * channels * (kw * kw + 2 * hid + channels),
+            transcendentals=cells * hid,
+            bytes_accessed=cells * channels * 8,
+        ),
+    )(padded, conv_weight, atmosphere, gain.reshape(1, channels), w_up, w_down, flux_weight, wet)
 
 
 def normalize(values, scales):
@@ -248,16 +306,10 @@
     capacity = ocean_state.shape[2]
     tile_cells = ocean_state.shape[3]
     padded = halo_pad(atmosphere, margin)
-    mixed = depthwise(padded, conv_weight, lat_rows, lon_cols).reshape(
-        lat_rows * lon_cols, channels
+    wet_cells = land_mask.reshape(lat_rows * lon_cols, 1).astype(jnp.float32)
+    atmos_new, fluxes = atmosphere_block(
+        padded, conv_weight, atmosphere, atm_gain, atm_up, atm_down, flux_weight, wet_cells
     )
-    branch = channel_mixer(mixed, atm_gain, atm_up, atm_down)
-    flat_atmos = atmosphere.reshape(lat_rows * lon_cols, channels)
-    atmos_new = (flat_atmos.astype(jnp.float32) + branch).astype(jnp.bfloat16)
-    wet_cells = land_mask.reshape(lat_rows * lon_cols, 1).astype(jnp.float32)
-    fluxes = (
-        jnp.dot(atmos_new, flux_weight, preferred_element_type=jnp.float32) * wet_cells
-    ).astype(jnp.bfloat16)
     flux_tiles = fluxes.reshape(tile_count, tile_cells * channels)
     member = (owners[:, None] == jnp.arange(peer_count, dtype=jnp.int32)[None, :]).astype(jnp.int32)
     tile_rank = jnp.sum(jnp.cumsum(member, axis=0) * member, axis=1) - 1
@@ -270,7 +322,7 @@
     outgoing = jnp.where(used[:, None], outgoing, jnp.nan).astype(jnp.bfloat16)
     outgoing = outgoing.reshape(peer_count, capacity, tile_cells, channels)
     ocean_out = exchange_and_ocean(outgoing, ocean_state[0], ocn_gain, ocn_up, ocn_down)[None]
-    return (atmos_new.reshape(lat_rows, lon_cols, channels), ocean_out)
+    return (atmos_new, ocean_out)
 
 
 def solution(mesh):

time: 101 us -> 103 us (1.020)
  Pallas kernels: 62.4 us -> 84.9 us
  other arithmetic: 21.6 us -> 5 us
  matrix products: 5.87 us -> 0.7 us
    pallas_call x0 -> x1, Pallas kernels: none -> 22.5 us  [atmosphere_block(): pl.pallas_call(functools.partial(atmos_body, kw, 4), out_shape=(jax.Shape...]
    reduce_sum x2 -> x0, other arithmetic: 16.5 us -> none  [the longest x1 15.9 us: normalize(): average = jnp.mean(values, axis=-1, keepdims=True)]
    dot_general x2 -> x0, matrix products: 5.17 us -> none  [the longest x1 4.72 us: channel_mixer(): return jnp.dot(hidden, w_down, preferred_element_type=jnp.float32)]
    convert_element_type x1 -> x0, other arithmetic: 1.65 us -> none  [channel_mixer(): normed = normalize(values, scales).astype(jnp.bfloat16)]
    concatenate x1, other arithmetic: 2.79 us -> 1.68 us  [halo_pad(): return jnp.concatenate([top, mid, bottom], axis=0)]
    unnamed x33 -> x20, local copies, waits for them, and re-layouts: 4.51 us -> 4.59 us
where the time goes in v6:
time: 103 us; the launch traced here: 102 us
  Pallas kernels  84.9 us (82%)
  local copies, waits for them, and re-layouts  10.8 us (10%)
  other arithmetic  5 us (5%)
    pallas_call x1, Pallas kernels, exchange_and_ocean(): pl.pallas_call(functools.partial(exchange_body, n_lon, n, group), out_sha...  51 us
    pallas_call x1, Pallas kernels, atmosphere_block(): pl.pallas_call(functools.partial(atmos_body, kw, 4), out_shape=(jax.Shape...  22.5 us
    pallas_call x1, Pallas kernels, halo_pad(): pl.pallas_call(functools.partial(halo_body, lax.axis_size('lat'), lax.axi...  11.5 us
    unnamed x20, local copies, waits for them, and re-layouts  4.59 us

profile of v6, /device:TPU:65, one launch (start us, length us, event | category | flops | bytes accessed | tf_op | source)
XLA Modules:
  0.0 102.2 jit_solution(3308174895713393470)
XLA Ops:
  0.6 0.8 convert_element_type.19
  1.4 1.4 %fusion.4 = (bf16[3,3,256]{2,1,0:T(4,128)(2,1)}, bf16[3,3,256]{2,1,0:T(4,128)(2,1)}, bf16[3,3,256]{2,1,0:T(4,128)(2,1)}, bf16[3,3,256]{2,1,0:T(4,128)(2,1)}) fusion(bf16[32,64,256]{2,1,0:T(8,128)(2,1)} %atm_ref.1), kind=kLoop, calls=%fused_computation.12 | loop fusion | bytes 36864 | tf_op jit(solution)/shard_map/slice | solution.py:76
  2.8 0.7 fusion.3
  3.6 0.2 reduce_window_sum.11
  3.7 0.8 select_reduce_fusion
  4.6 0.7 add_add_fusion
  5.2 0.1 convert_reduce_fusion
  5.4 1.7 %fusion.5 = (bf16[32,3,256]{2,1,0:T(4,128)(2,1)}, bf16[32,3,256]{2,1,0:T(4,128)(2,1)}) fusion(bf16[32,64,256]{2,1,0:T(8,128)(2,1)} %atm_ref.1), kind=kLoop, calls=%fused_computation.13 | loop fusion | bytes 196608 | tf_op jit(solution)/shard_map/slice | solution.py:75
  7.0 1.6 %fusion.6 = (bf16[3,64,256]{2,1,0:T(8,128)(2,1)}, bf16[3,64,256]{2,1,0:T(8,128)(2,1)}) fusion(bf16[32,64,256]{2,1,0:T(8,128)(2,1)} %atm_ref.1), kind=kLoop, calls=%fused_computation.14 | loop fusion | bytes 393216 | tf_op jit(solution)/shard_map/slice | solution.py:75
  8.7 11.5 %shard_map.131 = (bf16[3,64,256]{2,1,0:T(8,128)(2,1)}, bf16[3,64,256]{2,1,0:T(8,128)(2,1)}, bf16[32,3,256]{2,1,0:T(4,128)(2,1)}, bf16[32,3,256]{2,1,0:T(4,128)(2...) custom-call(bf16[3,64,256]{2,1,0:T(8,128)(2,1)} %get-tuple-element.2, ...), custom_call_target="tpu_custom_call" | custom-call | tf_op jit(solution)/shard_map/pallas_call | solution.py:79
  20.2 1.0 convert_element_type.25.wet_ref
  21.2 1.7 %maximum_maximum_fusion.pad_ref = bf16[38,70,256]{2,1,0:T(8,128)(2,1)S(1)} fusion(bf16[3,3,256]{2,1,0:T(4,128)(2,1)} %get-tuple-element.19, bf16[3,64,256]{2,1,0:T(8,128)(2,1)} %get-tuple-element.18, bf16[3,3,256]{2,1,0:T(4,128)(2,1)} %get-tuple-element.17, bf16[32,3,256]{2,1,0:T(4,128)(2,1)} %get-tuple-element.16, bf16[32,64,256]{2,1,0:T(8,128)(2,1)S(1)} %copy-done, ...), kind=kLoop, calls=%fused_computation.2 | loop fusion | flops 12257280 | bytes 2723840 | tf_op jit(solution)/shard_map/concatenate | solution.py:91
  22.9 0.0 copy-start.1
  22.9 1.0 %copy-done.1 = bf16[256,1024]{1,0:T(8,128)(2,1)S(1)} copy-done((bf16[256,1024]{1,0:T(8,128)(2,1)S(1)}, bf16[256,1024]{1,0:T(8,128)(2,1)}, u32[]{:S(2)}) %copy-start.1) | copy-done | bytes 524312
  24.0 1.0 %copy-done.2 = bf16[1024,256]{1,0:T(8,128)(2,1)S(1)} copy-done((bf16[1024,256]{1,0:T(8,128)(2,1)S(1)}, bf16[1024,256]{1,0:T(8,128)(2,1)}, u32[]{:S(2)}) %copy-start.2) | copy-done | bytes 524312
  25.0 22.5 %shard_map.132 = (bf16[32,64,256]{2,1,0:T(8,128)(2,1)}, bf16[2048,256]{1,0:T(8,128)(2,1)S(1)}) custom-call(bf16[38,70,256]{2,1,0:T(8,128)(2,1)S(1)} %maximum_maximum_fusion.pad_ref, f32[7,7,256]{2,1,0:T(8,128)S(1)} %copy-done.6, bf16[32,64,256]{2,1,0:T(8,128)(2,1)S(1)} %copy-done, f32[1,256]{1,0:T(1,128)S(1)} %bitcast.12, bf16[256,1024]{1,0:T(8,128)(2,1)S(1)} %copy-done.1, ...), custom_call_target="tpu_custom_call" | custom-call | flops 2467299328 | bytes 4194304 | tf_op jit(solution)/shard_map/pallas_call | solution.py:251
  47.5 0.5 reshape.48
  48.0 0.7 fusion
  48.7 0.0 copy-start.3
  48.7 0.6 copy.16
  49.4 0.4 copy-done.3
  49.7 0.2 copy-done.4
  49.9 51.0 %shard_map.133 = bf16[128,2,16,256]{3,2,1,0:T(8,128)(2,1)S(1)} custom-call(bf16[128,2,16,256]{3,2,1,0:T(8,128)(2,1)S(1)} %bitcast.10, bf16[128,2,16,256]{3,2,1,0:T(8,128)(2,1)} %bitcast.17, f32[1,256]{1,0:T(1,128)S(1)} %bitcast.13, bf16[256,1024]{1,0:T(8,128)(2,1)S(1)} %copy-done.3, bf16[1024,256]{1,0:T(8,128)(2,1)S(1)} %copy-done.4), custom_call_target="tpu_custom_call" | custom-call | flops 4294967296 | bytes 8388608 | tf_op jit(solution)/shard_map/pallas_call | solution.py:183
  100.9 1.3 %copy.18 = bf16[1,128,2,16,256]{4,3,2,1,0:T(8,128)(2,1)} copy(bf16[1,128,2,16,256]{4,3,2,1,0:T(8,128)(2,1)S(1)} %bitcast.11) | data formatting | bytes 4194304
  (13 shorter events, 0.0 us)
Async XLA Ops:
  0.6 20.6 %copy-start = (bf16[32,64,256]{2,1,0:T(8,128)(2,1)S(1)}, bf16[32,64,256]{2,1,0:T(8,128)(2,1)}, u32[]{:S(2)}) copy-start(bf16[32,64,256]{2,1,0:T(8,128)(2,1)} %atm_ref.1) | copy-start | bytes 3145732
  8.7 14.2 %copy-start.5 = (bf16[256,256]{1,0:T(8,128)(2,1)S(1)}, bf16[256,256]{1,0:T(8,128)(2,1)}, u32[]{:S(2)}) copy-start(bf16[256,256]{1,0:T(8,128)(2,1)} %fw_ref.1) | copy-start | bytes 393220
  8.7 14.2 %copy-start.6 = (f32[7,7,256]{2,1,0:T(8,128)S(1)}, f32[7,7,256]{2,1,0:T(8,128)}, u32[]{:S(2)}) copy-start(f32[7,7,256]{2,1,0:T(8,128)} %w_ref.1) | copy-start | bytes 150532
  8.7 14.2 %copy-start.7 = (f32[256]{0:T(256)S(1)}, f32[256]{0:T(256)}, u32[]{:S(2)}) copy-start(f32[256]{0:T(256)} %param.14) | copy-start | bytes 3076
  22.9 1.0 %copy-start.1 = (bf16[256,1024]{1,0:T(8,128)(2,1)S(1)}, bf16[256,1024]{1,0:T(8,128)(2,1)}, u32[]{:S(2)}) copy-start(bf16[256,1024]{1,0:T(8,128)(2,1)} %up_ref.2) | copy-start | bytes 1572868
  24.0 1.0 %copy-start.2 = (bf16[1024,256]{1,0:T(8,128)(2,1)S(1)}, bf16[1024,256]{1,0:T(8,128)(2,1)}, u32[]{:S(2)}) copy-start(bf16[1024,256]{1,0:T(8,128)(2,1)} %down_ref.2) | copy-start | bytes 1572868
  48.7 1.0 %copy-start.3 = (bf16[256,1024]{1,0:T(8,128)(2,1)S(1)}, bf16[256,1024]{1,0:T(8,128)(2,1)}, u32[]{:S(2)}) copy-start(bf16[256,1024]{1,0:T(8,128)(2,1)} %up_ref.3) | copy-start | bytes 1572868
  48.7 1.2 %copy-start.4 = (bf16[1024,256]{1,0:T(8,128)(2,1)S(1)}, bf16[1024,256]{1,0:T(8,128)(2,1)}, u32[]{:S(2)}) copy-start(bf16[1024,256]{1,0:T(8,128)(2,1)} %down_ref.3) | copy-start | bytes 1572868
  48.7 1.2 %copy-start.8 = (f32[256]{0:T(256)S(1)}, f32[256]{0:T(256)}, u32[]{:S(2)}) copy-start(f32[256]{0:T(256)} %param.21) | copy-start | bytes 3076

commit v7 on v6

--- a/solution.py
+++ b/solution.py
@@ -200,10 +200,22 @@
     )(outgoing, state, gain.reshape(1, channels), w_up, w_down)
 
 
-def atmos_body(kw, band, pad_ref, w_ref, atm_ref, gain_ref, up_ref, down_ref, fw_ref, wet_ref,
-               out_ref, flux_ref, xf_ref, mixed_ref):
+def atmos_body(kw, band, pad_ref, w_ref, atm_ref, gain_ref, up_hbm, down_hbm, fw_hbm, wet_ref,
+               out_ref, flux_ref, xf_ref, xs_ref, mixed_ref, up_ref, down_ref, fw_ref, sems):
     rows, cols, channels = atm_ref.shape
+    weights = [
+        pltpu.make_async_copy(up_hbm, up_ref, sems.at[0]),
+        pltpu.make_async_copy(down_hbm, down_ref, sems.at[1]),
+        pltpu.make_async_copy(fw_hbm, fw_ref, sems.at[2]),
+    ]
+    for copy in weights:
+        copy.start()
     xf_ref[:, : pad_ref.shape[1], :] = pad_ref[...].astype(jnp.float32)
+
+    @pl.loop(0, pad_ref.shape[0])
+    def _(i):
+        for q in range(kw):
+            xs_ref[q, i] = xf_ref[i, pl.ds(q, cols), :]
 
     @pl.loop(0, rows // band)
     def _(b):
@@ -213,13 +225,16 @@
             acc = [jnp.zeros((cols, 128), jnp.float32) for _ in range(band)]
             for q in range(kw):
                 for i in range(band + kw - 1):
-                    line = xf_ref[r0 + i, pl.ds(q, cols), lanes]
+                    line = xs_ref[q, r0 + i, :, lanes]
                     for p in range(kw):
                         r = i - p
                         if 0 <= r < band:
                             acc[r] = acc[r] + line * w_ref[p, pl.ds(q, 1), lanes]
             for r in range(band):
                 mixed_ref[r0 + r, :, lanes] = acc[r]
+
+    for copy in weights:
+        copy.wait()
 
     chunk = 8
 
@@ -247,6 +262,7 @@
     kw = conv_weight.shape[0]
     hid = w_up.shape[1]
     vmem = pl.BlockSpec(memory_space=pltpu.VMEM)
+    hbm = pl.BlockSpec(memory_space=pl.ANY)
     cells = rows * cols
     return pl.pallas_call(
         functools.partial(atmos_body, kw, 4),
@@ -254,13 +270,18 @@
             jax.ShapeDtypeStruct(atmosphere.shape, atmosphere.dtype),
             jax.ShapeDtypeStruct((cells, channels), jnp.bfloat16),
         ),
-        in_specs=[vmem] * 8,
+        in_specs=[vmem] * 4 + [hbm] * 3 + [vmem],
         out_specs=(vmem, vmem),
         scratch_shapes=[
             pltpu.VMEM((padded.shape[0], -(-padded.shape[1] // 8) * 8, channels), jnp.float32),
+            pltpu.VMEM((kw, padded.shape[0], cols, channels), jnp.float32),
             pltpu.VMEM((rows, cols, channels), jnp.float32),
+            pltpu.VMEM(w_up.shape, w_up.dtype),
+            pltpu.VMEM(w_down.shape, w_down.dtype),
+            pltpu.VMEM(flux_weight.shape, flux_weight.dtype),
+            pltpu.SemaphoreType.DMA((3,)),
         ],
-        compiler_params=pltpu.CompilerParams(vmem_limit_bytes=48 * 1024 * 1024),
+        compiler_params=pltpu.CompilerParams(vmem_limit_bytes=56 * 1024 * 1024),
         cost_estimate=pl.CostEstimate(
             flops=2 * cells * channels * (kw * kw + 2 * hid + channels),
             transcendentals=cells * hid,

time: 103 us -> 99.2 us (0.963)
  Pallas kernels: 84.9 us -> 80.8 us
    pallas_call x1, Pallas kernels: 22.5 us -> 18.5 us  [atmosphere_block(): pl.pallas_call(functools.partial(atmos_body, kw, 4), out_shape=(jax.Shape...]
    unnamed x20 -> x10, local copies, waits for them, and re-layouts: 4.59 us -> 2.5 us
    reshape x1, local copies, waits for them, and re-layouts: 0.51 us -> 1.55 us  [per_device(): flux_tiles = fluxes.reshape(tile_count, tile_cells * channels)]
where the time goes in v7:
time: 99.2 us; the launch traced here: 98.8 us
  Pallas kernels  80.8 us (81%)
  local copies, waits for them, and re-layouts  10.7 us (11%)
  other arithmetic  5.83 us (6%)
    pallas_call x1, Pallas kernels, exchange_and_ocean(): pl.pallas_call(functools.partial(exchange_body, n_lon, n, group), out_sha...  51 us
    pallas_call x1, Pallas kernels, atmosphere_block(): pl.pallas_call(functools.partial(atmos_body, kw, 4), out_shape=(jax.Shape...  18.5 us
    pallas_call x1, Pallas kernels, halo_pad(): pl.pallas_call(functools.partial(halo_body, lax.axis_size('lat'), lax.axi...  11.4 us
    concatenate x1, other arithmetic, halo_pad(): return jnp.concatenate([top, mid, bottom], axis=0)  2.51 us
    unnamed x10, local copies, waits for them, and re-layouts  2.5 us
    convert_element_type x1, local copies, waits for them, and re-layouts, per_device(): wet_cells = land_mask.reshape(lat_rows * lon_cols, 1).astype(jnp.float32)  2 us

profile of v7, /device:TPU:65, one launch (start us, length us, event | category | flops | bytes accessed | tf_op | source)
XLA Modules:
  0.0 98.8 jit_solution(15296317671658196501)
XLA Ops:
  0.6 0.0 copy-start.3
  0.6 0.8 convert_element_type.19
  1.4 1.4 %fusion.4 = (bf16[3,3,256]{2,1,0:T(4,128)(2,1)}, bf16[3,3,256]{2,1,0:T(4,128)(2,1)}, bf16[3,3,256]{2,1,0:T(4,128)(2,1)}, bf16[3,3,256]{2,1,0:T(4,128)(2,1)}) fusion(bf16[32,64,256]{2,1,0:T(8,128)(2,1)} %atm_ref.1), kind=kLoop, calls=%fused_computation.12 | loop fusion | bytes 36864 | tf_op jit(solution)/shard_map/slice | solution.py:76
  2.8 0.7 fusion.3
  3.6 0.2 reduce_window_sum.11
  3.7 0.8 select_reduce_fusion
  4.6 0.7 add_add_fusion
  5.2 0.1 convert_reduce_fusion
  5.4 1.7 %fusion.5 = (bf16[32,3,256]{2,1,0:T(4,128)(2,1)}, bf16[32,3,256]{2,1,0:T(4,128)(2,1)}) fusion(bf16[32,64,256]{2,1,0:T(8,128)(2,1)} %atm_ref.1), kind=kLoop, calls=%fused_computation.13 | loop fusion | bytes 196608 | tf_op jit(solution)/shard_map/slice | solution.py:75
  7.0 1.6 %fusion.6 = (bf16[3,64,256]{2,1,0:T(8,128)(2,1)}, bf16[3,64,256]{2,1,0:T(8,128)(2,1)}) fusion(bf16[32,64,256]{2,1,0:T(8,128)(2,1)} %atm_ref.1), kind=kLoop, calls=%fused_computation.14 | loop fusion | bytes 393216 | tf_op jit(solution)/shard_map/slice | solution.py:75
  8.7 11.4 %shard_map.131 = (bf16[3,64,256]{2,1,0:T(8,128)(2,1)}, bf16[3,64,256]{2,1,0:T(8,128)(2,1)}, bf16[32,3,256]{2,1,0:T(4,128)(2,1)}, bf16[32,3,256]{2,1,0:T(4,128)(2...) custom-call(bf16[3,64,256]{2,1,0:T(8,128)(2,1)} %get-tuple-element.2, ...), custom_call_target="tpu_custom_call" | custom-call | tf_op jit(solution)/shard_map/pallas_call | solution.py:79
  20.0 2.0 %convert_element_type.25.wet_ref = f32[2048,1]{1,0:T(8,128)} reshape(f32[32,64]{1,0:T(8,128)S(1)} %convert_element_type.19) | data formatting | bytes 16384 | tf_op jit(solution)/shard_map/convert_element_type | solution.py:330
  22.0 2.5 %maximum_maximum_fusion.pad_ref = bf16[38,70,256]{2,1,0:T(8,128)(2,1)} fusion(bf16[3,3,256]{2,1,0:T(4,128)(2,1)} %get-tuple-element.19, bf16[3,64,256]{2,1,0:T(8,128)(2,1)} %get-tuple-element.18, bf16[3,3,256]{2,1,0:T(4,128)(2,1)} %get-tuple-element.17, bf16[32,3,256]{2,1,0:T(4,128)(2,1)} %get-tuple-element.16, bf16[32,64,256]{2,1,0:T(8,128)(2,1)S(1)} %copy-done.3, ...), kind=kLoop, calls=%fused_computation.2 | loop fusion | flops 12257280 | bytes 2723840 | tf_op jit(solution)/shard_map/concatenate | solution.py:91
  24.6 18.5 %shard_map.132 = (bf16[32,64,256]{2,1,0:T(8,128)(2,1)}, bf16[2048,256]{1,0:T(8,128)(2,1)}) custom-call(bf16[38,70,256]{2,1,0:T(8,128)(2,1)} %maximum_maximum_fusion.pad_ref, f32[7,7,256]{2,1,0:T(8,128)} %w_ref.1, bf16[32,64,256]{2,1,0:T(8,128)(2,1)} %atm_ref.1, f32[1,256]{1,0:T(1,128)} %bitcast.17, bf16[256,1024]{1,0:T(8,128)(2,1)} %up_hbm.1, ...), custom_call_target="tpu_custom_call" | custom-call | flops 2467299328 | bytes 4194304 | tf_op jit(solution)/shard_map/pallas_call | solution.py:267
  43.0 1.6 %reshape.48 = bf16[128,4096]{1,0:T(8,128)(2,1)S(1)} reshape(bf16[2048,256]{1,0:T(8,128)(2,1)} %get-tuple-element.21) | data formatting | bytes 2097152 | tf_op jit(solution)/shard_map/reshape | solution.py:334
  44.6 0.7 fusion
  45.3 0.0 copy-start
  45.3 0.0 copy-start.1
  45.3 0.0 copy-start.2
  45.3 0.6 copy.16
  46.0 0.4 copy-done
  46.3 0.2 copy-done.1
  46.5 51.0 %shard_map.133 = bf16[128,2,16,256]{3,2,1,0:T(8,128)(2,1)S(1)} custom-call(bf16[128,2,16,256]{3,2,1,0:T(8,128)(2,1)S(1)} %bitcast.10, bf16[128,2,16,256]{3,2,1,0:T(8,128)(2,1)} %bitcast.16, f32[1,256]{1,0:T(1,128)S(1)} %bitcast.12, bf16[256,1024]{1,0:T(8,128)(2,1)S(1)} %copy-done, bf16[1024,256]{1,0:T(8,128)(2,1)S(1)} %copy-done.1), custom_call_target="tpu_custom_call" | custom-call | flops 4294967296 | bytes 8388608 | tf_op jit(solution)/shard_map/pallas_call | solution.py:183
  97.5 1.3 %copy.18 = bf16[1,128,2,16,256]{4,3,2,1,0:T(8,128)(2,1)} copy(bf16[1,128,2,16,256]{4,3,2,1,0:T(8,128)(2,1)S(1)} %bitcast.11) | data formatting | bytes 4194304
  (3 shorter events, 0.0 us)
Async XLA Ops:
  0.6 21.4 %copy-start.3 = (bf16[32,64,256]{2,1,0:T(8,128)(2,1)S(1)}, bf16[32,64,256]{2,1,0:T(8,128)(2,1)}, u32[]{:S(2)}) copy-start(bf16[32,64,256]{2,1,0:T(8,128)(2,1)} %atm_ref.1) | copy-start | bytes 3145732
  45.3 1.0 %copy-start = (bf16[256,1024]{1,0:T(8,128)(2,1)S(1)}, bf16[256,1024]{1,0:T(8,128)(2,1)}, u32[]{:S(2)}) copy-start(bf16[256,1024]{1,0:T(8,128)(2,1)} %up_ref.1) | copy-start | bytes 1572868
  45.3 1.2 %copy-start.1 = (bf16[1024,256]{1,0:T(8,128)(2,1)S(1)}, bf16[1024,256]{1,0:T(8,128)(2,1)}, u32[]{:S(2)}) copy-start(bf16[1024,256]{1,0:T(8,128)(2,1)} %down_ref.1) | copy-start | bytes 1572868
  45.3 1.2 %copy-start.2 = (f32[256]{0:T(256)S(1)}, f32[256]{0:T(256)}, u32[]{:S(2)}) copy-start(f32[256]{0:T(256)} %param.21) | copy-start | bytes 3076

commit v8 on v7

--- a/solution.py
+++ b/solution.py
@@ -200,8 +200,8 @@
     )(outgoing, state, gain.reshape(1, channels), w_up, w_down)
 
 
-def atmos_body(kw, band, pad_ref, w_ref, atm_ref, gain_ref, up_hbm, down_hbm, fw_hbm, wet_ref,
-               out_ref, flux_ref, xf_ref, xs_ref, mixed_ref, up_ref, down_ref, fw_ref, sems):
+def atmos_body(kw, band, pad_ref, w_ref, atm_ref, gain_ref, up_hbm, down_hbm, fw_hbm, wet_ref, tile_ref, used_ref,
+               out_ref, slots_ref, flux_ref, xf_ref, xs_ref, mixed_ref, up_ref, down_ref, fw_ref, sems):
     rows, cols, channels = atm_ref.shape
     weights = [
         pltpu.make_async_copy(up_hbm, up_ref, sems.at[0]),
@@ -256,8 +256,18 @@
         flux = jnp.dot(new, fw_ref[...], preferred_element_type=jnp.float32) * wet_ref[pl.ds(k * cells, cells)]
         flux_ref[pl.ds(k * cells, cells)] = flux.astype(jnp.bfloat16)
 
-
-def atmosphere_block(padded, conv_weight, atmosphere, gain, w_up, w_down, flux_weight, wet):
+    capacity, tile_cells = slots_ref.shape[1], slots_ref.shape[2]
+
+    @pl.loop(0, slots_ref.shape[0] * capacity)
+    def _(t):
+        start = pl.multiple_of(tile_ref[t] * tile_cells, tile_cells)
+        cells_of_tile = flux_ref[pl.ds(start, tile_cells)]
+        keep = jnp.full(cells_of_tile.shape, used_ref[t], jnp.int32) > 0
+        slots_ref[t // capacity, t % capacity] = jnp.where(keep, cells_of_tile, jnp.nan).astype(jnp.bfloat16)
+
+
+def atmosphere_block(padded, conv_weight, atmosphere, gain, w_up, w_down, flux_weight, wet, tile_of_slot, used,
+                     slot_shape):
     rows, cols, channels = atmosphere.shape
     kw = conv_weight.shape[0]
     hid = w_up.shape[1]
@@ -268,11 +278,12 @@
         functools.partial(atmos_body, kw, 4),
         out_shape=(
             jax.ShapeDtypeStruct(atmosphere.shape, atmosphere.dtype),
-            jax.ShapeDtypeStruct((cells, channels), jnp.bfloat16),
+            jax.ShapeDtypeStruct(slot_shape, jnp.bfloat16),
         ),
-        in_specs=[vmem] * 4 + [hbm] * 3 + [vmem],
+        in_specs=[vmem] * 4 + [hbm] * 3 + [vmem] + [pl.BlockSpec(memory_space=pltpu.SMEM)] * 2,
         out_specs=(vmem, vmem),
         scratch_shapes=[
+            pltpu.VMEM((cells, channels), jnp.bfloat16),
             pltpu.VMEM((padded.shape[0], -(-padded.shape[1] // 8) * 8, channels), jnp.float32),
             pltpu.VMEM((kw, padded.shape[0], cols, channels), jnp.float32),
             pltpu.VMEM((rows, cols, channels), jnp.float32),
@@ -287,7 +298,7 @@
             transcendentals=cells * hid,
             bytes_accessed=cells * channels * 8,
         ),
-    )(padded, conv_weight, atmosphere, gain.reshape(1, channels), w_up, w_down, flux_weight, wet)
+    )(padded, conv_weight, atmosphere, gain.reshape(1, channels), w_up, w_down, flux_weight, wet, tile_of_slot, used)
 
 
 def normalize(values, scales):
@@ -321,27 +332,22 @@
 ):
     lat_rows, lon_cols, channels = atmosphere.shape
     margin = conv_weight.shape[0] // 2
+    padded = halo_pad(atmosphere, margin)
     owners = tile_owner.reshape(-1)
     tile_count = owners.shape[0]
-    peer_count = ocean_state.shape[1]
-    capacity = ocean_state.shape[2]
-    tile_cells = ocean_state.shape[3]
-    padded = halo_pad(atmosphere, margin)
+    peer_count, capacity, tile_cells = ocean_state.shape[1], ocean_state.shape[2], ocean_state.shape[3]
+    order = jnp.arange(tile_count, dtype=jnp.int32)
+    earlier_same = (owners[:, None] == owners[None, :]) & (order[None, :] < order[:, None])
+    tile_rank = jnp.sum(earlier_same.astype(jnp.int32), axis=1)
+    slot_index = owners * capacity + tile_rank
+    hits = jnp.arange(peer_count * capacity, dtype=jnp.int32)[:, None] == slot_index[None, :]
+    used = jnp.sum(hits.astype(jnp.int32), axis=1)
+    tile_of_slot = jnp.sum(jnp.where(hits, order[None, :], 0), axis=1)
     wet_cells = land_mask.reshape(lat_rows * lon_cols, 1).astype(jnp.float32)
-    atmos_new, fluxes = atmosphere_block(
-        padded, conv_weight, atmosphere, atm_gain, atm_up, atm_down, flux_weight, wet_cells
+    atmos_new, outgoing = atmosphere_block(
+        padded, conv_weight, atmosphere, atm_gain, atm_up, atm_down, flux_weight, wet_cells,
+        tile_of_slot, used, (peer_count, capacity, tile_cells, channels),
     )
-    flux_tiles = fluxes.reshape(tile_count, tile_cells * channels)
-    member = (owners[:, None] == jnp.arange(peer_count, dtype=jnp.int32)[None, :]).astype(jnp.int32)
-    tile_rank = jnp.sum(jnp.cumsum(member, axis=0) * member, axis=1) - 1
-    slot_index = owners * capacity + tile_rank
-    onehot = (
-        jnp.arange(peer_count * capacity, dtype=jnp.int32)[:, None] == slot_index[None, :]
-    ).astype(jnp.bfloat16)
-    outgoing = jnp.dot(onehot, flux_tiles, preferred_element_type=jnp.float32).astype(jnp.bfloat16)
-    used = jnp.sum(onehot.astype(jnp.float32), axis=1) > 0
-    outgoing = jnp.where(used[:, None], outgoing, jnp.nan).astype(jnp.bfloat16)
-    outgoing = outgoing.reshape(peer_count, capacity, tile_cells, channels)
     ocean_out = exchange_and_ocean(outgoing, ocean_state[0], ocn_gain, ocn_up, ocn_down)[None]
     return (atmos_new, ocean_out)
 

time: 99.2 us -> 101 us (1.018)
  Pallas kernels: 80.8 us -> 84.2 us
  local copies, waits for them, and re-layouts: 10.7 us -> 9.58 us
    pallas_call x1, Pallas kernels: 18.5 us -> 21.9 us  [atmosphere_block(): pl.pallas_call(functools.partial(atmos_body, kw, 4), out_shape=(jax.Shape...]
    reshape x1 -> x0, local copies, waits for them, and re-layouts: 1.55 us -> none  [per_device(): flux_tiles = fluxes.reshape(tile_count, tile_cells * channels)]
    unnamed x10 -> x11, local copies, waits for them, and re-layouts: 2.5 us -> 2.93 us
where the time goes in v8:
time: 101 us; the launch traced here: 100 us
  Pallas kernels  84.2 us (83%)
  local copies, waits for them, and re-layouts  9.58 us (9%)
  other arithmetic  5.59 us (6%)
    pallas_call x1, Pallas kernels, exchange_and_ocean(): pl.pallas_call(functools.partial(exchange_body, n_lon, n, group), out_sha...  50.9 us
    pallas_call x1, Pallas kernels, atmosphere_block(): pl.pallas_call(functools.partial(atmos_body, kw, 4), out_shape=(jax.Shape...  21.9 us
    pallas_call x1, Pallas kernels, halo_pad(): pl.pallas_call(functools.partial(halo_body, lax.axis_size('lat'), lax.axi...  11.4 us
    unnamed x11, local copies, waits for them, and re-layouts  2.93 us
    concatenate x1, other arithmetic, halo_pad(): return jnp.concatenate([top, mid, bottom], axis=0)  2.55 us

profile of v8, /device:TPU:65, one launch (start us, length us, event | category | flops | bytes accessed | tf_op | source)
XLA Modules:
  0.0 100.1 jit_solution(5811311911908442407)
XLA Ops:
  0.6 0.0 copy-start.4
  0.6 0.9 convert_reduce_fusion.1
  1.6 0.7 multiply_add_fusion
  2.2 0.7 convert_reduce_fusion
  3.0 0.7 convert_element_type.11
  3.7 1.4 %fusion.1 = (bf16[3,3,256]{2,1,0:T(4,128)(2,1)}, bf16[3,3,256]{2,1,0:T(4,128)(2,1)}, bf16[3,3,256]{2,1,0:T(4,128)(2,1)}, bf16[3,3,256]{2,1,0:T(4,128)(2,1)}) fusion(bf16[32,64,256]{2,1,0:T(8,128)(2,1)} %atm_ref.1), kind=kLoop, calls=%fused_computation.8 | loop fusion | bytes 36864 | tf_op jit(solution)/shard_map/slice | solution.py:76
  5.1 1.7 %fusion.2 = (bf16[32,3,256]{2,1,0:T(4,128)(2,1)}, bf16[32,3,256]{2,1,0:T(4,128)(2,1)}) fusion(bf16[32,64,256]{2,1,0:T(8,128)(2,1)} %atm_ref.1), kind=kLoop, calls=%fused_computation.9 | loop fusion | bytes 196608 | tf_op jit(solution)/shard_map/slice | solution.py:75
  6.7 1.6 %fusion.3 = (bf16[3,64,256]{2,1,0:T(8,128)(2,1)}, bf16[3,64,256]{2,1,0:T(8,128)(2,1)}) fusion(bf16[32,64,256]{2,1,0:T(8,128)(2,1)} %atm_ref.1), kind=kLoop, calls=%fused_computation.10 | loop fusion | bytes 393216 | tf_op jit(solution)/shard_map/slice | solution.py:75
  8.4 11.4 %shard_map.131 = (bf16[3,64,256]{2,1,0:T(8,128)(2,1)}, bf16[3,64,256]{2,1,0:T(8,128)(2,1)}, bf16[32,3,256]{2,1,0:T(4,128)(2,1)}, bf16[32,3,256]{2,1,0:T(4,128)(2...) custom-call(bf16[3,64,256]{2,1,0:T(8,128)(2,1)} %get-tuple-element.3, ...), custom_call_target="tpu_custom_call" | custom-call | tf_op jit(solution)/shard_map/pallas_call | solution.py:79
  19.8 2.0 %convert_element_type.15.wet_ref = f32[2048,1]{1,0:T(8,128)} reshape(f32[32,64]{1,0:T(8,128)S(1)} %convert_element_type.11) | data formatting | bytes 16384 | tf_op jit(solution)/shard_map/convert_element_type | solution.py:346
  21.7 0.0 copy-done.4
  21.7 2.6 %maximum_maximum_fusion.pad_ref = bf16[38,70,256]{2,1,0:T(8,128)(2,1)} fusion(bf16[3,3,256]{2,1,0:T(4,128)(2,1)} %get-tuple-element.19, bf16[3,64,256]{2,1,0:T(8,128)(2,1)} %get-tuple-element.18, bf16[3,3,256]{2,1,0:T(4,128)(2,1)} %get-tuple-element.17, bf16[32,3,256]{2,1,0:T(4,128)(2,1)} %get-tuple-element.16, bf16[32,64,256]{2,1,0:T(8,128)(2,1)S(1)} %copy-done.4, ...), kind=kLoop, calls=%fused_computation | loop fusion | flops 12257280 | bytes 2723840 | tf_op jit(solution)/shard_map/concatenate | solution.py:91
  24.3 0.0 copy-start
  24.3 0.0 copy-start.1
  24.3 0.0 copy-start.2
  24.3 21.9 %shard_map.132 = (bf16[32,64,256]{2,1,0:T(8,128)(2,1)}, bf16[128,2,16,256]{3,2,1,0:T(8,128)(2,1)}) custom-call(bf16[38,70,256]{2,1,0:T(8,128)(2,1)} %maximum_maximum_fusion.pad_ref, f32[7,7,256]{2,1,0:T(8,128)} %w_ref.1, bf16[32,64,256]{2,1,0:T(8,128)(2,1)} %atm_ref.1, f32[1,256]{1,0:T(1,128)} %bitcast.9, bf16[256,1024]{1,0:T(8,128)(2,1)} %up_hbm.1, ...), custom_call_target="tpu_custom_call" | custom-call | flops 2467299328 | bytes 4194304 | tf_op jit(solution)/shard_map/pallas_call | solution.py:277
  46.2 0.0 copy-done
  46.3 0.0 copy-done.1
  46.3 0.0 copy-done.2
  46.3 0.0 copy-start.3
  46.3 1.6 %copy-done.3 = bf16[128,2,16,256]{3,2,1,0:T(8,128)(2,1)S(1)} copy-done((bf16[128,2,16,256]{3,2,1,0:T(8,128)(2,1)S(1)}, bf16[128,2,16,256]{3,2,1,0:T(8,128)(2,1)}, u32[]{:S(2)}) %copy-start.3) | copy-done | bytes 2097176
  47.9 50.9 %shard_map.133 = bf16[128,2,16,256]{3,2,1,0:T(8,128)(2,1)S(1)} custom-call(bf16[128,2,16,256]{3,2,1,0:T(8,128)(2,1)S(1)} %copy-done.3, bf16[128,2,16,256]{3,2,1,0:T(8,128)(2,1)} %bitcast.8, f32[1,256]{1,0:T(1,128)S(1)} %bitcast.7, bf16[256,1024]{1,0:T(8,128)(2,1)S(1)} %copy-done, bf16[1024,256]{1,0:T(8,128)(2,1)S(1)} %copy-done.1), custom_call_target="tpu_custom_call" | custom-call | flops 4294967296 | bytes 8388608 | tf_op jit(solution)/shard_map/pallas_call | solution.py:183
  98.8 1.3 %copy.17 = bf16[1,128,2,16,256]{4,3,2,1,0:T(8,128)(2,1)} copy(bf16[1,128,2,16,256]{4,3,2,1,0:T(8,128)(2,1)S(1)} %bitcast.6) | data formatting | bytes 4194304
Async XLA Ops:
  0.6 21.1 %copy-start.4 = (bf16[32,64,256]{2,1,0:T(8,128)(2,1)S(1)}, bf16[32,64,256]{2,1,0:T(8,128)(2,1)}, u32[]{:S(2)}) copy-start(bf16[32,64,256]{2,1,0:T(8,128)(2,1)} %atm_ref.1) | copy-start | bytes 3145732
  24.3 22.0 %copy-start = (bf16[256,1024]{1,0:T(8,128)(2,1)S(1)}, bf16[256,1024]{1,0:T(8,128)(2,1)}, u32[]{:S(2)}) copy-start(bf16[256,1024]{1,0:T(8,128)(2,1)} %up_ref.1) | copy-start | bytes 1572868
  24.3 22.0 %copy-start.1 = (bf16[1024,256]{1,0:T(8,128)(2,1)S(1)}, bf16[1024,256]{1,0:T(8,128)(2,1)}, u32[]{:S(2)}) copy-start(bf16[1024,256]{1,0:T(8,128)(2,1)} %down_ref.1) | copy-start | bytes 1572868
  24.3 22.0 %copy-start.2 = (f32[256]{0:T(256)S(1)}, f32[256]{0:T(256)}, u32[]{:S(2)}) copy-start(f32[256]{0:T(256)} %param.21) | copy-start | bytes 3076
  46.3 1.6 %copy-start.3 = (bf16[128,2,16,256]{3,2,1,0:T(8,128)(2,1)S(1)}, bf16[128,2,16,256]{3,2,1,0:T(8,128)(2,1)}, u32[]{:S(2)}) copy-start(bf16[128,2,16,256]{3,2,1,0:T(8,128)(2,1)} %get-tuple-element.21.out_ref) | copy-start | bytes 6291460

commit v9 on v7

--- a/solution.py
+++ b/solution.py
@@ -15,11 +15,14 @@
 HALO_MOVES = ((1, 0), (-1, 0), (0, 1), (0, -1), (1, 1), (1, -1), (-1, 1), (-1, -1))
 
 
-def halo_body(n_lat, n_lon, *refs):
-    pieces, got, send_sems, recv_sems = refs[:8], refs[8:16], refs[16], refs[17]
+def halo_body(n_lat, n_lon, w, side, x_ref, *refs):
+    got, send_sems, recv_sems = refs[:8], refs[8], refs[9]
+    rows, cols = x_ref.shape[0], x_ref.shape[1]
     lat, lon = lax.axis_index("lat"), lax.axis_index("lon")
     has_up = lat > 0
     has_down = lat < n_lat - 1
+    row_part = {1: pl.ds(rows - w, w), -1: pl.ds(0, w), 0: pl.ds(0, rows)}
+    col_part = {1: pl.ds(cols - side, side), -1: pl.ds(0, side), 0: pl.ds(0, cols)}
 
     def exists(d_lat):
         return has_down if d_lat > 0 else (has_up if d_lat < 0 else lat >= 0)
@@ -41,7 +44,7 @@
     def copy(p):
         d_lat, d_lon = HALO_MOVES[p]
         return pltpu.make_async_remote_copy(
-            src_ref=pieces[p],
+            src_ref=x_ref.at[row_part[d_lat], col_part[d_lon]],
             dst_ref=got[p],
             send_sem=send_sems.at[p],
             recv_sem=recv_sems.at[p],
@@ -70,21 +73,23 @@
 
 
 def halo_pad(x, w):
-    rows, cols = x.shape[0], x.shape[1]
-    pieces = (
-        x[rows - w:], x[:w], x[:, cols - w:], x[:, :w],
-        x[rows - w:, cols - w:], x[rows - w:, :w], x[:w, cols - w:], x[:w, :w],
-    )
+    rows, cols, channels = x.shape
+    side = 8
+    shapes = []
+    for d_lat, d_lon in HALO_MOVES:
+        shapes.append((w if d_lat else rows, side if d_lon else cols, channels))
     vmem = pl.BlockSpec(memory_space=pltpu.VMEM)
     got = pl.pallas_call(
-        functools.partial(halo_body, lax.axis_size("lat"), lax.axis_size("lon")),
-        out_shape=tuple(jax.ShapeDtypeStruct(p.shape, p.dtype) for p in pieces),
-        in_specs=[vmem] * 8,
+        functools.partial(halo_body, lax.axis_size("lat"), lax.axis_size("lon"), w, side),
+        out_shape=tuple(jax.ShapeDtypeStruct(sh, x.dtype) for sh in shapes),
+        in_specs=[pl.BlockSpec(memory_space=pl.ANY)],
         out_specs=tuple([vmem] * 8),
         scratch_shapes=[pltpu.SemaphoreType.DMA((8,)), pltpu.SemaphoreType.DMA((8,))],
         compiler_params=pltpu.CompilerParams(collective_id=1, has_side_effects=True),
-    )(*pieces)
+    )(x)
     above, below, left, right, above_left, above_right, below_left, below_right = got
+    left, above_left, below_left = (a[:, side - w:] for a in (left, above_left, below_left))
+    right, above_right, below_right = (a[:, :w] for a in (right, above_right, below_right))
     top = jnp.concatenate([above_left, above, above_right], axis=1)
     mid = jnp.concatenate([left, x, right], axis=1)
     bottom = jnp.concatenate([below_left, below, below_right], axis=1)
@@ -200,7 +205,7 @@
     )(outgoing, state, gain.reshape(1, channels), w_up, w_down)
 
 
-def atmos_body(kw, band, pad_ref, w_ref, atm_ref, gain_ref, up_hbm, down_hbm, fw_hbm, wet_ref,
+def atmos_body(kw, band, pad_ref, w_ref, atm_ref, gain_ref, up_hbm, down_hbm, fw_hbm,
                out_ref, flux_ref, xf_ref, xs_ref, mixed_ref, up_ref, down_ref, fw_ref, sems):
     rows, cols, channels = atm_ref.shape
     weights = [
@@ -253,11 +258,11 @@
         atmos = atm_ref[pl.ds(k * chunk, chunk)].reshape(cells, channels).astype(jnp.float32)
         new = (atmos + branch).astype(jnp.bfloat16)
         out_ref[pl.ds(k * chunk, chunk)] = new.reshape(chunk, cols, channels)
-        flux = jnp.dot(new, fw_ref[...], preferred_element_type=jnp.float32) * wet_ref[pl.ds(k * cells, cells)]
+        flux = jnp.dot(new, fw_ref[...], preferred_element_type=jnp.float32)
         flux_ref[pl.ds(k * cells, cells)] = flux.astype(jnp.bfloat16)
 
 
-def atmosphere_block(padded, conv_weight, atmosphere, gain, w_up, w_down, flux_weight, wet):
+def atmosphere_block(padded, conv_weight, atmosphere, gain, w_up, w_down, flux_weight):
     rows, cols, channels = atmosphere.shape
     kw = conv_weight.shape[0]
     hid = w_up.shape[1]
@@ -270,7 +275,7 @@
             jax.ShapeDtypeStruct(atmosphere.shape, atmosphere.dtype),
             jax.ShapeDtypeStruct((cells, channels), jnp.bfloat16),
         ),
-        in_specs=[vmem] * 4 + [hbm] * 3 + [vmem],
+        in_specs=[vmem] * 4 + [hbm] * 3,
         out_specs=(vmem, vmem),
         scratch_shapes=[
             pltpu.VMEM((padded.shape[0], -(-padded.shape[1] // 8) * 8, channels), jnp.float32),
@@ -287,7 +292,7 @@
             transcendentals=cells * hid,
             bytes_accessed=cells * channels * 8,
         ),
-    )(padded, conv_weight, atmosphere, gain.reshape(1, channels), w_up, w_down, flux_weight, wet)
+    )(padded, conv_weight, atmosphere, gain.reshape(1, channels), w_up, w_down, flux_weight)
 
 
 def normalize(values, scales):
@@ -327,11 +332,9 @@
     capacity = ocean_state.shape[2]
     tile_cells = ocean_state.shape[3]
     padded = halo_pad(atmosphere, margin)
-    wet_cells = land_mask.reshape(lat_rows * lon_cols, 1).astype(jnp.float32)
-    atmos_new, fluxes = atmosphere_block(
-        padded, conv_weight, atmosphere, atm_gain, atm_up, atm_down, flux_weight, wet_cells
-    )
-    flux_tiles = fluxes.reshape(tile_count, tile_cells * channels)
+    atmos_new, fluxes = atmosphere_block(padded, conv_weight, atmosphere, atm_gain, atm_up, atm_down, flux_weight)
+    wet = land_mask.reshape(tile_count, tile_cells, 1).astype(jnp.bfloat16)
+    flux_tiles = (fluxes.reshape(tile_count, tile_cells, channels) * wet).reshape(tile_count, tile_cells * channels)
     member = (owners[:, None] == jnp.arange(peer_count, dtype=jnp.int32)[None, :]).astype(jnp.int32)
     tile_rank = jnp.sum(jnp.cumsum(member, axis=0) * member, axis=1) - 1
     slot_index = owners * capacity + tile_rank

time: 99.2 us -> 97.3 us (0.981)
  the two profiles are of different devices: /device:TPU:65 before, /device:TPU:99 now
where the time goes in v9:
time: 97.3 us; the launch traced here: 96.2 us
  Pallas kernels  80.2 us (82%)
  local copies, waits for them, and re-layouts  9.66 us (10%)
  other arithmetic  4.83 us (5%)
    pallas_call x1, Pallas kernels, exchange_and_ocean(): pl.pallas_call(functools.partial(exchange_body, n_lon, n, group), out_sha...  52.4 us
    pallas_call x1, Pallas kernels, atmosphere_block(): pl.pallas_call(functools.partial(atmos_body, kw, 4), out_shape=(jax.Shape...  18.1 us
    pallas_call x1, Pallas kernels, halo_pad(): pl.pallas_call(functools.partial(halo_body, lax.axis_size('lat'), lax.axi...  9.76 us
    unnamed x15, local copies, waits for them, and re-layouts  2.93 us
    slice x3, local copies, waits for them, and re-layouts, halo_pad(): a[:, side - w:]  2.4 us
    slice x3, local copies, waits for them, and re-layouts, halo_pad(): a[:, :w]  2.35 us

profile of v9, /device:TPU:99, one launch (start us, length us, event | category | flops | bytes accessed | tf_op | source)
XLA Modules:
  0.0 96.2 jit_solution(5176547082031909008)
XLA Ops:
  0.6 0.7 convert_element_type.28
  1.4 0.7 fusion.4
  2.2 0.2 reduce_window_sum.11
  2.4 0.8 select_reduce_fusion
  3.2 0.7 add_add_fusion
  3.9 0.1 convert_reduce_fusion
  4.0 9.8 %shard_map.131 = (bf16[3,64,256]{2,1,0:T(8,128)(2,1)}, bf16[3,64,256]{2,1,0:T(8,128)(2,1)}, bf16[32,8,256]{2,1,0:T(8,128)(2,1)}, bf16[32,8,256]{2,1,0:T(8,128)(2...) custom-call(bf16[32,64,256]{2,1,0:T(8,128)(2,1)} %atm_ref.1), custom_call_target="tpu_custom_call" | custom-call | tf_op jit(solution)/shard_map/pallas_call | solution.py:82
  13.8 0.8 slice.18
  14.5 0.7 slice.19
  15.2 0.7 slice.22
  15.9 0.7 slice.23
  16.7 0.9 slice.20
  17.6 0.9 slice.21
  18.5 0.3 mul.27
  18.9 0.4 copy.14
  19.3 1.6 %maximum_maximum_fusion.pad_ref = bf16[38,70,256]{2,1,0:T(8,128)(2,1)} fusion(bf16[3,3,256]{2,1,0:T(4,128)(2,1)S(1)} %slice.23, bf16[3,64,256]{2,1,0:T(8,128)(2,1)S(1)} %copy-done.5, bf16[3,3,256]{2,1,0:T(4,128)(2,1)S(1)} %slice.22, bf16[32,3,256]{2,1,0:T(4,128)(2,1)S(1)} %slice.21, bf16[32,64,256]{2,1,0:T(8,128)(2,1)S(1)} %copy-done.3, ...), kind=kLoop, calls=%fused_computation.2 | loop fusion | flops 12257280 | bytes 2723840 | tf_op jit(solution)/shard_map/concatenate | solution.py:96
  20.9 18.1 %shard_map.132 = (bf16[32,64,256]{2,1,0:T(8,128)(2,1)}, bf16[2048,256]{1,0:T(8,128)(2,1)}) custom-call(bf16[38,70,256]{2,1,0:T(8,128)(2,1)} %maximum_maximum_fusion.pad_ref, f32[7,7,256]{2,1,0:T(8,128)} %w_ref.1, bf16[32,64,256]{2,1,0:T(8,128)(2,1)} %atm_ref.1, f32[1,256]{1,0:T(1,128)} %bitcast.20, bf16[256,1024]{1,0:T(8,128)(2,1)} %up_hbm.1, ...), custom_call_target="tpu_custom_call" | custom-call | flops 2467299328 | bytes 4194304 | tf_op jit(solution)/shard_map/pallas_call | solution.py:272
  39.0 1.6 %reshape.46 = bf16[128,4096]{1,0:T(8,128)(2,1)S(1)} reshape(bf16[2048,256]{1,0:T(8,128)(2,1)} %get-tuple-element.21) | data formatting | bytes 2097152 | tf_op jit(solution)/shard_map/reshape | solution.py:337
  40.6 0.7 fusion
  41.3 0.6 copy.15
  42.0 0.4 copy-done
  42.3 0.2 copy-done.1
  42.5 52.4 %shard_map.133 = bf16[128,2,16,256]{3,2,1,0:T(8,128)(2,1)S(1)} custom-call(bf16[128,2,16,256]{3,2,1,0:T(8,128)(2,1)S(1)} %bitcast.11, bf16[128,2,16,256]{3,2,1,0:T(8,128)(2,1)} %bitcast.19, f32[1,256]{1,0:T(1,128)S(1)} %bitcast.13, bf16[256,1024]{1,0:T(8,128)(2,1)S(1)} %copy-done, bf16[1024,256]{1,0:T(8,128)(2,1)S(1)} %copy-done.1), custom_call_target="tpu_custom_call" | custom-call | flops 4294967296 | bytes 8388608 | tf_op jit(solution)/shard_map/pallas_call | solution.py:188
  94.9 1.3 %copy.17 = bf16[1,128,2,16,256]{4,3,2,1,0:T(8,128)(2,1)} copy(bf16[1,128,2,16,256]{4,3,2,1,0:T(8,128)(2,1)S(1)} %bitcast.12) | data formatting | bytes 4194304
  (12 shorter events, 0.1 us)
Async XLA Ops:
  4.0 15.3 %copy-start.3 = (bf16[32,64,256]{2,1,0:T(8,128)(2,1)S(1)}, bf16[32,64,256]{2,1,0:T(8,128)(2,1)}, u32[]{:S(2)}) copy-start(bf16[32,64,256]{2,1,0:T(8,128)(2,1)} %atm_ref.1) | copy-start | bytes 3145732
  13.8 5.6 %copy-start.4 = (bf16[3,64,256]{2,1,0:T(8,128)(2,1)S(1)}, bf16[3,64,256]{2,1,0:T(8,128)(2,1)}, u32[]{:S(2)}) copy-start(bf16[3,64,256]{2,1,0:T(8,128)(2,1)} %get-tuple-element.13) | copy-start | bytes 294916
  13.8 5.6 %copy-start.5 = (bf16[3,64,256]{2,1,0:T(8,128)(2,1)S(1)}, bf16[3,64,256]{2,1,0:T(8,128)(2,1)}, u32[]{:S(2)}) copy-start(bf16[3,64,256]{2,1,0:T(8,128)(2,1)} %get-tuple-element.18) | copy-start | bytes 294916
  41.3 1.0 %copy-start = (bf16[256,1024]{1,0:T(8,128)(2,1)S(1)}, bf16[256,1024]{1,0:T(8,128)(2,1)}, u32[]{:S(2)}) copy-start(bf16[256,1024]{1,0:T(8,128)(2,1)} %up_ref.1) | copy-start | bytes 1572868
  41.3 1.2 %copy-start.1 = (bf16[1024,256]{1,0:T(8,128)(2,1)S(1)}, bf16[1024,256]{1,0:T(8,128)(2,1)}, u32[]{:S(2)}) copy-start(bf16[1024,256]{1,0:T(8,128)(2,1)} %down_ref.1) | copy-start | bytes 1572868
  41.3 1.2 %copy-start.2 = (f32[256]{0:T(256)S(1)}, f32[256]{0:T(256)}, u32[]{:S(2)}) copy-start(f32[256]{0:T(256)} %param.21) | copy-start | bytes 3076

commit v10 on v9

--- a/solution.py
+++ b/solution.py
@@ -87,13 +87,7 @@
         scratch_shapes=[pltpu.SemaphoreType.DMA((8,)), pltpu.SemaphoreType.DMA((8,))],
         compiler_params=pltpu.CompilerParams(collective_id=1, has_side_effects=True),
     )(x)
-    above, below, left, right, above_left, above_right, below_left, below_right = got
-    left, above_left, below_left = (a[:, side - w:] for a in (left, above_left, below_left))
-    right, above_right, below_right = (a[:, :w] for a in (right, above_right, below_right))
-    top = jnp.concatenate([above_left, above, above_right], axis=1)
-    mid = jnp.concatenate([left, x, right], axis=1)
-    bottom = jnp.concatenate([below_left, below, below_right], axis=1)
-    return jnp.concatenate([top, mid, bottom], axis=0)
+    return got
 
 
 def exchange_body(n_lon, n, group, out_ref, state_ref, gain_ref, up_ref, down_ref,
@@ -205,7 +199,8 @@
     )(outgoing, state, gain.reshape(1, channels), w_up, w_down)
 
 
-def atmos_body(kw, band, pad_ref, w_ref, atm_ref, gain_ref, up_hbm, down_hbm, fw_hbm,
+def atmos_body(kw, band, side, w_ref, atm_ref, gain_ref, up_hbm, down_hbm, fw_hbm,
+               above, below, left, right, above_left, above_right, below_left, below_right,
                out_ref, flux_ref, xf_ref, xs_ref, mixed_ref, up_ref, down_ref, fw_ref, sems):
     rows, cols, channels = atm_ref.shape
     weights = [
@@ -215,12 +210,20 @@
     ]
     for copy in weights:
         copy.start()
-    xf_ref[:, : pad_ref.shape[1], :] = pad_ref[...].astype(jnp.float32)
-
-    @pl.loop(0, pad_ref.shape[0])
+    m = kw // 2
+    for r0, r1, l_ref, c_ref, r_ref in (
+        (0, m, above_left, above, above_right),
+        (m, m + rows, left, atm_ref, right),
+        (m + rows, 2 * m + rows, below_left, below, below_right),
+    ):
+        xf_ref[r0:r1, 0:side, :] = l_ref[...].astype(jnp.float32)
+        xf_ref[r0:r1, side:side + cols, :] = c_ref[...].astype(jnp.float32)
+        xf_ref[r0:r1, side + cols:, :] = r_ref[...].astype(jnp.float32)
+
+    @pl.loop(0, rows + 2 * m)
     def _(i):
         for q in range(kw):
-            xs_ref[q, i] = xf_ref[i, pl.ds(q, cols), :]
+            xs_ref[q, i] = xf_ref[i, pl.ds(side - m + q, cols), :]
 
     @pl.loop(0, rows // band)
     def _(b):
@@ -262,7 +265,7 @@
         flux_ref[pl.ds(k * cells, cells)] = flux.astype(jnp.bfloat16)
 
 
-def atmosphere_block(padded, conv_weight, atmosphere, gain, w_up, w_down, flux_weight):
+def atmosphere_block(pieces, conv_weight, atmosphere, gain, w_up, w_down, flux_weight):
     rows, cols, channels = atmosphere.shape
     kw = conv_weight.shape[0]
     hid = w_up.shape[1]
@@ -270,16 +273,16 @@
     hbm = pl.BlockSpec(memory_space=pl.ANY)
     cells = rows * cols
     return pl.pallas_call(
-        functools.partial(atmos_body, kw, 4),
+        functools.partial(atmos_body, kw, 4, pieces[2].shape[1]),
         out_shape=(
             jax.ShapeDtypeStruct(atmosphere.shape, atmosphere.dtype),
             jax.ShapeDtypeStruct((cells, channels), jnp.bfloat16),
         ),
-        in_specs=[vmem] * 4 + [hbm] * 3,
+        in_specs=[vmem] * 3 + [hbm] * 3 + [vmem] * 8,
         out_specs=(vmem, vmem),
         scratch_shapes=[
-            pltpu.VMEM((padded.shape[0], -(-padded.shape[1] // 8) * 8, channels), jnp.float32),
-            pltpu.VMEM((kw, padded.shape[0], cols, channels), jnp.float32),
+            pltpu.VMEM((rows + kw - 1, cols + 2 * pieces[2].shape[1], channels), jnp.float32),
+            pltpu.VMEM((kw, rows + kw - 1, cols, channels), jnp.float32),
             pltpu.VMEM((rows, cols, channels), jnp.float32),
             pltpu.VMEM(w_up.shape, w_up.dtype),
             pltpu.VMEM(w_down.shape, w_down.dtype),
@@ -292,7 +295,7 @@
             transcendentals=cells * hid,
             bytes_accessed=cells * channels * 8,
         ),
-    )(padded, conv_weight, atmosphere, gain.reshape(1, channels), w_up, w_down, flux_weight)
+    )(conv_weight, atmosphere, gain.reshape(1, channels), w_up, w_down, flux_weight, *pieces)
 
 
 def normalize(values, scales):
@@ -331,8 +334,8 @@
     peer_count = ocean_state.shape[1]
     capacity = ocean_state.shape[2]
     tile_cells = ocean_state.shape[3]
-    padded = halo_pad(atmosphere, margin)
-    atmos_new, fluxes = atmosphere_block(padded, conv_weight, atmosphere, atm_gain, atm_up, atm_down, flux_weight)
+    pieces = halo_pad(atmosphere, margin)
+    atmos_new, fluxes = atmosphere_block(pieces, conv_weight, atmosphere, atm_gain, atm_up, atm_down, flux_weight)
     wet = land_mask.reshape(tile_count, tile_cells, 1).astype(jnp.bfloat16)
     flux_tiles = (fluxes.reshape(tile_count, tile_cells, channels) * wet).reshape(tile_count, tile_cells * channels)
     member = (owners[:, None] == jnp.arange(peer_count, dtype=jnp.int32)[None, :]).astype(jnp.int32)

time: 97.3 us -> 90.5 us (0.930)
  local copies, waits for them, and re-layouts: 9.66 us -> 4.89 us
  other arithmetic: 4.83 us -> 3.24 us
    slice x6 -> x0, local copies, waits for them, and re-layouts: 4.75 us -> none  [the longest x3 2.4 us: halo_pad(): a[:, side - w:]]
    concatenate x1 -> x0, other arithmetic: 1.6 us -> none  [halo_pad(): return jnp.concatenate([top, mid, bottom], axis=0)]
    unnamed x15 -> x9, local copies, waits for them, and re-layouts: 2.93 us -> 2.92 us
where the time goes in v10:
time: 90.5 us; the launch traced here: 89.6 us
  Pallas kernels  80 us (88%)
  local copies, waits for them, and re-layouts  4.89 us (5%)
  other arithmetic  3.24 us (4%)
    pallas_call x1, Pallas kernels, exchange_and_ocean(): pl.pallas_call(functools.partial(exchange_body, n_lon, n, group), out_sha...  52.4 us
    pallas_call x1, Pallas kernels, atmosphere_block(): pl.pallas_call(functools.partial(atmos_body, kw, 4, pieces[2].shape[1]),...  17.9 us
    pallas_call x1, Pallas kernels, halo_pad(): pl.pallas_call(functools.partial(halo_body, lax.axis_size('lat'), lax.axi...  9.76 us
    unnamed x9, local copies, waits for them, and re-layouts  2.92 us

profile of v10, /device:TPU:99, one launch (start us, length us, event | category | flops | bytes accessed | tf_op | source)
XLA Modules:
  0.0 89.6 jit_solution(1889106650910156368)
XLA Ops:
  0.6 0.7 convert_element_type.28
  1.4 0.1 convert_element_type.29
  1.4 0.7 fusion.4
  2.2 0.2 reduce_window_sum.11
  2.4 0.8 select_reduce_fusion
  3.2 0.7 add_add_fusion
  3.9 0.1 convert_reduce_fusion
  4.0 9.8 %shard_map.131 = (bf16[3,64,256]{2,1,0:T(8,128)(2,1)}, bf16[3,64,256]{2,1,0:T(8,128)(2,1)}, bf16[32,8,256]{2,1,0:T(8,128)(2,1)}, bf16[32,8,256]{2,1,0:T(8,128)(2...) custom-call(bf16[32,64,256]{2,1,0:T(8,128)(2,1)} %atm_ref.1), custom_call_target="tpu_custom_call" | custom-call | tf_op jit(solution)/shard_map/pallas_call | solution.py:82
  13.7 0.3 mul.27
  14.1 0.4 copy.14
  14.5 17.9 %shard_map.132 = (bf16[32,64,256]{2,1,0:T(8,128)(2,1)}, bf16[2048,256]{1,0:T(8,128)(2,1)}) custom-call(f32[7,7,256]{2,1,0:T(8,128)} %w_ref.1, bf16[32,64,256]{2,1,0:T(8,128)(2,1)} %atm_ref.1, f32[1,256]{1,0:T(1,128)} %bitcast.20, bf16[256,1024]{1,0:T(8,128)(2,1)} %up_hbm.1, bf16[1024,256]{1,0:T(8,128)(2,1)} %down_hbm.1, bf16[256,256]{1,0:T(8,128)(2,1)} %fw_hbm.1, ...), custom_call_target="tpu_custom_call" | custom-call | flops 2467299328 | bytes 4194304 | tf_op jit(solution)/shard_map/pallas_call | solution.py:275
  32.4 1.6 %reshape.46 = bf16[128,4096]{1,0:T(8,128)(2,1)S(1)} reshape(bf16[2048,256]{1,0:T(8,128)(2,1)} %get-tuple-element.21) | data formatting | bytes 2097152 | tf_op jit(solution)/shard_map/reshape | solution.py:340
  33.9 0.7 fusion
  34.7 0.0 copy-start
  34.7 0.0 copy-start.1
  34.7 0.0 copy-start.2
  34.7 0.6 copy.15
  35.3 0.4 copy-done
  35.7 0.2 copy-done.1
  35.9 0.0 copy-done.2
  35.9 52.4 %shard_map.133 = bf16[128,2,16,256]{3,2,1,0:T(8,128)(2,1)S(1)} custom-call(bf16[128,2,16,256]{3,2,1,0:T(8,128)(2,1)S(1)} %bitcast.11, bf16[128,2,16,256]{3,2,1,0:T(8,128)(2,1)} %bitcast.19, f32[1,256]{1,0:T(1,128)S(1)} %bitcast.13, bf16[256,1024]{1,0:T(8,128)(2,1)S(1)} %copy-done, bf16[1024,256]{1,0:T(8,128)(2,1)S(1)} %copy-done.1), custom_call_target="tpu_custom_call" | custom-call | flops 4294967296 | bytes 8388608 | tf_op jit(solution)/shard_map/pallas_call | solution.py:182
  88.2 1.3 %copy.17 = bf16[1,128,2,16,256]{4,3,2,1,0:T(8,128)(2,1)} copy(bf16[1,128,2,16,256]{4,3,2,1,0:T(8,128)(2,1)S(1)} %bitcast.12) | data formatting | bytes 4194304
  (1 shorter events, 0.0 us)
Async XLA Ops:
  34.7 1.0 %copy-start = (bf16[256,1024]{1,0:T(8,128)(2,1)S(1)}, bf16[256,1024]{1,0:T(8,128)(2,1)}, u32[]{:S(2)}) copy-start(bf16[256,1024]{1,0:T(8,128)(2,1)} %up_ref.1) | copy-start | bytes 1572868
  34.7 1.2 %copy-start.1 = (bf16[1024,256]{1,0:T(8,128)(2,1)S(1)}, bf16[1024,256]{1,0:T(8,128)(2,1)}, u32[]{:S(2)}) copy-start(bf16[1024,256]{1,0:T(8,128)(2,1)} %down_ref.1) | copy-start | bytes 1572868
  34.7 1.2 %copy-start.2 = (f32[256]{0:T(256)S(1)}, f32[256]{0:T(256)}, u32[]{:S(2)}) copy-start(f32[256]{0:T(256)} %param.21) | copy-start | bytes 3076

commit v11 on v10

--- a/solution.py
+++ b/solution.py
@@ -90,6 +90,15 @@
     return got
 
 
+def partner(a, b, n):
+    total = 0
+    bit = 1
+    while bit < n:
+        total = total + lax.rem(lax.div(a, bit) + lax.div(b, bit), 2) * bit
+        bit *= 2
+    return total
+
+
 def exchange_body(n_lon, n, group, out_ref, state_ref, gain_ref, up_ref, down_ref,
                   res_ref, recv_ref, stage_ref, send_sems, recv_sems):
     me = lax.axis_index("lat") * n_lon + lax.axis_index("lon")
@@ -101,12 +110,12 @@
 
     @pl.loop(1, n)
     def _(j):
-        pl.semaphore_signal(barrier, inc=1, device_id=coords(lax.rem(me + j, n)), device_id_type=MESH)
+        pl.semaphore_signal(barrier, inc=1, device_id=coords(partner(me, j, n)), device_id_type=MESH)
 
     pl.semaphore_wait(barrier, n - 1)
 
     def send_copy(j):
-        peer = lax.rem(me + j, n)
+        peer = partner(me, j, n)
         return pltpu.make_async_remote_copy(
             src_ref=out_ref.at[peer],
             dst_ref=recv_ref.at[j],
@@ -117,7 +126,7 @@
         )
 
     def recv_copy(j):
-        source = lax.rem(me - j + n, n)
+        source = partner(me, j, n)
         return pltpu.make_async_remote_copy(
             src_ref=out_ref.at[source],
             dst_ref=recv_ref.at[j],
@@ -147,7 +156,7 @@
             def _():
                 recv_copy(j).wait_recv()
 
-            stage_ref[i] = state_ref[lax.rem(me - j + n, n)]
+            stage_ref[i] = state_ref[partner(me, j, n)]
 
         fluxes = recv_ref[pl.ds(base, group)]
         used = fluxes[:, :, 0:1, 0:1] == fluxes[:, :, 0:1, 0:1]
@@ -165,7 +174,7 @@
 
         @pl.loop(0, group)
         def _(i):
-            res_ref[lax.rem(me - base - i + n, n)] = stage_ref[i]
+            res_ref[partner(me, base + i, n)] = stage_ref[i]
 
     @pl.loop(1, n)
     def _(j):
@@ -175,6 +184,7 @@
 def exchange_and_ocean(outgoing, state, gain, w_up, w_down):
     n_lon = lax.axis_size("lon")
     n = n_lon * lax.axis_size("lat")
+    assert n & (n - 1) == 0
     group = 16
     rows = outgoing.shape[0] * outgoing.shape[1] * outgoing.shape[2]
     channels, hid = w_up.shape

time: 90.5 us -> 99.3 us (1.097)
  the two profiles are of different devices: /device:TPU:99 before, /device:TPU:1 now
where the time goes in v11:
time: 99.3 us; the launch traced here: 99 us
  Pallas kernels  89.4 us (90%)
  local copies, waits for them, and re-layouts  4.89 us (5%)
  other arithmetic  3.24 us (3%)
    pallas_call x1, Pallas kernels, exchange_and_ocean(): pl.pallas_call(functools.partial(exchange_body, n_lon, n, group), out_sha...  58.3 us
    pallas_call x1, Pallas kernels, atmosphere_block(): pl.pallas_call(functools.partial(atmos_body, kw, 4, pieces[2].shape[1]),...  17.9 us
    pallas_call x1, Pallas kernels, halo_pad(): pl.pallas_call(functools.partial(halo_body, lax.axis_size('lat'), lax.axi...  13.3 us
    unnamed x9, local copies, waits for them, and re-layouts  2.92 us

profile of v11, /device:TPU:1, one launch (start us, length us, event | category | flops | bytes accessed | tf_op | source)
XLA Modules:
  0.0 99.0 jit_solution(5590235940636312409)
XLA Ops:
  0.6 0.7 convert_element_type.28
  1.4 0.1 convert_element_type.29
  1.4 0.7 fusion.4
  2.2 0.2 reduce_window_sum.11
  2.4 0.8 select_reduce_fusion
  3.2 0.7 add_add_fusion
  3.9 0.1 convert_reduce_fusion
  4.0 13.3 %shard_map.131 = (bf16[3,64,256]{2,1,0:T(8,128)(2,1)}, bf16[3,64,256]{2,1,0:T(8,128)(2,1)}, bf16[32,8,256]{2,1,0:T(8,128)(2,1)}, bf16[32,8,256]{2,1,0:T(8,128)(2...) custom-call(bf16[32,64,256]{2,1,0:T(8,128)(2,1)} %atm_ref.1), custom_call_target="tpu_custom_call" | custom-call | tf_op jit(solution)/shard_map/pallas_call | solution.py:82
  17.3 0.3 mul.27
  17.6 0.4 copy.14
  18.1 17.9 %shard_map.132 = (bf16[32,64,256]{2,1,0:T(8,128)(2,1)}, bf16[2048,256]{1,0:T(8,128)(2,1)}) custom-call(f32[7,7,256]{2,1,0:T(8,128)} %w_ref.1, bf16[32,64,256]{2,1,0:T(8,128)(2,1)} %atm_ref.1, f32[1,256]{1,0:T(1,128)} %bitcast.20, bf16[256,1024]{1,0:T(8,128)(2,1)} %up_hbm.1, bf16[1024,256]{1,0:T(8,128)(2,1)} %down_hbm.1, bf16[256,256]{1,0:T(8,128)(2,1)} %fw_hbm.1, ...), custom_call_target="tpu_custom_call" | custom-call | flops 2467299328 | bytes 4194304 | tf_op jit(solution)/shard_map/pallas_call | solution.py:285
  35.9 1.6 %reshape.46 = bf16[128,4096]{1,0:T(8,128)(2,1)S(1)} reshape(bf16[2048,256]{1,0:T(8,128)(2,1)} %get-tuple-element.21) | data formatting | bytes 2097152 | tf_op jit(solution)/shard_map/reshape | solution.py:350
  37.5 0.7 fusion
  38.2 0.0 copy-start
  38.2 0.0 copy-start.1
  38.2 0.0 copy-start.2
  38.2 0.6 copy.15
  38.9 0.4 copy-done
  39.3 0.2 copy-done.1
  39.4 0.0 copy-done.2
  39.4 58.3 %shard_map.133 = bf16[128,2,16,256]{3,2,1,0:T(8,128)(2,1)S(1)} custom-call(bf16[128,2,16,256]{3,2,1,0:T(8,128)(2,1)S(1)} %bitcast.11, bf16[128,2,16,256]{3,2,1,0:T(8,128)(2,1)} %bitcast.19, f32[1,256]{1,0:T(1,128)S(1)} %bitcast.13, bf16[256,1024]{1,0:T(8,128)(2,1)S(1)} %copy-done, bf16[1024,256]{1,0:T(8,128)(2,1)S(1)} %copy-done.1), custom_call_target="tpu_custom_call" | custom-call | flops 4294967296 | bytes 8388608 | tf_op jit(solution)/shard_map/pallas_call | solution.py:192
  97.7 1.3 %copy.17 = bf16[1,128,2,16,256]{4,3,2,1,0:T(8,128)(2,1)} copy(bf16[1,128,2,16,256]{4,3,2,1,0:T(8,128)(2,1)S(1)} %bitcast.12) | data formatting | bytes 4194304
  (1 shorter events, 0.0 us)
Async XLA Ops:
  38.2 1.0 %copy-start = (bf16[256,1024]{1,0:T(8,128)(2,1)S(1)}, bf16[256,1024]{1,0:T(8,128)(2,1)}, u32[]{:S(2)}) copy-start(bf16[256,1024]{1,0:T(8,128)(2,1)} %up_ref.1) | copy-start | bytes 1572868
  38.2 1.2 %copy-start.1 = (bf16[1024,256]{1,0:T(8,128)(2,1)S(1)}, bf16[1024,256]{1,0:T(8,128)(2,1)}, u32[]{:S(2)}) copy-start(bf16[1024,256]{1,0:T(8,128)(2,1)} %down_ref.1) | copy-start | bytes 1572868
  38.2 1.2 %copy-start.2 = (f32[256]{0:T(256)S(1)}, f32[256]{0:T(256)}, u32[]{:S(2)}) copy-start(f32[256]{0:T(256)} %param.21) | copy-start | bytes 3076

commit v12 on v10

--- a/solution.py
+++ b/solution.py
@@ -128,15 +128,21 @@
         )
 
     @pl.loop(1, n)
-    def _(j):
-        send_copy(j).start()
+    def _(t):
+        half = lax.div(t + 1, 2)
+        odd = lax.rem(t, 2)
+        send_copy(odd * half + (1 - odd) * (n - half)).start()
 
     recv_ref[0] = out_ref[me]
     slots, cells, channels = out_ref.shape[1], out_ref.shape[2], out_ref.shape[3]
     rows = group * slots * cells
 
-    @pl.loop(0, n // group)
-    def _(g):
+    groups = n // group
+
+    @pl.loop(0, groups)
+    def _(gi):
+        odd = lax.rem(gi, 2)
+        g = odd * (groups - 1 - lax.div(gi, 2)) + (1 - odd) * lax.div(gi, 2)
         base = g * group
 
         @pl.loop(0, group)

time: 90.5 us -> 93.9 us (1.038)
  Pallas kernels: 80 us -> 84.1 us
    pallas_call x1, Pallas kernels: 52.4 us -> 56.5 us  [exchange_and_ocean(): pl.pallas_call(functools.partial(exchange_body, n_lon, n, group), out_sha...]
where the time goes in v12:
time: 93.9 us; the launch traced here: 93.6 us
  Pallas kernels  84.1 us (90%)
  local copies, waits for them, and re-layouts  4.89 us (5%)
  other arithmetic  3.24 us (3%)
    pallas_call x1, Pallas kernels, exchange_and_ocean(): pl.pallas_call(functools.partial(exchange_body, n_lon, n, group), out_sha...  56.5 us
    pallas_call x1, Pallas kernels, atmosphere_block(): pl.pallas_call(functools.partial(atmos_body, kw, 4, pieces[2].shape[1]),...  17.9 us
    pallas_call x1, Pallas kernels, halo_pad(): pl.pallas_call(functools.partial(halo_body, lax.axis_size('lat'), lax.axi...  9.76 us
    unnamed x9, local copies, waits for them, and re-layouts  2.92 us

profile of v12, /device:TPU:99, one launch (start us, length us, event | category | flops | bytes accessed | tf_op | source)
XLA Modules:
  0.0 93.6 jit_solution(11260109949705986529)
XLA Ops:
  0.6 0.7 convert_element_type.28
  1.4 0.1 convert_element_type.29
  1.4 0.7 fusion.4
  2.2 0.2 reduce_window_sum.11
  2.4 0.8 select_reduce_fusion
  3.2 0.7 add_add_fusion
  3.9 0.1 convert_reduce_fusion
  4.0 9.8 %shard_map.131 = (bf16[3,64,256]{2,1,0:T(8,128)(2,1)}, bf16[3,64,256]{2,1,0:T(8,128)(2,1)}, bf16[32,8,256]{2,1,0:T(8,128)(2,1)}, bf16[32,8,256]{2,1,0:T(8,128)(2...) custom-call(bf16[32,64,256]{2,1,0:T(8,128)(2,1)} %atm_ref.1), custom_call_target="tpu_custom_call" | custom-call | tf_op jit(solution)/shard_map/pallas_call | solution.py:82
  13.7 0.3 mul.27
  14.1 0.4 copy.14
  14.5 17.9 %shard_map.132 = (bf16[32,64,256]{2,1,0:T(8,128)(2,1)}, bf16[2048,256]{1,0:T(8,128)(2,1)}) custom-call(f32[7,7,256]{2,1,0:T(8,128)} %w_ref.1, bf16[32,64,256]{2,1,0:T(8,128)(2,1)} %atm_ref.1, f32[1,256]{1,0:T(1,128)} %bitcast.20, bf16[256,1024]{1,0:T(8,128)(2,1)} %up_hbm.1, bf16[1024,256]{1,0:T(8,128)(2,1)} %down_hbm.1, bf16[256,256]{1,0:T(8,128)(2,1)} %fw_hbm.1, ...), custom_call_target="tpu_custom_call" | custom-call | flops 2467299328 | bytes 4194304 | tf_op jit(solution)/shard_map/pallas_call | solution.py:281
  32.4 1.6 %reshape.46 = bf16[128,4096]{1,0:T(8,128)(2,1)S(1)} reshape(bf16[2048,256]{1,0:T(8,128)(2,1)} %get-tuple-element.21) | data formatting | bytes 2097152 | tf_op jit(solution)/shard_map/reshape | solution.py:346
  33.9 0.7 fusion
  34.7 0.0 copy-start
  34.7 0.0 copy-start.1
  34.7 0.0 copy-start.2
  34.7 0.6 copy.15
  35.3 0.4 copy-done
  35.7 0.2 copy-done.1
  35.9 0.0 copy-done.2
  35.9 56.5 %shard_map.133 = bf16[128,2,16,256]{3,2,1,0:T(8,128)(2,1)S(1)} custom-call(bf16[128,2,16,256]{3,2,1,0:T(8,128)(2,1)S(1)} %bitcast.11, bf16[128,2,16,256]{3,2,1,0:T(8,128)(2,1)} %bitcast.19, f32[1,256]{1,0:T(1,128)S(1)} %bitcast.13, bf16[256,1024]{1,0:T(8,128)(2,1)S(1)} %copy-done, bf16[1024,256]{1,0:T(8,128)(2,1)S(1)} %copy-done.1), custom_call_target="tpu_custom_call" | custom-call | flops 4294967296 | bytes 8388608 | tf_op jit(solution)/shard_map/pallas_call | solution.py:188
  92.3 1.3 %copy.17 = bf16[1,128,2,16,256]{4,3,2,1,0:T(8,128)(2,1)} copy(bf16[1,128,2,16,256]{4,3,2,1,0:T(8,128)(2,1)S(1)} %bitcast.12) | data formatting | bytes 4194304
  (1 shorter events, 0.0 us)
Async XLA Ops:
  34.7 1.0 %copy-start = (bf16[256,1024]{1,0:T(8,128)(2,1)S(1)}, bf16[256,1024]{1,0:T(8,128)(2,1)}, u32[]{:S(2)}) copy-start(bf16[256,1024]{1,0:T(8,128)(2,1)} %up_ref.1) | copy-start | bytes 1572868
  34.7 1.2 %copy-start.1 = (bf16[1024,256]{1,0:T(8,128)(2,1)S(1)}, bf16[1024,256]{1,0:T(8,128)(2,1)}, u32[]{:S(2)}) copy-start(bf16[1024,256]{1,0:T(8,128)(2,1)} %down_ref.1) | copy-start | bytes 1572868
  34.7 1.2 %copy-start.2 = (f32[256]{0:T(256)S(1)}, f32[256]{0:T(256)}, u32[]{:S(2)}) copy-start(f32[256]{0:T(256)} %param.21) | copy-start | bytes 3076

commit v13 on v9

--- a/solution.py
+++ b/solution.py
@@ -13,87 +13,6 @@
 
 
 HALO_MOVES = ((1, 0), (-1, 0), (0, 1), (0, -1), (1, 1), (1, -1), (-1, 1), (-1, -1))
-
-
-def halo_body(n_lat, n_lon, w, side, x_ref, *refs):
-    got, send_sems, recv_sems = refs[:8], refs[8], refs[9]
-    rows, cols = x_ref.shape[0], x_ref.shape[1]
-    lat, lon = lax.axis_index("lat"), lax.axis_index("lon")
-    has_up = lat > 0
-    has_down = lat < n_lat - 1
-    row_part = {1: pl.ds(rows - w, w), -1: pl.ds(0, w), 0: pl.ds(0, rows)}
-    col_part = {1: pl.ds(cols - side, side), -1: pl.ds(0, side), 0: pl.ds(0, cols)}
-
-    def exists(d_lat):
-        return has_down if d_lat > 0 else (has_up if d_lat < 0 else lat >= 0)
-
-    def exists_from(d_lat):
-        return has_up if d_lat > 0 else (has_down if d_lat < 0 else lat >= 0)
-
-    def target(d_lat, d_lon):
-        return (lax.rem(lon + d_lon + n_lon, n_lon), lat + d_lat)
-
-    barrier = pltpu.get_barrier_semaphore()
-    for d_lat, d_lon in HALO_MOVES:
-        @pl.when(exists(d_lat))
-        def _():
-            pl.semaphore_signal(barrier, inc=1, device_id=target(d_lat, d_lon), device_id_type=MESH)
-
-    pl.semaphore_wait(barrier, 2 + 3 * has_up.astype(jnp.int32) + 3 * has_down.astype(jnp.int32))
-
-    def copy(p):
-        d_lat, d_lon = HALO_MOVES[p]
-        return pltpu.make_async_remote_copy(
-            src_ref=x_ref.at[row_part[d_lat], col_part[d_lon]],
-            dst_ref=got[p],
-            send_sem=send_sems.at[p],
-            recv_sem=recv_sems.at[p],
-            device_id=target(d_lat, d_lon),
-            device_id_type=MESH,
-        )
-
-    for p, (d_lat, d_lon) in enumerate(HALO_MOVES):
-        @pl.when(exists(d_lat))
-        def _():
-            copy(p).start()
-
-    for p, (d_lat, d_lon) in enumerate(HALO_MOVES):
-        @pl.when(exists_from(d_lat))
-        def _():
-            copy(p).wait_recv()
-
-        @pl.when(jnp.logical_not(exists_from(d_lat)))
-        def _():
-            got[p][...] = jnp.zeros(got[p].shape, got[p].dtype)
-
-    for p, (d_lat, d_lon) in enumerate(HALO_MOVES):
-        @pl.when(exists(d_lat))
-        def _():
-            copy(p).wait_send()
-
-
-def halo_pad(x, w):
-    rows, cols, channels = x.shape
-    side = 8
-    shapes = []
-    for d_lat, d_lon in HALO_MOVES:
-        shapes.append((w if d_lat else rows, side if d_lon else cols, channels))
-    vmem = pl.BlockSpec(memory_space=pltpu.VMEM)
-    got = pl.pallas_call(
-        functools.partial(halo_body, lax.axis_size("lat"), lax.axis_size("lon"), w, side),
-        out_shape=tuple(jax.ShapeDtypeStruct(sh, x.dtype) for sh in shapes),
-        in_specs=[pl.BlockSpec(memory_space=pl.ANY)],
-        out_specs=tuple([vmem] * 8),
-        scratch_shapes=[pltpu.SemaphoreType.DMA((8,)), pltpu.SemaphoreType.DMA((8,))],
-        compiler_params=pltpu.CompilerParams(collective_id=1, has_side_effects=True),
-    )(x)
-    above, below, left, right, above_left, above_right, below_left, below_right = got
-    left, above_left, below_left = (a[:, side - w:] for a in (left, above_left, below_left))
-    right, above_right, below_right = (a[:, :w] for a in (right, above_right, below_right))
-    top = jnp.concatenate([above_left, above, above_right], axis=1)
-    mid = jnp.concatenate([left, x, right], axis=1)
-    bottom = jnp.concatenate([below_left, below, below_right], axis=1)
-    return jnp.concatenate([top, mid, bottom], axis=0)
 
 
 def exchange_body(n_lon, n, group, out_ref, state_ref, gain_ref, up_ref, down_ref,
@@ -205,9 +124,51 @@
     )(outgoing, state, gain.reshape(1, channels), w_up, w_down)
 
 
-def atmos_body(kw, band, pad_ref, w_ref, atm_ref, gain_ref, up_hbm, down_hbm, fw_hbm,
-               out_ref, flux_ref, xf_ref, xs_ref, mixed_ref, up_ref, down_ref, fw_ref, sems):
+def atmos_body(n_lat, n_lon, kw, band, side, x_hbm, w_ref, atm_ref, gain_ref, up_hbm, down_hbm, fw_hbm,
+               out_ref, flux_ref, above, below, left, right, above_left, above_right, below_left, below_right,
+               xf_ref, xs_ref, mixed_ref, up_ref, down_ref, fw_ref, sems, send_sems, recv_sems):
     rows, cols, channels = atm_ref.shape
+    m = kw // 2
+    got = (above, below, left, right, above_left, above_right, below_left, below_right)
+    lat, lon = lax.axis_index("lat"), lax.axis_index("lon")
+    has_up = lat > 0
+    has_down = lat < n_lat - 1
+    row_part = {1: pl.ds(rows - m, m), -1: pl.ds(0, m), 0: pl.ds(0, rows)}
+    col_part = {1: pl.ds(cols - side, side), -1: pl.ds(0, side), 0: pl.ds(0, cols)}
+
+    def exists(d_lat):
+        return has_down if d_lat > 0 else (has_up if d_lat < 0 else lat >= 0)
+
+    def exists_from(d_lat):
+        return has_up if d_lat > 0 else (has_down if d_lat < 0 else lat >= 0)
+
+    def target(d_lat, d_lon):
+        return (lax.rem(lon + d_lon + n_lon, n_lon), lat + d_lat)
+
+    barrier = pltpu.get_barrier_semaphore()
+    for d_lat, d_lon in HALO_MOVES:
+        @pl.when(exists(d_lat))
+        def _():
+            pl.semaphore_signal(barrier, inc=1, device_id=target(d_lat, d_lon), device_id_type=MESH)
+
+    pl.semaphore_wait(barrier, 2 + 3 * has_up.astype(jnp.int32) + 3 * has_down.astype(jnp.int32))
+
+    def halo_copy(p):
+        d_lat, d_lon = HALO_MOVES[p]
+        return pltpu.make_async_remote_copy(
+            src_ref=x_hbm.at[row_part[d_lat], col_part[d_lon]],
+            dst_ref=got[p],
+            send_sem=send_sems.at[p],
+            recv_sem=recv_sems.at[p],
+            device_id=target(d_lat, d_lon),
+            device_id_type=MESH,
+        )
+
+    for p, (d_lat, d_lon) in enumerate(HALO_MOVES):
+        @pl.when(exists(d_lat))
+        def _():
+            halo_copy(p).start()
+
     weights = [
         pltpu.make_async_copy(up_hbm, up_ref, sems.at[0]),
         pltpu.make_async_copy(down_hbm, down_ref, sems.at[1]),
@@ -215,31 +176,78 @@
     ]
     for copy in weights:
         copy.start()
-    xf_ref[:, : pad_ref.shape[1], :] = pad_ref[...].astype(jnp.float32)
-
-    @pl.loop(0, pad_ref.shape[0])
-    def _(i):
-        for q in range(kw):
-            xs_ref[q, i] = xf_ref[i, pl.ds(q, cols), :]
-
-    @pl.loop(0, rows // band)
-    def _(b):
-        r0 = b * band
+
+    xf_ref[m:m + rows, 0:side, :] = jnp.zeros((rows, side, channels), jnp.float32)
+    xf_ref[m:m + rows, side:side + cols, :] = atm_ref[...].astype(jnp.float32)
+    xf_ref[m:m + rows, side + cols:, :] = jnp.zeros((rows, side, channels), jnp.float32)
+
+    def shift_rows(lo, hi, c0, width):
+        @pl.loop(lo, hi)
+        def _(i):
+            for q in range(kw):
+                xs_ref[q, i, pl.ds(c0, width), :] = xf_ref[i, pl.ds(side - m + q + c0, width), :]
+
+    def conv_band(r0, c0, width):
         for cb in range(channels // 128):
             lanes = pl.ds(cb * 128, 128)
-            acc = [jnp.zeros((cols, 128), jnp.float32) for _ in range(band)]
+            acc = [jnp.zeros((width, 128), jnp.float32) for _ in range(band)]
             for q in range(kw):
                 for i in range(band + kw - 1):
-                    line = xs_ref[q, r0 + i, :, lanes]
+                    line = xs_ref[q, r0 + i, pl.ds(c0, width), lanes]
                     for p in range(kw):
                         r = i - p
                         if 0 <= r < band:
                             acc[r] = acc[r] + line * w_ref[p, pl.ds(q, 1), lanes]
             for r in range(band):
-                mixed_ref[r0 + r, :, lanes] = acc[r]
+                mixed_ref[r0 + r, pl.ds(c0, width), lanes] = acc[r]
+
+    shift_rows(m, m + rows, 0, cols)
+    bands = rows // band
+
+    @pl.loop(1, bands - 1)
+    def _(b):
+        conv_band(b * band, 0, cols)
+
+    for p, (d_lat, d_lon) in enumerate(HALO_MOVES):
+        @pl.when(exists_from(d_lat))
+        def _():
+            halo_copy(p).wait_recv()
+
+        @pl.when(jnp.logical_not(exists_from(d_lat)))
+        def _():
+            got[p][...] = jnp.zeros(got[p].shape, got[p].dtype)
+
+    for r0, r1, l_ref, c_ref, r_ref in (
+        (0, m, above_left, above, above_right),
+        (m, m + rows, left, None, right),
+        (m + rows, 2 * m + rows, below_left, below, below_right),
+    ):
+        xf_ref[r0:r1, 0:side, :] = l_ref[...].astype(jnp.float32)
+        if c_ref is not None:
+            xf_ref[r0:r1, side:side + cols, :] = c_ref[...].astype(jnp.float32)
+        xf_ref[r0:r1, side + cols:, :] = r_ref[...].astype(jnp.float32)
+
+    shift_rows(0, m, 0, cols)
+    shift_rows(m + rows, rows + 2 * m, 0, cols)
+    shift_rows(m, m + rows, 0, 8)
+    shift_rows(m, m + rows, cols - 8, 8)
+
+    @pl.loop(0, 2)
+    def _(t):
+        conv_band(t * (bands - 1) * band, 0, cols)
+
+    @pl.loop(1, bands - 1)
+    def _(b):
+        conv_band(b * band, 0, 8)
+        conv_band(b * band, cols - 8, 8)
 
     for copy in weights:
         copy.wait()
+
+    for p, (d_lat, d_lon) in enumerate(HALO_MOVES):
+        @pl.when(exists(d_lat))
+        def _():
+            halo_copy(p).wait_send()
 
     chunk = 8
 
@@ -262,37 +270,46 @@
         flux_ref[pl.ds(k * cells, cells)] = flux.astype(jnp.bfloat16)
 
 
-def atmosphere_block(padded, conv_weight, atmosphere, gain, w_up, w_down, flux_weight):
+def atmosphere_block(conv_weight, atmosphere, gain, w_up, w_down, flux_weight):
     rows, cols, channels = atmosphere.shape
     kw = conv_weight.shape[0]
+    m = kw // 2
+    side = 8
     hid = w_up.shape[1]
     vmem = pl.BlockSpec(memory_space=pltpu.VMEM)
     hbm = pl.BlockSpec(memory_space=pl.ANY)
     cells = rows * cols
+    pieces = []
+    for d_lat, d_lon in HALO_MOVES:
+        pieces.append(pltpu.VMEM((m if d_lat else rows, side if d_lon else cols, channels), atmosphere.dtype))
     return pl.pallas_call(
-        functools.partial(atmos_body, kw, 4),
+        functools.partial(atmos_body, lax.axis_size("lat"), lax.axis_size("lon"), kw, 4, side),
         out_shape=(
             jax.ShapeDtypeStruct(atmosphere.shape, atmosphere.dtype),
             jax.ShapeDtypeStruct((cells, channels), jnp.bfloat16),
         ),
-        in_specs=[vmem] * 4 + [hbm] * 3,
+        in_specs=[hbm] + [vmem] * 3 + [hbm] * 3,
         out_specs=(vmem, vmem),
-        scratch_shapes=[
-            pltpu.VMEM((padded.shape[0], -(-padded.shape[1] // 8) * 8, channels), jnp.float32),
-            pltpu.VMEM((kw, padded.shape[0], cols, channels), jnp.float32),
+        scratch_shapes=pieces + [
+            pltpu.VMEM((rows + kw - 1, cols + 2 * side, channels), jnp.float32),
+            pltpu.VMEM((kw, rows + kw - 1, cols, channels), jnp.float32),
             pltpu.VMEM((rows, cols, channels), jnp.float32),
             pltpu.VMEM(w_up.shape, w_up.dtype),
             pltpu.VMEM(w_down.shape, w_down.dtype),
             pltpu.VMEM(flux_weight.shape, flux_weight.dtype),
             pltpu.SemaphoreType.DMA((3,)),
+            pltpu.SemaphoreType.DMA((8,)),
+            pltpu.SemaphoreType.DMA((8,)),
         ],
-        compiler_params=pltpu.CompilerParams(vmem_limit_bytes=56 * 1024 * 1024),
+        compiler_params=pltpu.CompilerParams(
+            collective_id=1, has_side_effects=True, vmem_limit_bytes=56 * 1024 * 1024
+        ),
         cost_estimate=pl.CostEstimate(
             flops=2 * cells * channels * (kw * kw + 2 * hid + channels),
             transcendentals=cells * hid,
             bytes_accessed=cells * channels * 8,
         ),
-    )(padded, conv_weight, atmosphere, gain.reshape(1, channels), w_up, w_down, flux_weight)
+    )(atmosphere, conv_weight, atmosphere, gain.reshape(1, channels), w_up, w_down, flux_weight)
 
 
 def normalize(values, scales):
@@ -331,8 +348,7 @@
     peer_count = ocean_state.shape[1]
     capacity = ocean_state.shape[2]
     tile_cells = ocean_state.shape[3]
-    padded = halo_pad(atmosphere, margin)
-    atmos_new, fluxes = atmosphere_block(padded, conv_weight, atmosphere, atm_gain, atm_up, atm_down, flux_weight)
+    atmos_new, fluxes = atmosphere_block(conv_weight, atmosphere, atm_gain, atm_up, atm_down, flux_weight)
     wet = land_mask.reshape(tile_count, tile_cells, 1).astype(jnp.bfloat16)
     flux_tiles = (fluxes.reshape(tile_count, tile_cells, channels) * wet).reshape(tile_count, tile_cells * channels)
     member = (owners[:, None] == jnp.arange(peer_count, dtype=jnp.int32)[None, :]).astype(jnp.int32)

time: 97.3 us -> 86.2 us (0.89)
  Pallas kernels: 80.2 us -> 74.3 us
  local copies, waits for them, and re-layouts: 9.66 us -> 5.87 us
  other arithmetic: 4.83 us -> 3.24 us
    pallas_call x2 -> x1, Pallas kernels: 27.8 us -> 22.3 us  [atmosphere_block(): pl.pallas_call(functools.partial(atmos_body, lax.axis_size('lat'), lax.ax...]
    slice x6 -> x0, local copies, waits for them, and re-layouts: 4.75 us -> none  [the longest x3 2.4 us: halo_pad(): a[:, side - w:]]
    concatenate x1 -> x0, other arithmetic: 1.6 us -> none  [halo_pad(): return jnp.concatenate([top, mid, bottom], axis=0)]
    unnamed x15 -> x12, local copies, waits for them, and re-layouts: 2.93 us -> 3.89 us
where the time goes in v13:
time: 86.2 us; the launch traced here: 84.9 us
  Pallas kernels  74.3 us (86%)
  local copies, waits for them, and re-layouts  5.87 us (7%)
  other arithmetic  3.24 us (4%)
    pallas_call x1, Pallas kernels, exchange_and_ocean(): pl.pallas_call(functools.partial(exchange_body, n_lon, n, group), out_sha...  52.1 us
    pallas_call x1, Pallas kernels, atmosphere_block(): pl.pallas_call(functools.partial(atmos_body, lax.axis_size('lat'), lax.ax...  22.3 us
    unnamed x12, local copies, waits for them, and re-layouts  3.89 us

profile of v13, /device:TPU:99, one launch (start us, length us, event | category | flops | bytes accessed | tf_op | source)
XLA Modules:
  0.0 84.9 jit_solution(14311563278961069931)
XLA Ops:
  0.6 0.7 convert_element_type.28
  1.4 0.1 convert_element_type.29
  1.4 0.7 fusion.4
  2.2 0.2 reduce_window_sum.11
  2.4 0.8 select_reduce_fusion
  3.2 0.7 add_add_fusion
  3.9 0.1 convert_reduce_fusion
  4.0 0.3 mul.27
  4.3 0.4 copy.14
  4.8 22.3 %shard_map.131 = (bf16[32,64,256]{2,1,0:T(8,128)(2,1)}, bf16[2048,256]{1,0:T(8,128)(2,1)}) custom-call(bf16[32,64,256]{2,1,0:T(8,128)(2,1)} %atm_ref.1, f32[7,7,256]{2,1,0:T(8,128)} %w_ref.1, bf16[32,64,256]{2,1,0:T(8,128)(2,1)} %atm_ref.1, f32[1,256]{1,0:T(1,128)} %bitcast.20, bf16[256,1024]{1,0:T(8,128)(2,1)} %up_hbm.1, bf16[1024,256]{1,0:T(8,128)(2,1)} %down_hbm.1, ...), custom_call_target="tpu_custom_call" | custom-call | flops 2467299328 | bytes 4194304 | tf_op jit(solution)/shard_map/pallas_call | solution.py:285
  27.0 1.6 %reshape.46 = bf16[128,4096]{1,0:T(8,128)(2,1)S(1)} reshape(bf16[2048,256]{1,0:T(8,128)(2,1)} %get-tuple-element.5) | data formatting | bytes 2097152 | tf_op jit(solution)/shard_map/reshape | solution.py:353
  28.6 0.7 fusion
  29.3 0.0 copy-start
  29.3 0.0 copy-start.1
  29.3 0.0 copy-start.2
  29.3 0.6 copy.15
  30.0 0.4 copy-done
  30.3 0.2 copy-done.1
  30.5 0.0 copy-done.2
  30.5 0.0 copy-start.3
  30.5 52.1 %shard_map.132 = bf16[128,2,16,256]{3,2,1,0:T(8,128)(2,1)S(1)} custom-call(bf16[128,2,16,256]{3,2,1,0:T(8,128)(2,1)S(1)} %bitcast.12, bf16[128,2,16,256]{3,2,1,0:T(8,128)(2,1)} %bitcast.19, f32[1,256]{1,0:T(1,128)S(1)} %bitcast.13, bf16[256,1024]{1,0:T(8,128)(2,1)S(1)} %copy-done, bf16[1024,256]{1,0:T(8,128)(2,1)S(1)} %copy-done.1), custom_call_target="tpu_custom_call" | custom-call | flops 4294967296 | bytes 8388608 | tf_op jit(solution)/shard_map/pallas_call | solution.py:107
  82.6 0.0 copy-done.3
  82.6 1.0 %copy.18 = bf16[32,64,256]{2,1,0:T(8,128)(2,1)} copy(bf16[32,64,256]{2,1,0:T(8,128)(2,1)S(1)} %copy-done.3) | data formatting | bytes 2097152
  83.5 1.3 %copy.19 = bf16[1,128,2,16,256]{4,3,2,1,0:T(8,128)(2,1)} copy(bf16[1,128,2,16,256]{4,3,2,1,0:T(8,128)(2,1)S(1)} %bitcast.11) | data formatting | bytes 4194304
  (1 shorter events, 0.0 us)
Async XLA Ops:
  29.3 1.0 %copy-start = (bf16[256,1024]{1,0:T(8,128)(2,1)S(1)}, bf16[256,1024]{1,0:T(8,128)(2,1)}, u32[]{:S(2)}) copy-start(bf16[256,1024]{1,0:T(8,128)(2,1)} %up_ref.1) | copy-start | bytes 1572868
  29.3 1.2 %copy-start.1 = (bf16[1024,256]{1,0:T(8,128)(2,1)S(1)}, bf16[1024,256]{1,0:T(8,128)(2,1)}, u32[]{:S(2)}) copy-start(bf16[1024,256]{1,0:T(8,128)(2,1)} %down_ref.1) | copy-start | bytes 1572868
  29.3 1.2 %copy-start.2 = (f32[256]{0:T(256)S(1)}, f32[256]{0:T(256)}, u32[]{:S(2)}) copy-start(f32[256]{0:T(256)} %param.21) | copy-start | bytes 3076
  30.5 52.1 %copy-start.3 = (bf16[32,64,256]{2,1,0:T(8,128)(2,1)S(1)}, bf16[32,64,256]{2,1,0:T(8,128)(2,1)}, u32[]{:S(2)}) copy-start(bf16[32,64,256]{2,1,0:T(8,128)(2,1)} %get-tuple-element.8) | copy-start | bytes 3145732

commit v14 on v13

--- a/solution.py
+++ b/solution.py
@@ -100,7 +100,7 @@
 def exchange_and_ocean(outgoing, state, gain, w_up, w_down):
     n_lon = lax.axis_size("lon")
     n = n_lon * lax.axis_size("lat")
-    group = 16
+    group = 8
     rows = outgoing.shape[0] * outgoing.shape[1] * outgoing.shape[2]
     channels, hid = w_up.shape
     vmem = pl.BlockSpec(memory_space=pltpu.VMEM)

time: 86.2 us -> 88 us (1.021)
  Pallas kernels: 74.3 us -> 76.1 us
    pallas_call x1, Pallas kernels: 52.1 us -> 53.8 us  [exchange_and_ocean(): pl.pallas_call(functools.partial(exchange_body, n_lon, n, group), out_sha...]
where the time goes in v14:
time: 88 us; the launch traced here: 86.6 us
  Pallas kernels  76.1 us (86%)
  local copies, waits for them, and re-layouts  5.87 us (7%)
  other arithmetic  3.24 us (4%)
    pallas_call x1, Pallas kernels, exchange_and_ocean(): pl.pallas_call(functools.partial(exchange_body, n_lon, n, group), out_sha...  53.8 us
    pallas_call x1, Pallas kernels, atmosphere_block(): pl.pallas_call(functools.partial(atmos_body, lax.axis_size('lat'), lax.ax...  22.3 us
    unnamed x12, local copies, waits for them, and re-layouts  3.89 us

profile of v14, /device:TPU:99, one launch (start us, length us, event | category | flops | bytes accessed | tf_op | source)
XLA Modules:
  0.0 86.6 jit_solution(3720706423035967076)
XLA Ops:
  0.6 0.7 convert_element_type.28
  1.4 0.1 convert_element_type.29
  1.4 0.7 fusion.4
  2.2 0.2 reduce_window_sum.11
  2.4 0.8 select_reduce_fusion
  3.2 0.7 add_add_fusion
  3.9 0.1 convert_reduce_fusion
  4.0 0.3 mul.27
  4.3 0.4 copy.14
  4.8 22.3 %shard_map.131 = (bf16[32,64,256]{2,1,0:T(8,128)(2,1)}, bf16[2048,256]{1,0:T(8,128)(2,1)}) custom-call(bf16[32,64,256]{2,1,0:T(8,128)(2,1)} %atm_ref.1, f32[7,7,256]{2,1,0:T(8,128)} %w_ref.1, bf16[32,64,256]{2,1,0:T(8,128)(2,1)} %atm_ref.1, f32[1,256]{1,0:T(1,128)} %bitcast.20, bf16[256,1024]{1,0:T(8,128)(2,1)} %up_hbm.1, bf16[1024,256]{1,0:T(8,128)(2,1)} %down_hbm.1, ...), custom_call_target="tpu_custom_call" | custom-call | flops 2467299328 | bytes 4194304 | tf_op jit(solution)/shard_map/pallas_call | solution.py:285
  27.0 1.6 %reshape.46 = bf16[128,4096]{1,0:T(8,128)(2,1)S(1)} reshape(bf16[2048,256]{1,0:T(8,128)(2,1)} %get-tuple-element.5) | data formatting | bytes 2097152 | tf_op jit(solution)/shard_map/reshape | solution.py:353
  28.6 0.7 fusion
  29.3 0.0 copy-start
  29.3 0.0 copy-start.1
  29.3 0.0 copy-start.2
  29.3 0.6 copy.15
  30.0 0.4 copy-done
  30.3 0.2 copy-done.1
  30.5 0.0 copy-done.2
  30.5 0.0 copy-start.3
  30.5 53.8 %shard_map.132 = bf16[128,2,16,256]{3,2,1,0:T(8,128)(2,1)S(1)} custom-call(bf16[128,2,16,256]{3,2,1,0:T(8,128)(2,1)S(1)} %bitcast.12, bf16[128,2,16,256]{3,2,1,0:T(8,128)(2,1)} %bitcast.19, f32[1,256]{1,0:T(1,128)S(1)} %bitcast.13, bf16[256,1024]{1,0:T(8,128)(2,1)S(1)} %copy-done, bf16[1024,256]{1,0:T(8,128)(2,1)S(1)} %copy-done.1), custom_call_target="tpu_custom_call" | custom-call | flops 4294967296 | bytes 8388608 | tf_op jit(solution)/shard_map/pallas_call | solution.py:107
  84.3 0.0 copy-done.3
  84.3 1.0 %copy.18 = bf16[32,64,256]{2,1,0:T(8,128)(2,1)} copy(bf16[32,64,256]{2,1,0:T(8,128)(2,1)S(1)} %copy-done.3) | data formatting | bytes 2097152
  85.3 1.3 %copy.19 = bf16[1,128,2,16,256]{4,3,2,1,0:T(8,128)(2,1)} copy(bf16[1,128,2,16,256]{4,3,2,1,0:T(8,128)(2,1)S(1)} %bitcast.11) | data formatting | bytes 4194304
  (1 shorter events, 0.0 us)
Async XLA Ops:
  29.3 1.0 %copy-start = (bf16[256,1024]{1,0:T(8,128)(2,1)S(1)}, bf16[256,1024]{1,0:T(8,128)(2,1)}, u32[]{:S(2)}) copy-start(bf16[256,1024]{1,0:T(8,128)(2,1)} %up_ref.1) | copy-start | bytes 1572868
  29.3 1.2 %copy-start.1 = (bf16[1024,256]{1,0:T(8,128)(2,1)S(1)}, bf16[1024,256]{1,0:T(8,128)(2,1)}, u32[]{:S(2)}) copy-start(bf16[1024,256]{1,0:T(8,128)(2,1)} %down_ref.1) | copy-start | bytes 1572868
  29.3 1.2 %copy-start.2 = (f32[256]{0:T(256)S(1)}, f32[256]{0:T(256)}, u32[]{:S(2)}) copy-start(f32[256]{0:T(256)} %param.21) | copy-start | bytes 3076
  30.5 53.8 %copy-start.3 = (bf16[32,64,256]{2,1,0:T(8,128)(2,1)S(1)}, bf16[32,64,256]{2,1,0:T(8,128)(2,1)}, u32[]{:S(2)}) copy-start(bf16[32,64,256]{2,1,0:T(8,128)(2,1)} %get-tuple-element.8) | copy-start | bytes 3145732

commit v15 on v14

--- a/solution.py
+++ b/solution.py
@@ -100,7 +100,7 @@
 def exchange_and_ocean(outgoing, state, gain, w_up, w_down):
     n_lon = lax.axis_size("lon")
     n = n_lon * lax.axis_size("lat")
-    group = 8
+    group = 32
     rows = outgoing.shape[0] * outgoing.shape[1] * outgoing.shape[2]
     channels, hid = w_up.shape
     vmem = pl.BlockSpec(memory_space=pltpu.VMEM)

time: 88 us -> 86.6 us (0.984)
  Pallas kernels: 76.1 us -> 74.6 us
    pallas_call x1, Pallas kernels: 53.8 us -> 52.4 us  [exchange_and_ocean(): pl.pallas_call(functools.partial(exchange_body, n_lon, n, group), out_sha...]
where the time goes in v15:
time: 86.6 us; the launch traced here: 85.2 us
  Pallas kernels  74.6 us (86%)
  local copies, waits for them, and re-layouts  5.87 us (7%)
  other arithmetic  3.24 us (4%)
    pallas_call x1, Pallas kernels, exchange_and_ocean(): pl.pallas_call(functools.partial(exchange_body, n_lon, n, group), out_sha...  52.4 us
    pallas_call x1, Pallas kernels, atmosphere_block(): pl.pallas_call(functools.partial(atmos_body, lax.axis_size('lat'), lax.ax...  22.3 us
    unnamed x12, local copies, waits for them, and re-layouts  3.89 us

profile of v15, /device:TPU:99, one launch (start us, length us, event | category | flops | bytes accessed | tf_op | source)
XLA Modules:
  0.0 85.2 jit_solution(7649404492775357614)
XLA Ops:
  0.6 0.7 convert_element_type.28
  1.4 0.1 convert_element_type.29
  1.4 0.7 fusion.4
  2.2 0.2 reduce_window_sum.11
  2.4 0.8 select_reduce_fusion
  3.2 0.7 add_add_fusion
  3.9 0.1 convert_reduce_fusion
  4.0 0.3 mul.27
  4.3 0.4 copy.14
  4.8 22.3 %shard_map.131 = (bf16[32,64,256]{2,1,0:T(8,128)(2,1)}, bf16[2048,256]{1,0:T(8,128)(2,1)}) custom-call(bf16[32,64,256]{2,1,0:T(8,128)(2,1)} %atm_ref.1, f32[7,7,256]{2,1,0:T(8,128)} %w_ref.1, bf16[32,64,256]{2,1,0:T(8,128)(2,1)} %atm_ref.1, f32[1,256]{1,0:T(1,128)} %bitcast.20, bf16[256,1024]{1,0:T(8,128)(2,1)} %up_hbm.1, bf16[1024,256]{1,0:T(8,128)(2,1)} %down_hbm.1, ...), custom_call_target="tpu_custom_call" | custom-call | flops 2467299328 | bytes 4194304 | tf_op jit(solution)/shard_map/pallas_call | solution.py:285
  27.0 1.6 %reshape.46 = bf16[128,4096]{1,0:T(8,128)(2,1)S(1)} reshape(bf16[2048,256]{1,0:T(8,128)(2,1)} %get-tuple-element.5) | data formatting | bytes 2097152 | tf_op jit(solution)/shard_map/reshape | solution.py:353
  28.6 0.7 fusion
  29.3 0.0 copy-start
  29.3 0.0 copy-start.1
  29.3 0.0 copy-start.2
  29.3 0.6 copy.15
  30.0 0.4 copy-done
  30.3 0.2 copy-done.1
  30.5 0.0 copy-done.2
  30.5 0.0 copy-start.3
  30.5 52.4 %shard_map.132 = bf16[128,2,16,256]{3,2,1,0:T(8,128)(2,1)S(1)} custom-call(bf16[128,2,16,256]{3,2,1,0:T(8,128)(2,1)S(1)} %bitcast.12, bf16[128,2,16,256]{3,2,1,0:T(8,128)(2,1)} %bitcast.19, f32[1,256]{1,0:T(1,128)S(1)} %bitcast.13, bf16[256,1024]{1,0:T(8,128)(2,1)S(1)} %copy-done, bf16[1024,256]{1,0:T(8,128)(2,1)S(1)} %copy-done.1), custom_call_target="tpu_custom_call" | custom-call | flops 4294967296 | bytes 8388608 | tf_op jit(solution)/shard_map/pallas_call | solution.py:107
  82.9 0.0 copy-done.3
  82.9 1.0 %copy.18 = bf16[32,64,256]{2,1,0:T(8,128)(2,1)} copy(bf16[32,64,256]{2,1,0:T(8,128)(2,1)S(1)} %copy-done.3) | data formatting | bytes 2097152
  83.9 1.3 %copy.19 = bf16[1,128,2,16,256]{4,3,2,1,0:T(8,128)(2,1)} copy(bf16[1,128,2,16,256]{4,3,2,1,0:T(8,128)(2,1)S(1)} %bitcast.11) | data formatting | bytes 4194304
  (1 shorter events, 0.0 us)
Async XLA Ops:
  29.3 1.0 %copy-start = (bf16[256,1024]{1,0:T(8,128)(2,1)S(1)}, bf16[256,1024]{1,0:T(8,128)(2,1)}, u32[]{:S(2)}) copy-start(bf16[256,1024]{1,0:T(8,128)(2,1)} %up_ref.1) | copy-start | bytes 1572868
  29.3 1.2 %copy-start.1 = (bf16[1024,256]{1,0:T(8,128)(2,1)S(1)}, bf16[1024,256]{1,0:T(8,128)(2,1)}, u32[]{:S(2)}) copy-start(bf16[1024,256]{1,0:T(8,128)(2,1)} %down_ref.1) | copy-start | bytes 1572868
  29.3 1.2 %copy-start.2 = (f32[256]{0:T(256)S(1)}, f32[256]{0:T(256)}, u32[]{:S(2)}) copy-start(f32[256]{0:T(256)} %param.21) | copy-start | bytes 3076
  30.5 52.4 %copy-start.3 = (bf16[32,64,256]{2,1,0:T(8,128)(2,1)S(1)}, bf16[32,64,256]{2,1,0:T(8,128)(2,1)}, u32[]{:S(2)}) copy-start(bf16[32,64,256]{2,1,0:T(8,128)(2,1)} %get-tuple-element.8) | copy-start | bytes 3145732

commit v16 on v13

--- a/solution.py
+++ b/solution.py
@@ -15,8 +15,8 @@
 HALO_MOVES = ((1, 0), (-1, 0), (0, 1), (0, -1), (1, 1), (1, -1), (-1, 1), (-1, -1))
 
 
-def exchange_body(n_lon, n, group, out_ref, state_ref, gain_ref, up_ref, down_ref,
-                  res_ref, recv_ref, stage_ref, send_sems, recv_sems):
+def exchange_body(n_lon, n, group, flux_ref, wet_ref, tile_ref, used_ref, state_ref, gain_ref, up_ref, down_ref,
+                  res_ref, out_ref, recv_ref, stage_ref, send_sems, recv_sems):
     me = lax.axis_index("lat") * n_lon + lax.axis_index("lon")
 
     def coords(d):
@@ -27,6 +27,17 @@
     @pl.loop(1, n)
     def _(j):
         pl.semaphore_signal(barrier, inc=1, device_id=coords(lax.rem(me + j, n)), device_id_type=MESH)
+
+    capacity = out_ref.shape[1]
+
+    @pl.loop(0, n * capacity // 8)
+    def _(t8):
+        for u in range(8):
+            t = t8 * 8 + u
+            k = tile_ref[t]
+            cells = (flux_ref[k].astype(jnp.float32) * wet_ref[k].astype(jnp.float32)).astype(jnp.bfloat16)
+            keep = jnp.full(cells.shape, used_ref[t], jnp.int32) > 0
+            out_ref[t // capacity, t % capacity] = jnp.where(keep, cells, jnp.nan).astype(jnp.bfloat16)
 
     pl.semaphore_wait(barrier, n - 1)
 
@@ -97,19 +108,22 @@
         send_copy(j).wait_send()
 
 
-def exchange_and_ocean(outgoing, state, gain, w_up, w_down):
+def exchange_and_ocean(flux_tiles, wet, tile_of_slot, used, state, gain, w_up, w_down):
     n_lon = lax.axis_size("lon")
     n = n_lon * lax.axis_size("lat")
     group = 16
+    outgoing = jax.ShapeDtypeStruct(state.shape, state.dtype)
     rows = outgoing.shape[0] * outgoing.shape[1] * outgoing.shape[2]
     channels, hid = w_up.shape
     vmem = pl.BlockSpec(memory_space=pltpu.VMEM)
+    smem = pl.BlockSpec(memory_space=pltpu.SMEM)
     return pl.pallas_call(
         functools.partial(exchange_body, n_lon, n, group),
         out_shape=jax.ShapeDtypeStruct(outgoing.shape, outgoing.dtype),
-        in_specs=[vmem] * 5,
+        in_specs=[vmem, vmem, smem, smem] + [vmem] * 4,
         out_specs=vmem,
         scratch_shapes=[
+            pltpu.VMEM(outgoing.shape, outgoing.dtype),
             pltpu.VMEM(outgoing.shape, outgoing.dtype),
             pltpu.VMEM((group,) + outgoing.shape[1:], outgoing.dtype),
             pltpu.SemaphoreType.DMA((n,)),
@@ -121,7 +135,7 @@
         cost_estimate=pl.CostEstimate(
             flops=4 * rows * channels * hid, transcendentals=rows * hid, bytes_accessed=4 * rows * channels * 2
         ),
-    )(outgoing, state, gain.reshape(1, channels), w_up, w_down)
+    )(flux_tiles, wet, tile_of_slot, used, state, gain.reshape(1, channels), w_up, w_down)
 
 
 def atmos_body(n_lat, n_lon, kw, band, side, x_hbm, w_ref, atm_ref, gain_ref, up_hbm, down_hbm, fw_hbm,
@@ -350,18 +364,16 @@
     tile_cells = ocean_state.shape[3]
     atmos_new, fluxes = atmosphere_block(conv_weight, atmosphere, atm_gain, atm_up, atm_down, flux_weight)
     wet = land_mask.reshape(tile_count, tile_cells, 1).astype(jnp.bfloat16)
-    flux_tiles = (fluxes.reshape(tile_count, tile_cells, channels) * wet).reshape(tile_count, tile_cells * channels)
-    member = (owners[:, None] == jnp.arange(peer_count, dtype=jnp.int32)[None, :]).astype(jnp.int32)
-    tile_rank = jnp.sum(jnp.cumsum(member, axis=0) * member, axis=1) - 1
-    slot_index = owners * capacity + tile_rank
-    onehot = (
-        jnp.arange(peer_count * capacity, dtype=jnp.int32)[:, None] == slot_index[None, :]
-    ).astype(jnp.bfloat16)
-    outgoing = jnp.dot(onehot, flux_tiles, preferred_element_type=jnp.float32).astype(jnp.bfloat16)
-    used = jnp.sum(onehot.astype(jnp.float32), axis=1) > 0
-    outgoing = jnp.where(used[:, None], outgoing, jnp.nan).astype(jnp.bfloat16)
-    outgoing = outgoing.reshape(peer_count, capacity, tile_cells, channels)
-    ocean_out = exchange_and_ocean(outgoing, ocean_state[0], ocn_gain, ocn_up, ocn_down)[None]
+    flux_tiles = fluxes.reshape(tile_count, tile_cells, channels)
+    order = jnp.arange(tile_count, dtype=jnp.int32)
+    earlier_same = (owners[:, None] == owners[None, :]) & (order[None, :] < order[:, None])
+    slot_index = owners * capacity + jnp.sum(earlier_same.astype(jnp.int32), axis=1)
+    hits = jnp.arange(peer_count * capacity, dtype=jnp.int32)[:, None] == slot_index[None, :]
+    used = jnp.sum(hits.astype(jnp.int32), axis=1)
+    tile_of_slot = jnp.sum(jnp.where(hits, order[None, :], 0), axis=1)
+    ocean_out = exchange_and_ocean(
+        flux_tiles, wet, tile_of_slot, used, ocean_state[0], ocn_gain, ocn_up, ocn_down
+    )[None]
     return (atmos_new, ocean_out)
 
 

time: 86.2 us -> 84.4 us (0.979)
  the two profiles are of different devices: /device:TPU:99 before, /device:TPU:101 now
where the time goes in v16:
time: 84.4 us; the launch traced here: 84.2 us
  Pallas kernels  76.4 us (91%)
  local copies, waits for them, and re-layouts  4.63 us (5%)
  other arithmetic  2.44 us (3%)
    pallas_call x1, Pallas kernels, exchange_and_ocean(): pl.pallas_call(functools.partial(exchange_body, n_lon, n, group), out_sha...  53.2 us
    pallas_call x1, Pallas kernels, atmosphere_block(): pl.pallas_call(functools.partial(atmos_body, lax.axis_size('lat'), lax.ax...  23.2 us
    unnamed x12, local copies, waits for them, and re-layouts  3.53 us

profile of v16, /device:TPU:101, one launch (start us, length us, event | category | flops | bytes accessed | tf_op | source)
XLA Modules:
  0.0 84.2 jit_solution(8806120340795858985)
XLA Ops:
  0.6 0.9 %convert_reduce_fusion.1 = s32[128]{0:T(128)S(1)} fusion(s32[128]{0:T(128)} %bitcast.12), kind=kLoop, calls=%fused_computation.3 | loop fusion | flops 81792 | bytes 1024 | tf_op jit(solution)/shard_map/reduce_sum | solution.py:370
  1.5 0.7 multiply_add_fusion
  2.2 0.2 convert_reduce_fusion
  2.4 0.7 convert_element_type.11
  3.1 1.1 %convert_element_type.15.wet_ref = bf16[128,16,1]{2,1,0:T(8,128)(2,1)S(1)} reshape(bf16[32,64]{1,0:T(8,128)(2,1)S(1)} %convert_element_type.11) | data formatting | bytes 8192 | tf_op jit(solution)/shard_map/convert_element_type | solution.py:366
  4.2 0.0 copy-start
  4.2 0.0 copy-start.1
  4.2 0.0 copy-start.2
  4.2 23.2 %shard_map.131 = (bf16[32,64,256]{2,1,0:T(8,128)(2,1)}, bf16[2048,256]{1,0:T(8,128)(2,1)}) custom-call(bf16[32,64,256]{2,1,0:T(8,128)(2,1)} %atm_ref.1, f32[7,7,256]{2,1,0:T(8,128)} %w_ref.1, bf16[32,64,256]{2,1,0:T(8,128)(2,1)} %atm_ref.1, f32[1,256]{1,0:T(1,128)} %bitcast.11, bf16[256,1024]{1,0:T(8,128)(2,1)} %up_hbm.1, bf16[1024,256]{1,0:T(8,128)(2,1)} %down_hbm.1, ...), custom_call_target="tpu_custom_call" | custom-call | flops 2467299328 | bytes 4194304 | tf_op jit(solution)/shard_map/pallas_call | solution.py:299
  27.4 0.0 copy-done
  27.4 0.0 copy-done.1
  27.4 0.0 copy-done.2
  27.5 0.0 copy-start.3
  27.5 1.2 %copy-done.3 = bf16[2048,256]{1,0:T(8,128)(2,1)S(1)} copy-done((bf16[2048,256]{1,0:T(8,128)(2,1)S(1)}, bf16[2048,256]{1,0:T(8,128)(2,1)}, u32[]{:S(2)}) %copy-start.3) | copy-done | bytes 1048600
  28.7 0.0 copy-start.4
  28.7 53.2 %shard_map.132 = bf16[128,2,16,256]{3,2,1,0:T(8,128)(2,1)S(1)} custom-call(bf16[128,16,256]{2,1,0:T(8,128)(2,1)S(1)} %bitcast.9, bf16[128,16,1]{2,1,0:T(8,128)(2,1)S(1)} %convert_element_type.15.wet_ref, s32[256]{0:T(256)S(1)} %get-tuple-element.7.tile_ref, s32[256]{0:T(256)S(1)} %get-tuple-element.6.used_ref, bf16[128,2,16,256]{3,2,1,0:T(8,128)(2,1)} %bitcast.10, ...), custom_call_target="tpu_custom_call" | custom-call | flops 4294967296 | bytes 8388608 | tf_op jit(solution)/shard_map/pallas_call | solution.py:120
  81.9 0.0 copy-done.4
  81.9 1.0 %copy.18 = bf16[32,64,256]{2,1,0:T(8,128)(2,1)} copy(bf16[32,64,256]{2,1,0:T(8,128)(2,1)S(1)} %copy-done.4) | data formatting | bytes 2097152
  82.8 1.3 %copy.19 = bf16[1,128,2,16,256]{4,3,2,1,0:T(8,128)(2,1)} copy(bf16[1,128,2,16,256]{4,3,2,1,0:T(8,128)(2,1)S(1)} %bitcast.7) | data formatting | bytes 4194304
Async XLA Ops:
  4.2 23.2 %copy-start = (bf16[256,1024]{1,0:T(8,128)(2,1)S(1)}, bf16[256,1024]{1,0:T(8,128)(2,1)}, u32[]{:S(2)}) copy-start(bf16[256,1024]{1,0:T(8,128)(2,1)} %up_ref.1) | copy-start | bytes 1572868
  4.2 23.2 %copy-start.1 = (bf16[1024,256]{1,0:T(8,128)(2,1)S(1)}, bf16[1024,256]{1,0:T(8,128)(2,1)}, u32[]{:S(2)}) copy-start(bf16[1024,256]{1,0:T(8,128)(2,1)} %down_ref.1) | copy-start | bytes 1572868
  4.2 23.2 %copy-start.2 = (f32[256]{0:T(256)S(1)}, f32[256]{0:T(256)}, u32[]{:S(2)}) copy-start(f32[256]{0:T(256)} %param.21) | copy-start | bytes 3076
  27.5 1.2 %copy-start.3 = (bf16[2048,256]{1,0:T(8,128)(2,1)S(1)}, bf16[2048,256]{1,0:T(8,128)(2,1)}, u32[]{:S(2)}) copy-start(bf16[2048,256]{1,0:T(8,128)(2,1)} %get-tuple-element.5) | copy-start | bytes 3145732
  28.7 53.2 %copy-start.4 = (bf16[32,64,256]{2,1,0:T(8,128)(2,1)S(1)}, bf16[32,64,256]{2,1,0:T(8,128)(2,1)}, u32[]{:S(2)}) copy-start(bf16[32,64,256]{2,1,0:T(8,128)(2,1)} %get-tuple-element.10) | copy-start | bytes 3145732

commit v17 on v16

--- a/solution.py
+++ b/solution.py
@@ -15,8 +15,8 @@
 HALO_MOVES = ((1, 0), (-1, 0), (0, 1), (0, -1), (1, 1), (1, -1), (-1, 1), (-1, -1))
 
 
-def exchange_body(n_lon, n, group, flux_ref, wet_ref, tile_ref, used_ref, state_ref, gain_ref, up_ref, down_ref,
-                  res_ref, out_ref, recv_ref, stage_ref, send_sems, recv_sems):
+def exchange_body(n_lon, n, group, flux_ref, wet_ref, tile_ref, used_ref, state_hbm, gain_ref, up_ref, down_ref,
+                  res_ref, out_ref, recv_ref, stage_ref, send_sems, recv_sems, state_ref, state_sem):
     me = lax.axis_index("lat") * n_lon + lax.axis_index("lon")
 
     def coords(d):
@@ -27,6 +27,9 @@
     @pl.loop(1, n)
     def _(j):
         pl.semaphore_signal(barrier, inc=1, device_id=coords(lax.rem(me + j, n)), device_id_type=MESH)
+
+    state_copy = pltpu.make_async_copy(state_hbm, state_ref, state_sem)
+    state_copy.start()
 
     capacity = out_ref.shape[1]
 
@@ -68,6 +71,7 @@
         send_copy(j).start()
 
     recv_ref[0] = out_ref[me]
+    state_copy.wait()
     slots, cells, channels = out_ref.shape[1], out_ref.shape[2], out_ref.shape[3]
     rows = group * slots * cells
 
@@ -120,7 +124,7 @@
     return pl.pallas_call(
         functools.partial(exchange_body, n_lon, n, group),
         out_shape=jax.ShapeDtypeStruct(outgoing.shape, outgoing.dtype),
-        in_specs=[vmem, vmem, smem, smem] + [vmem] * 4,
+        in_specs=[vmem, vmem, smem, smem, pl.BlockSpec(memory_space=pl.ANY)] + [vmem] * 3,
         out_specs=vmem,
         scratch_shapes=[
             pltpu.VMEM(outgoing.shape, outgoing.dtype),
@@ -128,6 +132,8 @@
             pltpu.VMEM((group,) + outgoing.shape[1:], outgoing.dtype),
             pltpu.SemaphoreType.DMA((n,)),
             pltpu.SemaphoreType.DMA((n,)),
+            pltpu.VMEM(outgoing.shape, outgoing.dtype),
+            pltpu.SemaphoreType.DMA(()),
         ],
         compiler_params=pltpu.CompilerParams(
             collective_id=0, has_side_effects=True, vmem_limit_bytes=48 * 1024 * 1024

time: 84.4 us -> 83.2 us (0.986)
  Pallas kernels: 76.4 us -> 75.1 us
    pallas_call x1, Pallas kernels: 53.2 us -> 52 us  [exchange_and_ocean(): pl.pallas_call(functools.partial(exchange_body, n_lon, n, group), out_sha...]
where the time goes in v17:
time: 83.2 us; the launch traced here: 82.9 us
  Pallas kernels  75.1 us (90%)
  local copies, waits for them, and re-layouts  4.63 us (6%)
  other arithmetic  2.44 us (3%)
    pallas_call x1, Pallas kernels, exchange_and_ocean(): pl.pallas_call(functools.partial(exchange_body, n_lon, n, group), out_sha...  52 us
    pallas_call x1, Pallas kernels, atmosphere_block(): pl.pallas_call(functools.partial(atmos_body, lax.axis_size('lat'), lax.ax...  23.2 us
    unnamed x12, local copies, waits for them, and re-layouts  3.53 us

profile of v17, /device:TPU:101, one launch (start us, length us, event | category | flops | bytes accessed | tf_op | source)
XLA Modules:
  0.0 82.9 jit_solution(16276997584991104727)
XLA Ops:
  0.6 0.9 %convert_reduce_fusion.1 = s32[128]{0:T(128)S(1)} fusion(s32[128]{0:T(128)} %bitcast.12), kind=kLoop, calls=%fused_computation.3 | loop fusion | flops 81792 | bytes 1024 | tf_op jit(solution)/shard_map/reduce_sum | solution.py:376
  1.5 0.7 multiply_add_fusion
  2.2 0.2 convert_reduce_fusion
  2.4 0.7 convert_element_type.11
  3.1 1.1 %convert_element_type.15.wet_ref = bf16[128,16,1]{2,1,0:T(8,128)(2,1)S(1)} reshape(bf16[32,64]{1,0:T(8,128)(2,1)S(1)} %convert_element_type.11) | data formatting | bytes 8192 | tf_op jit(solution)/shard_map/convert_element_type | solution.py:372
  4.2 0.0 copy-start
  4.2 0.0 copy-start.1
  4.2 0.0 copy-start.2
  4.2 23.2 %shard_map.131 = (bf16[32,64,256]{2,1,0:T(8,128)(2,1)}, bf16[2048,256]{1,0:T(8,128)(2,1)}) custom-call(bf16[32,64,256]{2,1,0:T(8,128)(2,1)} %atm_ref.1, f32[7,7,256]{2,1,0:T(8,128)} %w_ref.1, bf16[32,64,256]{2,1,0:T(8,128)(2,1)} %atm_ref.1, f32[1,256]{1,0:T(1,128)} %bitcast.11, bf16[256,1024]{1,0:T(8,128)(2,1)} %up_hbm.1, bf16[1024,256]{1,0:T(8,128)(2,1)} %down_hbm.1, ...), custom_call_target="tpu_custom_call" | custom-call | flops 2467299328 | bytes 4194304 | tf_op jit(solution)/shard_map/pallas_call | solution.py:305
  27.4 0.0 copy-done
  27.4 0.0 copy-done.1
  27.4 0.0 copy-done.2
  27.5 0.0 copy-start.3
  27.5 1.2 %copy-done.3 = bf16[2048,256]{1,0:T(8,128)(2,1)S(1)} copy-done((bf16[2048,256]{1,0:T(8,128)(2,1)S(1)}, bf16[2048,256]{1,0:T(8,128)(2,1)}, u32[]{:S(2)}) %copy-start.3) | copy-done | bytes 1048600
  28.7 0.0 copy-start.4
  28.7 52.0 %shard_map.132 = bf16[128,2,16,256]{3,2,1,0:T(8,128)(2,1)S(1)} custom-call(bf16[128,16,256]{2,1,0:T(8,128)(2,1)S(1)} %bitcast.9, bf16[128,16,1]{2,1,0:T(8,128)(2,1)S(1)} %convert_element_type.15.wet_ref, s32[256]{0:T(256)S(1)} %get-tuple-element.7.tile_ref, s32[256]{0:T(256)S(1)} %get-tuple-element.6.used_ref, bf16[128,2,16,256]{3,2,1,0:T(8,128)(2,1)} %bitcast.10, ...), custom_call_target="tpu_custom_call" | custom-call | flops 4294967296 | bytes 8388608 | tf_op jit(solution)/shard_map/pallas_call | solution.py:124
  80.6 0.0 copy-done.4
  80.7 1.0 %copy.18 = bf16[32,64,256]{2,1,0:T(8,128)(2,1)} copy(bf16[32,64,256]{2,1,0:T(8,128)(2,1)S(1)} %copy-done.4) | data formatting | bytes 2097152
  81.6 1.3 %copy.19 = bf16[1,128,2,16,256]{4,3,2,1,0:T(8,128)(2,1)} copy(bf16[1,128,2,16,256]{4,3,2,1,0:T(8,128)(2,1)S(1)} %bitcast.7) | data formatting | bytes 4194304
Async XLA Ops:
  4.2 23.2 %copy-start = (bf16[256,1024]{1,0:T(8,128)(2,1)S(1)}, bf16[256,1024]{1,0:T(8,128)(2,1)}, u32[]{:S(2)}) copy-start(bf16[256,1024]{1,0:T(8,128)(2,1)} %up_ref.1) | copy-start | bytes 1572868
  4.2 23.2 %copy-start.1 = (bf16[1024,256]{1,0:T(8,128)(2,1)S(1)}, bf16[1024,256]{1,0:T(8,128)(2,1)}, u32[]{:S(2)}) copy-start(bf16[1024,256]{1,0:T(8,128)(2,1)} %down_ref.1) | copy-start | bytes 1572868
  4.2 23.2 %copy-start.2 = (f32[256]{0:T(256)S(1)}, f32[256]{0:T(256)}, u32[]{:S(2)}) copy-start(f32[256]{0:T(256)} %param.21) | copy-start | bytes 3076
  27.5 1.2 %copy-start.3 = (bf16[2048,256]{1,0:T(8,128)(2,1)S(1)}, bf16[2048,256]{1,0:T(8,128)(2,1)}, u32[]{:S(2)}) copy-start(bf16[2048,256]{1,0:T(8,128)(2,1)} %get-tuple-element.5) | copy-start | bytes 3145732
  28.7 52.0 %copy-start.4 = (bf16[32,64,256]{2,1,0:T(8,128)(2,1)S(1)}, bf16[32,64,256]{2,1,0:T(8,128)(2,1)}, u32[]{:S(2)}) copy-start(bf16[32,64,256]{2,1,0:T(8,128)(2,1)} %get-tuple-element.10) | copy-start | bytes 3145732

commit v18 on v17

--- a/solution.py
+++ b/solution.py
@@ -15,7 +15,7 @@
 HALO_MOVES = ((1, 0), (-1, 0), (0, 1), (0, -1), (1, 1), (1, -1), (-1, 1), (-1, -1))
 
 
-def exchange_body(n_lon, n, group, flux_ref, wet_ref, tile_ref, used_ref, state_hbm, gain_ref, up_ref, down_ref,
+def exchange_body(n_lon, n, group, flux_ref, tile_ref, used_ref, state_hbm, gain_ref, up_ref, down_ref,
                   res_ref, out_ref, recv_ref, stage_ref, send_sems, recv_sems, state_ref, state_sem):
     me = lax.axis_index("lat") * n_lon + lax.axis_index("lon")
 
@@ -38,7 +38,7 @@
         for u in range(8):
             t = t8 * 8 + u
             k = tile_ref[t]
-            cells = (flux_ref[k].astype(jnp.float32) * wet_ref[k].astype(jnp.float32)).astype(jnp.bfloat16)
+            cells = flux_ref[k]
             keep = jnp.full(cells.shape, used_ref[t], jnp.int32) > 0
             out_ref[t // capacity, t % capacity] = jnp.where(keep, cells, jnp.nan).astype(jnp.bfloat16)
 
@@ -112,7 +112,7 @@
         send_copy(j).wait_send()
 
 
-def exchange_and_ocean(flux_tiles, wet, tile_of_slot, used, state, gain, w_up, w_down):
+def exchange_and_ocean(flux_tiles, tile_of_slot, used, state, gain, w_up, w_down):
     n_lon = lax.axis_size("lon")
     n = n_lon * lax.axis_size("lat")
     group = 16
@@ -124,7 +124,7 @@
     return pl.pallas_call(
         functools.partial(exchange_body, n_lon, n, group),
         out_shape=jax.ShapeDtypeStruct(outgoing.shape, outgoing.dtype),
-        in_specs=[vmem, vmem, smem, smem, pl.BlockSpec(memory_space=pl.ANY)] + [vmem] * 3,
+        in_specs=[vmem, smem, smem, pl.BlockSpec(memory_space=pl.ANY)] + [vmem] * 3,
         out_specs=vmem,
         scratch_shapes=[
             pltpu.VMEM(outgoing.shape, outgoing.dtype),
@@ -141,12 +141,12 @@
         cost_estimate=pl.CostEstimate(
             flops=4 * rows * channels * hid, transcendentals=rows * hid, bytes_accessed=4 * rows * channels * 2
         ),
-    )(flux_tiles, wet, tile_of_slot, used, state, gain.reshape(1, channels), w_up, w_down)
-
-
-def atmos_body(n_lat, n_lon, kw, band, side, x_hbm, w_ref, atm_ref, gain_ref, up_hbm, down_hbm, fw_hbm,
+    )(flux_tiles, tile_of_slot, used, state, gain.reshape(1, channels), w_up, w_down)
+
+
+def atmos_body(n_lat, n_lon, kw, band, side, x_hbm, w_ref, atm_ref, gain_ref, up_hbm, down_hbm, fw_hbm, land_ref,
                out_ref, flux_ref, above, below, left, right, above_left, above_right, below_left, below_right,
-               xf_ref, xs_ref, mixed_ref, up_ref, down_ref, fw_ref, sems, send_sems, recv_sems):
+               xf_ref, xs_ref, mixed_ref, up_ref, down_ref, fw_ref, sems, send_sems, recv_sems, wet_ref):
     rows, cols, channels = atm_ref.shape
     m = kw // 2
     got = (above, below, left, right, above_left, above_right, below_left, below_right)
@@ -268,6 +268,14 @@
         @pl.when(exists(d_lat))
         def _():
             halo_copy(p).wait_send()
+
+    eye = (lax.broadcasted_iota(jnp.int32, (cols, cols), 0) == lax.broadcasted_iota(jnp.int32, (cols, cols), 1))
+    land_t = lax.dot_general(
+        eye.astype(jnp.bfloat16), land_ref[...].astype(jnp.bfloat16), (((1,), (1,)), ((), ())),
+        preferred_element_type=jnp.float32,
+    )
+    for r in range(rows):
+        wet_ref[r] = jnp.broadcast_to(land_t[:, r:r + 1], (cols, channels))
 
     chunk = 8
 
@@ -287,10 +295,11 @@
         new = (atmos + branch).astype(jnp.bfloat16)
         out_ref[pl.ds(k * chunk, chunk)] = new.reshape(chunk, cols, channels)
         flux = jnp.dot(new, fw_ref[...], preferred_element_type=jnp.float32)
+        flux = flux * wet_ref[pl.ds(k * chunk, chunk)].reshape(cells, channels)
         flux_ref[pl.ds(k * cells, cells)] = flux.astype(jnp.bfloat16)
 
 
-def atmosphere_block(conv_weight, atmosphere, gain, w_up, w_down, flux_weight):
+def atmosphere_block(conv_weight, atmosphere, gain, w_up, w_down, flux_weight, land_mask):
     rows, cols, channels = atmosphere.shape
     kw = conv_weight.shape[0]
     m = kw // 2
@@ -308,7 +317,7 @@
             jax.ShapeDtypeStruct(atmosphere.shape, atmosphere.dtype),
             jax.ShapeDtypeStruct((cells, channels), jnp.bfloat16),
         ),
-        in_specs=[hbm] + [vmem] * 3 + [hbm] * 3,
+        in_specs=[hbm] + [vmem] * 3 + [hbm] * 3 + [vmem],
         out_specs=(vmem, vmem),
         scratch_shapes=pieces + [
             pltpu.VMEM((rows + kw - 1, cols + 2 * side, channels), jnp.float32),
@@ -320,6 +329,7 @@
             pltpu.SemaphoreType.DMA((3,)),
             pltpu.SemaphoreType.DMA((8,)),
             pltpu.SemaphoreType.DMA((8,)),
+            pltpu.VMEM((rows, cols, channels), jnp.float32),
         ],
         compiler_params=pltpu.CompilerParams(
             collective_id=1, has_side_effects=True, vmem_limit_bytes=56 * 1024 * 1024
@@ -329,7 +339,7 @@
             transcendentals=cells * hid,
             bytes_accessed=cells * channels * 8,
         ),
-    )(atmosphere, conv_weight, atmosphere, gain.reshape(1, channels), w_up, w_down, flux_weight)
+    )(atmosphere, conv_weight, atmosphere, gain.reshape(1, channels), w_up, w_down, flux_weight, land_mask)
 
 
 def normalize(values, scales):
@@ -368,8 +378,9 @@
     peer_count = ocean_state.shape[1]
     capacity = ocean_state.shape[2]
     tile_cells = ocean_state.shape[3]
-    atmos_new, fluxes = atmosphere_block(conv_weight, atmosphere, atm_gain, atm_up, atm_down, flux_weight)
-    wet = land_mask.reshape(tile_count, tile_cells, 1).astype(jnp.bfloat16)
+    atmos_new, fluxes = atmosphere_block(
+        conv_weight, atmosphere, atm_gain, atm_up, atm_down, flux_weight, land_mask
+    )
     flux_tiles = fluxes.reshape(tile_count, tile_cells, channels)
     order = jnp.arange(tile_count, dtype=jnp.int32)
     earlier_same = (owners[:, None] == owners[None, :]) & (order[None, :] < order[:, None])
@@ -378,7 +389,7 @@
     used = jnp.sum(hits.astype(jnp.int32), axis=1)
     tile_of_slot = jnp.sum(jnp.where(hits, order[None, :], 0), axis=1)
     ocean_out = exchange_and_ocean(
-        flux_tiles, wet, tile_of_slot, used, ocean_state[0], ocn_gain, ocn_up, ocn_down
+        flux_tiles, tile_of_slot, used, ocean_state[0], ocn_gain, ocn_up, ocn_down
     )[None]
     return (atmos_new, ocean_out)
 

time: 83.2 us -> 81.4 us (0.978)
  the two profiles are of different devices: /device:TPU:101 before, /device:TPU:99 now
where the time goes in v18:
time: 81.4 us; the launch traced here: 80.1 us
  Pallas kernels  74.2 us (91%)
  local copies, waits for them, and re-layouts  3.53 us (4%)
  other arithmetic  1.72 us (2%)
    pallas_call x1, Pallas kernels, exchange_and_ocean(): pl.pallas_call(functools.partial(exchange_body, n_lon, n, group), out_sha...  51.3 us
    pallas_call x1, Pallas kernels, atmosphere_block(): pl.pallas_call(functools.partial(atmos_body, lax.axis_size('lat'), lax.ax...  22.8 us
    unnamed x12, local copies, waits for them, and re-layouts  3.53 us

profile of v18, /device:TPU:99, one launch (start us, length us, event | category | flops | bytes accessed | tf_op | source)
XLA Modules:
  0.0 80.1 jit_solution(1304840764202311193)
XLA Ops:
  0.6 0.9 %convert_reduce_fusion.1 = s32[128]{0:T(128)S(1)} fusion(s32[128]{0:T(128)} %bitcast.12), kind=kLoop, calls=%fused_computation.3 | loop fusion | flops 81792 | bytes 1024 | tf_op jit(solution)/shard_map/reduce_sum | solution.py:387
  1.5 0.7 multiply_add_fusion
  2.2 0.2 convert_reduce_fusion
  2.4 0.0 copy-start
  2.4 0.0 copy-start.1
  2.4 0.0 copy-start.2
  2.4 22.8 %shard_map.131 = (bf16[32,64,256]{2,1,0:T(8,128)(2,1)}, bf16[2048,256]{1,0:T(8,128)(2,1)}) custom-call(bf16[32,64,256]{2,1,0:T(8,128)(2,1)} %atm_ref.1, f32[7,7,256]{2,1,0:T(8,128)} %w_ref.1, bf16[32,64,256]{2,1,0:T(8,128)(2,1)} %atm_ref.1, f32[1,256]{1,0:T(1,128)} %bitcast.11, bf16[256,1024]{1,0:T(8,128)(2,1)} %up_hbm.1, bf16[1024,256]{1,0:T(8,128)(2,1)} %down_hbm.1, ...), custom_call_target="tpu_custom_call" | custom-call | flops 2467299328 | bytes 4194304 | tf_op jit(solution)/shard_map/pallas_call | solution.py:314
  25.2 0.0 copy-done
  25.3 0.0 copy-done.1
  25.3 0.0 copy-done.2
  25.3 0.0 copy-start.3
  25.3 1.2 %copy-done.3 = bf16[2048,256]{1,0:T(8,128)(2,1)S(1)} copy-done((bf16[2048,256]{1,0:T(8,128)(2,1)S(1)}, bf16[2048,256]{1,0:T(8,128)(2,1)}, u32[]{:S(2)}) %copy-start.3) | copy-done | bytes 1048600
  26.5 0.0 copy-start.4
  26.5 51.3 %shard_map.132 = bf16[128,2,16,256]{3,2,1,0:T(8,128)(2,1)S(1)} custom-call(bf16[128,16,256]{2,1,0:T(8,128)(2,1)S(1)} %bitcast.9, s32[256]{0:T(256)S(1)} %get-tuple-element.7.tile_ref, s32[256]{0:T(256)S(1)} %get-tuple-element.6.used_ref, bf16[128,2,16,256]{3,2,1,0:T(8,128)(2,1)} %bitcast.10, f32[1,256]{1,0:T(1,128)S(1)} %bitcast.8, ...), custom_call_target="tpu_custom_call" | custom-call | flops 4294967296 | bytes 8388608 | tf_op jit(solution)/shard_map/pallas_call | solution.py:124
  77.8 0.0 copy-done.4
  77.8 1.0 %copy.16 = bf16[32,64,256]{2,1,0:T(8,128)(2,1)} copy(bf16[32,64,256]{2,1,0:T(8,128)(2,1)S(1)} %copy-done.4) | data formatting | bytes 2097152
  78.8 1.3 %copy.17 = bf16[1,128,2,16,256]{4,3,2,1,0:T(8,128)(2,1)} copy(bf16[1,128,2,16,256]{4,3,2,1,0:T(8,128)(2,1)S(1)} %bitcast.7) | data formatting | bytes 4194304
Async XLA Ops:
  2.4 22.9 %copy-start = (bf16[256,1024]{1,0:T(8,128)(2,1)S(1)}, bf16[256,1024]{1,0:T(8,128)(2,1)}, u32[]{:S(2)}) copy-start(bf16[256,1024]{1,0:T(8,128)(2,1)} %up_ref.1) | copy-start | bytes 1572868
  2.4 22.9 %copy-start.1 = (bf16[1024,256]{1,0:T(8,128)(2,1)S(1)}, bf16[1024,256]{1,0:T(8,128)(2,1)}, u32[]{:S(2)}) copy-start(bf16[1024,256]{1,0:T(8,128)(2,1)} %down_ref.1) | copy-start | bytes 1572868
  2.4 22.9 %copy-start.2 = (f32[256]{0:T(256)S(1)}, f32[256]{0:T(256)}, u32[]{:S(2)}) copy-start(f32[256]{0:T(256)} %param.21) | copy-start | bytes 3076
  25.3 1.2 %copy-start.3 = (bf16[2048,256]{1,0:T(8,128)(2,1)S(1)}, bf16[2048,256]{1,0:T(8,128)(2,1)}, u32[]{:S(2)}) copy-start(bf16[2048,256]{1,0:T(8,128)(2,1)} %get-tuple-element.5) | copy-start | bytes 3145732
  26.5 51.3 %copy-start.4 = (bf16[32,64,256]{2,1,0:T(8,128)(2,1)S(1)}, bf16[32,64,256]{2,1,0:T(8,128)(2,1)}, u32[]{:S(2)}) copy-start(bf16[32,64,256]{2,1,0:T(8,128)(2,1)} %get-tuple-element.10) | copy-start | bytes 3145732

commit v19 on v18

--- a/solution.py
+++ b/solution.py
@@ -15,9 +15,12 @@
 HALO_MOVES = ((1, 0), (-1, 0), (0, 1), (0, -1), (1, 1), (1, -1), (-1, 1), (-1, -1))
 
 
-def exchange_body(n_lon, n, group, flux_ref, tile_ref, used_ref, state_hbm, gain_ref, up_ref, down_ref,
-                  res_ref, out_ref, recv_ref, stage_ref, send_sems, recv_sems, state_ref, state_sem):
+def exchange_body(n_lon, n, group, flux_hbm, tile_ref, used_ref, state_hbm, gain_ref, up_ref, down_ref,
+                  res_ref, out_ref, recv_ref, stage_ref, send_sems, recv_sems, state_ref, state_sem,
+                  flux_ref, flux_sem):
     me = lax.axis_index("lat") * n_lon + lax.axis_index("lon")
+    flux_copy = pltpu.make_async_copy(flux_hbm, flux_ref, flux_sem)
+    flux_copy.start()
 
     def coords(d):
         return (lax.rem(d, n_lon), lax.div(d, n_lon))
@@ -32,6 +35,7 @@
     state_copy.start()
 
     capacity = out_ref.shape[1]
+    flux_copy.wait()
 
     @pl.loop(0, n * capacity // 8)
     def _(t8):
@@ -124,7 +128,7 @@
     return pl.pallas_call(
         functools.partial(exchange_body, n_lon, n, group),
         out_shape=jax.ShapeDtypeStruct(outgoing.shape, outgoing.dtype),
-        in_specs=[vmem, smem, smem, pl.BlockSpec(memory_space=pl.ANY)] + [vmem] * 3,
+        in_specs=[pl.BlockSpec(memory_space=pl.ANY), smem, smem, pl.BlockSpec(memory_space=pl.ANY)] + [vmem] * 3,
         out_specs=vmem,
         scratch_shapes=[
             pltpu.VMEM(outgoing.shape, outgoing.dtype),
@@ -133,6 +137,8 @@
             pltpu.SemaphoreType.DMA((n,)),
             pltpu.SemaphoreType.DMA((n,)),
             pltpu.VMEM(outgoing.shape, outgoing.dtype),
+            pltpu.SemaphoreType.DMA(()),
+            pltpu.VMEM(flux_tiles.shape, flux_tiles.dtype),
             pltpu.SemaphoreType.DMA(()),
         ],
         compiler_params=pltpu.CompilerParams(

time: 81.4 us -> 81.4 us (level)
  no operation moved by 1% of the time
where the time goes in v19:
time: 81.4 us; the launch traced here: 80.2 us
  Pallas kernels  74.2 us (91%)
  local copies, waits for them, and re-layouts  3.53 us (4%)
  other arithmetic  1.72 us (2%)
    pallas_call x1, Pallas kernels, exchange_and_ocean(): pl.pallas_call(functools.partial(exchange_body, n_lon, n, group), out_sha...  51.4 us
    pallas_call x1, Pallas kernels, atmosphere_block(): pl.pallas_call(functools.partial(atmos_body, lax.axis_size('lat'), lax.ax...  22.8 us
    unnamed x12, local copies, waits for them, and re-layouts  3.53 us

profile of v19, /device:TPU:99, one launch (start us, length us, event | category | flops | bytes accessed | tf_op | source)
XLA Modules:
  0.0 80.2 jit_solution(4314114471017067423)
XLA Ops:
  0.6 0.9 %convert_reduce_fusion.1 = s32[128]{0:T(128)S(1)} fusion(s32[128]{0:T(128)} %bitcast.12), kind=kLoop, calls=%fused_computation.3 | loop fusion | flops 81792 | bytes 1024 | tf_op jit(solution)/shard_map/reduce_sum | solution.py:393
  1.5 0.7 multiply_add_fusion
  2.2 0.2 convert_reduce_fusion
  2.4 0.0 copy-start
  2.4 0.0 copy-start.1
  2.4 0.0 copy-start.2
  2.4 22.8 %shard_map.131 = (bf16[32,64,256]{2,1,0:T(8,128)(2,1)}, bf16[2048,256]{1,0:T(8,128)(2,1)}) custom-call(bf16[32,64,256]{2,1,0:T(8,128)(2,1)} %atm_ref.1, f32[7,7,256]{2,1,0:T(8,128)} %w_ref.1, bf16[32,64,256]{2,1,0:T(8,128)(2,1)} %atm_ref.1, f32[1,256]{1,0:T(1,128)} %bitcast.11, bf16[256,1024]{1,0:T(8,128)(2,1)} %up_hbm.1, bf16[1024,256]{1,0:T(8,128)(2,1)} %down_hbm.1, ...), custom_call_target="tpu_custom_call" | custom-call | flops 2467299328 | bytes 4194304 | tf_op jit(solution)/shard_map/pallas_call | solution.py:320
  25.2 0.0 copy-done
  25.3 0.0 copy-done.1
  25.3 0.0 copy-done.2
  25.3 0.0 copy-start.3
  25.3 1.2 %copy-done.3 = bf16[2048,256]{1,0:T(8,128)(2,1)S(1)} copy-done((bf16[2048,256]{1,0:T(8,128)(2,1)S(1)}, bf16[2048,256]{1,0:T(8,128)(2,1)}, u32[]{:S(2)}) %copy-start.3) | copy-done | bytes 1048600
  26.5 0.0 copy-start.4
  26.5 51.4 %shard_map.132 = bf16[128,2,16,256]{3,2,1,0:T(8,128)(2,1)S(1)} custom-call(bf16[128,16,256]{2,1,0:T(8,128)(2,1)S(1)} %bitcast.9, s32[256]{0:T(256)S(1)} %get-tuple-element.7.tile_ref, s32[256]{0:T(256)S(1)} %get-tuple-element.6.used_ref, bf16[128,2,16,256]{3,2,1,0:T(8,128)(2,1)} %bitcast.10, f32[1,256]{1,0:T(1,128)S(1)} %bitcast.8, ...), custom_call_target="tpu_custom_call" | custom-call | flops 4294967296 | bytes 8388608 | tf_op jit(solution)/shard_map/pallas_call | solution.py:128
  77.9 0.0 copy-done.4
  77.9 1.0 %copy.16 = bf16[32,64,256]{2,1,0:T(8,128)(2,1)} copy(bf16[32,64,256]{2,1,0:T(8,128)(2,1)S(1)} %copy-done.4) | data formatting | bytes 2097152
  78.9 1.3 %copy.17 = bf16[1,128,2,16,256]{4,3,2,1,0:T(8,128)(2,1)} copy(bf16[1,128,2,16,256]{4,3,2,1,0:T(8,128)(2,1)S(1)} %bitcast.7) | data formatting | bytes 4194304
Async XLA Ops:
  2.4 22.9 %copy-start = (bf16[256,1024]{1,0:T(8,128)(2,1)S(1)}, bf16[256,1024]{1,0:T(8,128)(2,1)}, u32[]{:S(2)}) copy-start(bf16[256,1024]{1,0:T(8,128)(2,1)} %up_ref.1) | copy-start | bytes 1572868
  2.4 22.9 %copy-start.1 = (bf16[1024,256]{1,0:T(8,128)(2,1)S(1)}, bf16[1024,256]{1,0:T(8,128)(2,1)}, u32[]{:S(2)}) copy-start(bf16[1024,256]{1,0:T(8,128)(2,1)} %down_ref.1) | copy-start | bytes 1572868
  2.4 22.9 %copy-start.2 = (f32[256]{0:T(256)S(1)}, f32[256]{0:T(256)}, u32[]{:S(2)}) copy-start(f32[256]{0:T(256)} %param.21) | copy-start | bytes 3076
  25.3 1.2 %copy-start.3 = (bf16[2048,256]{1,0:T(8,128)(2,1)S(1)}, bf16[2048,256]{1,0:T(8,128)(2,1)}, u32[]{:S(2)}) copy-start(bf16[2048,256]{1,0:T(8,128)(2,1)} %get-tuple-element.5) | copy-start | bytes 3145732
  26.5 51.4 %copy-start.4 = (bf16[32,64,256]{2,1,0:T(8,128)(2,1)S(1)}, bf16[32,64,256]{2,1,0:T(8,128)(2,1)}, u32[]{:S(2)}) copy-start(bf16[32,64,256]{2,1,0:T(8,128)(2,1)} %get-tuple-element.10) | copy-start | bytes 3145732

commit v20 on v18

--- a/solution.py
+++ b/solution.py
@@ -383,11 +383,15 @@
     )
     flux_tiles = fluxes.reshape(tile_count, tile_cells, channels)
     order = jnp.arange(tile_count, dtype=jnp.int32)
-    earlier_same = (owners[:, None] == owners[None, :]) & (order[None, :] < order[:, None])
-    slot_index = owners * capacity + jnp.sum(earlier_same.astype(jnp.int32), axis=1)
-    hits = jnp.arange(peer_count * capacity, dtype=jnp.int32)[:, None] == slot_index[None, :]
-    used = jnp.sum(hits.astype(jnp.int32), axis=1)
-    tile_of_slot = jnp.sum(jnp.where(hits, order[None, :], 0), axis=1)
+    assert capacity == 2
+    mine = jnp.arange(peer_count, dtype=jnp.int32)[:, None] == owners[None, :]
+    count = jnp.sum(mine.astype(jnp.int32), axis=1)
+    first = jnp.min(jnp.where(mine, order[None, :], tile_count), axis=1)
+    last = jnp.max(jnp.where(mine, order[None, :], -1), axis=1)
+    used = jnp.stack([(count >= 1).astype(jnp.int32), (count >= 2).astype(jnp.int32)], axis=1).reshape(-1)
+    tile_of_slot = jnp.stack(
+        [jnp.where(count >= 1, first, 0), jnp.where(count >= 2, last, 0)], axis=1
+    ).reshape(-1)
     ocean_out = exchange_and_ocean(
         flux_tiles, tile_of_slot, used, ocean_state[0], ocn_gain, ocn_up, ocn_down
     )[None]

time: 81.4 us -> 80.9 us (level)
  other arithmetic: 1.72 us -> 0.83 us
    reduce_sum x2 -> x0, other arithmetic: 1.05 us -> none  [the longest x1 0.9 us: per_device(): jnp.sum(earlier_same.astype(jnp.int32), axis=1)]
where the time goes in v20:
time: 80.9 us; the launch traced here: 79.7 us
  Pallas kernels  74.1 us (92%)
  local copies, waits for them, and re-layouts  4.04 us (5%)
  other arithmetic  0.83 us (1%)
    pallas_call x1, Pallas kernels, exchange_and_ocean(): pl.pallas_call(functools.partial(exchange_body, n_lon, n, group), out_sha...  51.2 us
    pallas_call x1, Pallas kernels, atmosphere_block(): pl.pallas_call(functools.partial(atmos_body, lax.axis_size('lat'), lax.ax...  22.8 us
    unnamed x12, local copies, waits for them, and re-layouts  3.53 us

profile of v20, /device:TPU:99, one launch (start us, length us, event | category | flops | bytes accessed | tf_op | source)
XLA Modules:
  0.0 79.7 jit_solution(8756920141426090618)
XLA Ops:
  0.6 0.8 %select_reduce_fusion.1 = (s32[128]{0:T(128)S(1)}, s32[128]{0:T(128)S(1)}, s32[128]{0:T(128)S(1)}) fusion(s32[128]{0:T(128)} %bitcast.17), kind=kLoop, calls=%fused_computation.1 | loop fusion | flops 114304 | bytes 2048 | tf_op jit(solution)/shard_map/reduce_min | solution.py:389
  1.5 0.1 copy.17
  1.6 0.1 reshape.83.used_ref
  1.7 0.1 copy.16
  1.9 0.1 reshape.78.tile_ref
  2.0 0.0 copy-start
  2.0 0.0 copy-start.1
  2.0 0.0 copy-start.2
  2.0 22.8 %shard_map.131 = (bf16[32,64,256]{2,1,0:T(8,128)(2,1)}, bf16[2048,256]{1,0:T(8,128)(2,1)}) custom-call(bf16[32,64,256]{2,1,0:T(8,128)(2,1)} %atm_ref.1, f32[7,7,256]{2,1,0:T(8,128)} %w_ref.1, bf16[32,64,256]{2,1,0:T(8,128)(2,1)} %atm_ref.1, f32[1,256]{1,0:T(1,128)} %bitcast.19, bf16[256,1024]{1,0:T(8,128)(2,1)} %up_hbm.1, bf16[1024,256]{1,0:T(8,128)(2,1)} %down_hbm.1, ...), custom_call_target="tpu_custom_call" | custom-call | flops 2467299328 | bytes 4194304 | tf_op jit(solution)/shard_map/pallas_call | solution.py:314
  24.9 0.0 copy-done
  24.9 0.0 copy-done.1
  24.9 0.0 copy-done.2
  24.9 0.0 copy-start.3
  24.9 1.2 %copy-done.3 = bf16[2048,256]{1,0:T(8,128)(2,1)S(1)} copy-done((bf16[2048,256]{1,0:T(8,128)(2,1)S(1)}, bf16[2048,256]{1,0:T(8,128)(2,1)}, u32[]{:S(2)}) %copy-start.3) | copy-done | bytes 1048600
  26.1 0.0 copy-start.4
  26.1 51.2 %shard_map.132 = bf16[128,2,16,256]{3,2,1,0:T(8,128)(2,1)S(1)} custom-call(bf16[128,16,256]{2,1,0:T(8,128)(2,1)S(1)} %bitcast.16, s32[256]{0:T(256)S(1)} %reshape.78.tile_ref, s32[256]{0:T(256)S(1)} %reshape.83.used_ref, bf16[128,2,16,256]{3,2,1,0:T(8,128)(2,1)} %bitcast.18, f32[1,256]{1,0:T(1,128)S(1)} %bitcast.15, bf16[256,1024]{1,0:T(8,128)(2,1)S(1)} %copy-done, ...), custom_call_target="tpu_custom_call" | custom-call | flops 4294967296 | bytes 8388608 | tf_op jit(solution)/shard_map/pallas_call | solution.py:124
  77.4 0.0 copy-done.4
  77.4 1.0 %copy.20 = bf16[32,64,256]{2,1,0:T(8,128)(2,1)} copy(bf16[32,64,256]{2,1,0:T(8,128)(2,1)S(1)} %copy-done.4) | data formatting | bytes 2097152
  78.3 1.3 %copy.21 = bf16[1,128,2,16,256]{4,3,2,1,0:T(8,128)(2,1)} copy(bf16[1,128,2,16,256]{4,3,2,1,0:T(8,128)(2,1)S(1)} %bitcast.14) | data formatting | bytes 4194304
  (4 shorter events, 0.0 us)
Async XLA Ops:
  2.0 22.9 %copy-start = (bf16[256,1024]{1,0:T(8,128)(2,1)S(1)}, bf16[256,1024]{1,0:T(8,128)(2,1)}, u32[]{:S(2)}) copy-start(bf16[256,1024]{1,0:T(8,128)(2,1)} %up_ref.1) | copy-start | bytes 1572868
  2.0 22.9 %copy-start.1 = (bf16[1024,256]{1,0:T(8,128)(2,1)S(1)}, bf16[1024,256]{1,0:T(8,128)(2,1)}, u32[]{:S(2)}) copy-start(bf16[1024,256]{1,0:T(8,128)(2,1)} %down_ref.1) | copy-start | bytes 1572868
  2.0 22.9 %copy-start.2 = (f32[256]{0:T(256)S(1)}, f32[256]{0:T(256)}, u32[]{:S(2)}) copy-start(f32[256]{0:T(256)} %param.21) | copy-start | bytes 3076
  24.9 1.2 %copy-start.3 = (bf16[2048,256]{1,0:T(8,128)(2,1)S(1)}, bf16[2048,256]{1,0:T(8,128)(2,1)}, u32[]{:S(2)}) copy-start(bf16[2048,256]{1,0:T(8,128)(2,1)} %get-tuple-element.5) | copy-start | bytes 3145732
  26.1 51.2 %copy-start.4 = (bf16[32,64,256]{2,1,0:T(8,128)(2,1)S(1)}, bf16[32,64,256]{2,1,0:T(8,128)(2,1)}, u32[]{:S(2)}) copy-start(bf16[32,64,256]{2,1,0:T(8,128)(2,1)} %get-tuple-element.15) | copy-start | bytes 3145732

commit v21 on v18

--- a/solution.py
+++ b/solution.py
@@ -33,10 +33,10 @@
 
     capacity = out_ref.shape[1]
 
-    @pl.loop(0, n * capacity // 8)
+    @pl.loop(0, n * capacity // 16)
     def _(t8):
-        for u in range(8):
-            t = t8 * 8 + u
+        for u in range(16):
+            t = t8 * 16 + u
             k = tile_ref[t]
             cells = flux_ref[k]
             keep = jnp.full(cells.shape, used_ref[t], jnp.int32) > 0

time: 81.4 us -> 81.4 us (level)
  no operation moved by 1% of the time
where the time goes in v21:
time: 81.4 us; the launch traced here: 80.1 us
  Pallas kernels  74.2 us (91%)
  local copies, waits for them, and re-layouts  3.53 us (4%)
  other arithmetic  1.72 us (2%)
    pallas_call x1, Pallas kernels, exchange_and_ocean(): pl.pallas_call(functools.partial(exchange_body, n_lon, n, group), out_sha...  51.3 us
    pallas_call x1, Pallas kernels, atmosphere_block(): pl.pallas_call(functools.partial(atmos_body, lax.axis_size('lat'), lax.ax...  22.8 us
    unnamed x12, local copies, waits for them, and re-layouts  3.53 us

profile of v21, /device:TPU:99, one launch (start us, length us, event | category | flops | bytes accessed | tf_op | source)
XLA Modules:
  0.0 80.1 jit_solution(7970868136496230841)
XLA Ops:
  0.6 0.9 %convert_reduce_fusion.1 = s32[128]{0:T(128)S(1)} fusion(s32[128]{0:T(128)} %bitcast.12), kind=kLoop, calls=%fused_computation.3 | loop fusion | flops 81792 | bytes 1024 | tf_op jit(solution)/shard_map/reduce_sum | solution.py:387
  1.5 0.7 multiply_add_fusion
  2.2 0.2 convert_reduce_fusion
  2.4 0.0 copy-start
  2.4 0.0 copy-start.1
  2.4 0.0 copy-start.2
  2.4 22.8 %shard_map.131 = (bf16[32,64,256]{2,1,0:T(8,128)(2,1)}, bf16[2048,256]{1,0:T(8,128)(2,1)}) custom-call(bf16[32,64,256]{2,1,0:T(8,128)(2,1)} %atm_ref.1, f32[7,7,256]{2,1,0:T(8,128)} %w_ref.1, bf16[32,64,256]{2,1,0:T(8,128)(2,1)} %atm_ref.1, f32[1,256]{1,0:T(1,128)} %bitcast.11, bf16[256,1024]{1,0:T(8,128)(2,1)} %up_hbm.1, bf16[1024,256]{1,0:T(8,128)(2,1)} %down_hbm.1, ...), custom_call_target="tpu_custom_call" | custom-call | flops 2467299328 | bytes 4194304 | tf_op jit(solution)/shard_map/pallas_call | solution.py:314
  25.2 0.0 copy-done
  25.3 0.0 copy-done.1
  25.3 0.0 copy-done.2
  25.3 0.0 copy-start.3
  25.3 1.2 %copy-done.3 = bf16[2048,256]{1,0:T(8,128)(2,1)S(1)} copy-done((bf16[2048,256]{1,0:T(8,128)(2,1)S(1)}, bf16[2048,256]{1,0:T(8,128)(2,1)}, u32[]{:S(2)}) %copy-start.3) | copy-done | bytes 1048600
  26.5 0.0 copy-start.4
  26.5 51.3 %shard_map.132 = bf16[128,2,16,256]{3,2,1,0:T(8,128)(2,1)S(1)} custom-call(bf16[128,16,256]{2,1,0:T(8,128)(2,1)S(1)} %bitcast.9, s32[256]{0:T(256)S(1)} %get-tuple-element.7.tile_ref, s32[256]{0:T(256)S(1)} %get-tuple-element.6.used_ref, bf16[128,2,16,256]{3,2,1,0:T(8,128)(2,1)} %bitcast.10, f32[1,256]{1,0:T(1,128)S(1)} %bitcast.8, ...), custom_call_target="tpu_custom_call" | custom-call | flops 4294967296 | bytes 8388608 | tf_op jit(solution)/shard_map/pallas_call | solution.py:124
  77.8 0.0 copy-done.4
  77.8 1.0 %copy.16 = bf16[32,64,256]{2,1,0:T(8,128)(2,1)} copy(bf16[32,64,256]{2,1,0:T(8,128)(2,1)S(1)} %copy-done.4) | data formatting | bytes 2097152
  78.8 1.3 %copy.17 = bf16[1,128,2,16,256]{4,3,2,1,0:T(8,128)(2,1)} copy(bf16[1,128,2,16,256]{4,3,2,1,0:T(8,128)(2,1)S(1)} %bitcast.7) | data formatting | bytes 4194304
Async XLA Ops:
  2.4 22.9 %copy-start = (bf16[256,1024]{1,0:T(8,128)(2,1)S(1)}, bf16[256,1024]{1,0:T(8,128)(2,1)}, u32[]{:S(2)}) copy-start(bf16[256,1024]{1,0:T(8,128)(2,1)} %up_ref.1) | copy-start | bytes 1572868
  2.4 22.9 %copy-start.1 = (bf16[1024,256]{1,0:T(8,128)(2,1)S(1)}, bf16[1024,256]{1,0:T(8,128)(2,1)}, u32[]{:S(2)}) copy-start(bf16[1024,256]{1,0:T(8,128)(2,1)} %down_ref.1) | copy-start | bytes 1572868
  2.4 22.9 %copy-start.2 = (f32[256]{0:T(256)S(1)}, f32[256]{0:T(256)}, u32[]{:S(2)}) copy-start(f32[256]{0:T(256)} %param.21) | copy-start | bytes 3076
  25.3 1.2 %copy-start.3 = (bf16[2048,256]{1,0:T(8,128)(2,1)S(1)}, bf16[2048,256]{1,0:T(8,128)(2,1)}, u32[]{:S(2)}) copy-start(bf16[2048,256]{1,0:T(8,128)(2,1)} %get-tuple-element.5) | copy-start | bytes 3145732
  26.5 51.3 %copy-start.4 = (bf16[32,64,256]{2,1,0:T(8,128)(2,1)S(1)}, bf16[32,64,256]{2,1,0:T(8,128)(2,1)}, u32[]{:S(2)}) copy-start(bf16[32,64,256]{2,1,0:T(8,128)(2,1)} %get-tuple-element.10) | copy-start | bytes 3145732

commit v22 on v18

--- a/solution.py
+++ b/solution.py
@@ -277,7 +277,7 @@
     for r in range(rows):
         wet_ref[r] = jnp.broadcast_to(land_t[:, r:r + 1], (cols, channels))
 
-    chunk = 8
+    chunk = 16
 
     @pl.loop(0, rows // chunk)
     def _(k):

time: 81.4 us -> 80.4 us (0.988)
  Pallas kernels: 74.2 us -> 73.2 us
    pallas_call x1, Pallas kernels: 22.8 us -> 21.9 us  [atmosphere_block(): pl.pallas_call(functools.partial(atmos_body, lax.axis_size('lat'), lax.ax...]
where the time goes in v22:
time: 80.4 us; the launch traced here: 79.1 us
  Pallas kernels  73.2 us (91%)
  local copies, waits for them, and re-layouts  3.53 us (4%)
  other arithmetic  1.72 us (2%)
    pallas_call x1, Pallas kernels, exchange_and_ocean(): pl.pallas_call(functools.partial(exchange_body, n_lon, n, group), out_sha...  51.3 us
    pallas_call x1, Pallas kernels, atmosphere_block(): pl.pallas_call(functools.partial(atmos_body, lax.axis_size('lat'), lax.ax...  21.9 us
    unnamed x12, local copies, waits for them, and re-layouts  3.53 us

profile of v22, /device:TPU:99, one launch (start us, length us, event | category | flops | bytes accessed | tf_op | source)
XLA Modules:
  0.0 79.1 jit_solution(15694379985543614694)
XLA Ops:
  0.6 0.9 %convert_reduce_fusion.1 = s32[128]{0:T(128)S(1)} fusion(s32[128]{0:T(128)} %bitcast.12), kind=kLoop, calls=%fused_computation.3 | loop fusion | flops 81792 | bytes 1024 | tf_op jit(solution)/shard_map/reduce_sum | solution.py:387
  1.5 0.7 multiply_add_fusion
  2.2 0.2 convert_reduce_fusion
  2.4 0.0 copy-start
  2.4 0.0 copy-start.1
  2.4 0.0 copy-start.2
  2.4 21.9 %shard_map.131 = (bf16[32,64,256]{2,1,0:T(8,128)(2,1)}, bf16[2048,256]{1,0:T(8,128)(2,1)}) custom-call(bf16[32,64,256]{2,1,0:T(8,128)(2,1)} %atm_ref.1, f32[7,7,256]{2,1,0:T(8,128)} %w_ref.1, bf16[32,64,256]{2,1,0:T(8,128)(2,1)} %atm_ref.1, f32[1,256]{1,0:T(1,128)} %bitcast.11, bf16[256,1024]{1,0:T(8,128)(2,1)} %up_hbm.1, bf16[1024,256]{1,0:T(8,128)(2,1)} %down_hbm.1, ...), custom_call_target="tpu_custom_call" | custom-call | flops 2467299328 | bytes 4194304 | tf_op jit(solution)/shard_map/pallas_call | solution.py:314
  24.3 0.0 copy-done
  24.3 0.0 copy-done.1
  24.3 0.0 copy-done.2
  24.3 0.0 copy-start.3
  24.3 1.2 %copy-done.3 = bf16[2048,256]{1,0:T(8,128)(2,1)S(1)} copy-done((bf16[2048,256]{1,0:T(8,128)(2,1)S(1)}, bf16[2048,256]{1,0:T(8,128)(2,1)}, u32[]{:S(2)}) %copy-start.3) | copy-done | bytes 1048600
  25.5 0.0 copy-start.4
  25.5 51.3 %shard_map.132 = bf16[128,2,16,256]{3,2,1,0:T(8,128)(2,1)S(1)} custom-call(bf16[128,16,256]{2,1,0:T(8,128)(2,1)S(1)} %bitcast.9, s32[256]{0:T(256)S(1)} %get-tuple-element.7.tile_ref, s32[256]{0:T(256)S(1)} %get-tuple-element.6.used_ref, bf16[128,2,16,256]{3,2,1,0:T(8,128)(2,1)} %bitcast.10, f32[1,256]{1,0:T(1,128)S(1)} %bitcast.8, ...), custom_call_target="tpu_custom_call" | custom-call | flops 4294967296 | bytes 8388608 | tf_op jit(solution)/shard_map/pallas_call | solution.py:124
  76.8 0.0 copy-done.4
  76.8 1.0 %copy.16 = bf16[32,64,256]{2,1,0:T(8,128)(2,1)} copy(bf16[32,64,256]{2,1,0:T(8,128)(2,1)S(1)} %copy-done.4) | data formatting | bytes 2097152
  77.8 1.3 %copy.17 = bf16[1,128,2,16,256]{4,3,2,1,0:T(8,128)(2,1)} copy(bf16[1,128,2,16,256]{4,3,2,1,0:T(8,128)(2,1)S(1)} %bitcast.7) | data formatting | bytes 4194304
Async XLA Ops:
  2.4 21.9 %copy-start = (bf16[256,1024]{1,0:T(8,128)(2,1)S(1)}, bf16[256,1024]{1,0:T(8,128)(2,1)}, u32[]{:S(2)}) copy-start(bf16[256,1024]{1,0:T(8,128)(2,1)} %up_ref.1) | copy-start | bytes 1572868
  2.4 21.9 %copy-start.1 = (bf16[1024,256]{1,0:T(8,128)(2,1)S(1)}, bf16[1024,256]{1,0:T(8,128)(2,1)}, u32[]{:S(2)}) copy-start(bf16[1024,256]{1,0:T(8,128)(2,1)} %down_ref.1) | copy-start | bytes 1572868
  2.4 21.9 %copy-start.2 = (f32[256]{0:T(256)S(1)}, f32[256]{0:T(256)}, u32[]{:S(2)}) copy-start(f32[256]{0:T(256)} %param.21) | copy-start | bytes 3076
  24.3 1.2 %copy-start.3 = (bf16[2048,256]{1,0:T(8,128)(2,1)S(1)}, bf16[2048,256]{1,0:T(8,128)(2,1)}, u32[]{:S(2)}) copy-start(bf16[2048,256]{1,0:T(8,128)(2,1)} %get-tuple-element.5) | copy-start | bytes 3145732
  25.5 51.3 %copy-start.4 = (bf16[32,64,256]{2,1,0:T(8,128)(2,1)S(1)}, bf16[32,64,256]{2,1,0:T(8,128)(2,1)}, u32[]{:S(2)}) copy-start(bf16[32,64,256]{2,1,0:T(8,128)(2,1)} %get-tuple-element.10) | copy-start | bytes 3145732
